TPU v7x, 512 devices: a whole 4x4x16 slice. The times are simulated.
512 devices in a mesh: clip: 4 (over x), tx: 16 (over z_lo, core), ty: 8 (over z_hi, y).
Axes of the slice: x: 4, y: 4, z: 16 (z_hi: 2, z_lo: 8; z = z_hi * 8 + z_lo), core: 2. Of those that a mesh axis runs over, the one named last changes fastest.
Arguments:
- query_states: bfloat16 [512, 128, 1152], P(('clip', 'tx', 'ty')), parts along dimension 0, may hold values from -64 to 64
- key_states: bfloat16 [512, 128, 1152], P(('clip', 'tx', 'ty')), parts along dimension 0, may hold values from -24 to 24
- value_states: bfloat16 [512, 128, 1152], P(('clip', 'tx', 'ty')), parts along dimension 0, may hold values from -6 to 6
- grad_output: bfloat16 [512, 128, 1152], P(('clip', 'tx', 'ty')), parts along dimension 0, may hold values from -6 to 6
- branch_gate: float32 [4608], P('clip'), parts along dimension 0, may hold values from 0.1 to 1.9
- out_weight: bfloat16 [1152, 1152], P('tx'), may hold values from -0.1875 to 0.1875
Outputs:
- query_grad: bfloat16 [512, 128, 1152], P(('clip', 'tx', 'ty')), parts along dimension 0
- key_grad: bfloat16 [512, 128, 1152], P(('clip', 'tx', 'ty')), parts along dimension 0
- value_grad: bfloat16 [512, 128, 1152], P(('clip', 'tx', 'ty')), parts along dimension 0
- gate_grad: float32 [4608], P('clip'), parts along dimension 0
There are 4 independent parts, one for each index of `clip`. A program takes and returns all parts, laid end to end along the dimension named above; an argument that names none is the same for every part. Nothing has to cross between parts.
All inputs are finite; a program needn't handle non-finite values.
Results may differ from a plain program's by a relative error of at most 0.025.
Values may be sent and summed in bfloat16 or wider, within the bound.
No kernel may reach another device: no remote copies, remote signals or barrier semaphores. Data moves between devices by JAX's collectives and lax.ppermute only.
A program may use at most 64 MiB of HBM per device.

v0:
```python
import jax
import jax.numpy as jnp
from jax import lax
from jax.sharding import Mesh
from jax.sharding import PartitionSpec as P

HEAD_DIM = 72
TX = ("tx_0", "tx_1")
TY = ("ty_0", "ty_1")
TX_TY = ("tx_0", "tx_1", "ty_0", "ty_1")
CLIP_TX_TY = ("clip", "tx_0", "tx_1", "ty_0", "ty_1")


def shortened(x):

    def short(part):
        return part.astype(jnp.bfloat16) if part.dtype == jnp.float32 else part

    return jax.tree.map(short, x)


def over_axes(x, axes):
    for axis in axes:
        x = lax.psum(x, axis)
    return x


def attend_block(queries, keys_in, values_in, grads_in):
    frames, block_pos, block_width = queries.shape
    heads_here = block_width // HEAD_DIM
    shape4 = (frames, block_pos, heads_here, HEAD_DIM)
    q_four = queries.reshape(shape4)
    k_four = keys_in.reshape(shape4)
    v_four = values_in.reshape(shape4)
    g_four = grads_in.reshape(shape4)
    factor = HEAD_DIM ** (-0.5)
    scores = (
        jnp.einsum("fphd,gphd->phfg", q_four, k_four, preferred_element_type=jnp.float32) * factor
    )
    peak = jnp.max(scores, axis=-1, keepdims=True)
    expon = jnp.exp(scores - peak)
    probs = expon / jnp.sum(expon, axis=-1, keepdims=True)
    probs_b = probs.astype(jnp.bfloat16)
    attn_out = jnp.einsum(
        "phfg,gphd->fphd", probs_b, v_four, preferred_element_type=jnp.float32
    ).astype(jnp.bfloat16)
    value_grad = jnp.einsum(
        "phfg,fphd->gphd", probs_b, g_four, preferred_element_type=jnp.float32
    ).astype(jnp.bfloat16)
    dprobs = jnp.einsum("fphd,gphd->phfg", g_four, v_four, preferred_element_type=jnp.float32)
    delta = jnp.sum(g_four.astype(jnp.float32) * attn_out.astype(jnp.float32), axis=-1)
    delta = jnp.transpose(delta, (1, 2, 0))[..., None]
    dscores = (probs * (dprobs - delta) * factor).astype(jnp.bfloat16)
    query_grad = jnp.einsum(
        "phfg,gphd->fphd", dscores, k_four, preferred_element_type=jnp.float32
    ).astype(jnp.bfloat16)
    key_grad = jnp.einsum(
        "phfg,fphd->gphd", dscores, q_four, preferred_element_type=jnp.float32
    ).astype(jnp.bfloat16)
    flat = (frames, block_pos, block_width)
    return (
        query_grad.reshape(flat),
        key_grad.reshape(flat),
        value_grad.reshape(flat),
        attn_out.reshape(flat),
    )


def split_for_direct(array, across_x, across_y):
    positions, width = array.shape
    pieces = array.reshape(across_y, positions // across_y, across_x, width // across_x)
    pieces = jnp.transpose(pieces, (2, 0, 1, 3))
    return pieces.reshape(1, across_x * across_y, positions // across_y, width // across_x)


def join_from_direct(array, across_x, across_y):
    block_pos, block_width = (array.shape[2], array.shape[3])
    pieces = array.reshape(across_x, across_y, block_pos, block_width)
    pieces = jnp.transpose(pieces, (1, 2, 0, 3))
    return pieces.reshape(1, across_y * block_pos, across_x * block_width)


def per_device(query_states, key_states, value_states, grad_output, branch_gate, out_weight):
    across_x = lax.axis_size(TX)
    across_y = lax.axis_size(TY)
    devices_here = across_x * across_y
    positions = grad_output.shape[1]
    width = grad_output.shape[2]
    block_pos = positions // across_y
    block_width = width // across_x
    grad_rows = grad_output[0]
    gated = (grad_rows.astype(jnp.float32) * branch_gate).astype(jnp.bfloat16)
    full_weight = lax.all_gather(out_weight, TX, axis=0, tiled=True)
    d_attn = lax.dot_general(
        gated, full_weight, (((1,), (1,)), ((), ())), preferred_element_type=jnp.float32
    )
    d_attn = d_attn.astype(jnp.bfloat16)
    sources = (query_states[0], key_states[0], value_states[0], d_attn)
    prepared = tuple((split_for_direct(arr, across_x, across_y) for arr in sources))
    moved = jax.tree.map(
        lambda part, own: part.astype(own.dtype),
        lax.all_to_all(shortened(prepared), TX_TY, split_axis=1, concat_axis=0, tiled=True),
        prepared,
    )
    moved = tuple((arr.reshape(devices_here, block_pos, block_width) for arr in moved))
    results = attend_block(moved[0], moved[1], moved[2], moved[3])
    outgoing = tuple((arr.reshape(devices_here, 1, block_pos, block_width) for arr in results))
    returned = jax.tree.map(
        lambda part, own: part.astype(own.dtype),
        lax.all_to_all(shortened(outgoing), TX_TY, split_axis=0, concat_axis=1, tiled=True),
        outgoing,
    )
    returned = tuple((join_from_direct(arr, across_x, across_y) for arr in returned))
    query_grad, key_grad, value_grad, attn_frame = returned
    attn_rows = attn_frame[0]
    branch_out = jnp.dot(attn_rows, full_weight, preferred_element_type=jnp.float32)
    local_terms = jnp.sum(grad_rows.astype(jnp.float32) * branch_out, axis=0)
    gate_grad = over_axes(local_terms, TX_TY)
    return (query_grad, key_grad, value_grad, gate_grad)


def solution(mesh):
    split = Mesh(
        mesh.devices.reshape(mesh.shape["clip"], 8, 2, 2, 4),
        ("clip", "tx_0", "tx_1", "ty_0", "ty_1"),
    )
    placed = (
        P(CLIP_TX_TY, None, None),
        P(CLIP_TX_TY, None, None),
        P(CLIP_TX_TY, None, None),
        P(CLIP_TX_TY, None, None),
        P("clip"),
        P(TX, None),
    )
    return jax.shard_map(
        per_device,
        mesh=split,
        in_specs=placed,
        out_specs=(
            P(CLIP_TX_TY, None, None),
            P(CLIP_TX_TY, None, None),
            P(CLIP_TX_TY, None, None),
            P("clip"),
        ),
        check_vma=False,
    )
```

profile of v0, /device:TPU:6, one launch (start us, length us, event | category | flops | bytes accessed | tf_op | source)
XLA Modules:
  0.0 446.0 jit_solution(15969806378032638530)
XLA Ops:
  10.8 20.0 %all-to-all-start = ((bf16[1,128,16,72]{3,2,0,1:T(8,128)(2,1)}), bf16[1,128,16,72]{3,2,0,1:T(8,128)(2,1)S(1)}, u32[]{:S(2)}, u32[]{:S(2)}) async-start(bf16[1,128,16,72]{3,2,0,1:T(8,128)(2,1)} %bitcast.2), calls=%async_computation | async-start | bytes 1048576 | tf_op jit(solution)/shard_map/all_to_all | solution.py:102
  32.6 33.7 %all-to-all-done = bf16[1,128,16,72]{3,2,0,1:T(8,128)(2,1)S(1)} async-done(((bf16[1,128,16,72]{3,2,0,1:T(8,128)(2,1)}), bf16[1,128,16,72]{3,2,0,1:T(8,128)(2,1)S(1)}, u32[]{:S(2)}, u32[]{:S(2)}) %all-to-all-start) | async-done | bytes 294944 | tf_op jit(solution)/shard_map/all_to_all | solution.py:102
  66.3 9.5 %all-to-all-start.1 = ((bf16[1,128,16,72]{3,2,0,1:T(8,128)(2,1)}), bf16[1,128,16,72]{3,2,0,1:T(8,128)(2,1)S(1)}, u32[]{:S(2)}, u32[]{:S(2)}) async-start(bf16[1,128,16,72]{3,2,0,1:T(8,128)(2,1)} %bitcast.6), calls=%async_computation.1 | async-start | bytes 1048576 | tf_op jit(solution)/shard_map/all_to_all | solution.py:102
  75.9 68.5 %all-gather.2.cloned.1.call-done = bf16[1152,1152]{1,0:T(8,128)(2,1)} async-done(((bf16[72,1152]{1,0:T(8,128)(2,1)}), bf16[1152,1152]{1,0:T(8,128)(2,1)}) %all-gather.2.cloned.1.call-update) | async-done | bytes 2654224 | tf_op jit(solution)/shard_map/all_gather | solution.py:93
  144.4 2.7 convolution_convert_fusion
  149.0 12.0 %all-to-all-start.2 = ((bf16[1,128,16,72]{3,2,0,1:T(8,128)(2,1)}), bf16[1,128,16,72]{3,2,0,1:T(8,128)(2,1)S(1)}, u32[]{:S(2)}, u32[]{:S(2)}) async-start(bf16[1,128,16,72]{3,2,0,1:T(8,128)(2,1)} %bitcast.11), calls=%async_computation.2 | async-start | bytes 1048576 | tf_op jit(solution)/shard_map/all_to_all | solution.py:102
  162.9 28.8 %all-to-all-done.2 = bf16[1,128,16,72]{3,2,0,1:T(8,128)(2,1)S(1)} async-done(((bf16[1,128,16,72]{3,2,0,1:T(8,128)(2,1)}), bf16[1,128,16,72]{3,2,0,1:T(8,128)(2,1)S(1)}, u32[]{:S(2)}, u32[]{:S(2)}) %all-to-all-start.2) | async-done | bytes 294944 | tf_op jit(solution)/shard_map/all_to_all | solution.py:102
  191.7 9.7 %all-to-all-start.3 = ((bf16[1,128,16,72]{3,2,0,1:T(8,128)(2,1)}), bf16[1,128,16,72]{3,2,0,1:T(8,128)(2,1)S(1)}, u32[]{:S(2)}, u32[]{:S(2)}) async-start(bf16[1,128,16,72]{3,2,0,1:T(8,128)(2,1)} %bitcast.15), calls=%async_computation.3 | async-start | bytes 1048576 | tf_op jit(solution)/shard_map/all_to_all | solution.py:102
  207.2 24.7 %all-to-all-done.3 = bf16[1,128,16,72]{3,2,0,1:T(8,128)(2,1)S(1)} async-done(((bf16[1,128,16,72]{3,2,0,1:T(8,128)(2,1)}), bf16[1,128,16,72]{3,2,0,1:T(8,128)(2,1)S(1)}, u32[]{:S(2)}, u32[]{:S(2)}) %all-to-all-start.3) | async-done | bytes 294944 | tf_op jit(solution)/shard_map/all_to_all | solution.py:102
  231.8 9.5 %all-to-all-start.6 = ((bf16[128,1,16,72]{3,2,1,0:T(8,128)(2,1)}), bf16[128,1,16,72]{3,2,1,0:T(8,128)(2,1)S(1)}, u32[]{:S(2)}, u32[]{:S(2)}) async-start(bf16[128,1,16,72]{3,2,1,0:T(8,128)(2,1)} %copy.83), calls=%async_computation.6 | async-start | bytes 1048576 | tf_op jit(solution)/shard_map/all_to_all | solution.py:110
  244.7 27.3 %all-to-all-done.6 = bf16[128,1,16,72]{3,2,1,0:T(8,128)(2,1)S(1)} async-done(((bf16[128,1,16,72]{3,2,1,0:T(8,128)(2,1)}), bf16[128,1,16,72]{3,2,1,0:T(8,128)(2,1)S(1)}, u32[]{:S(2)}, u32[]{:S(2)}) %all-to-all-start.6) | async-done | bytes 294944 | tf_op jit(solution)/shard_map/all_to_all | solution.py:110
  272.0 9.5 %all-to-all-start.7 = ((bf16[128,1,16,72]{3,2,1,0:T(8,128)(2,1)}), bf16[128,1,16,72]{3,2,1,0:T(8,128)(2,1)S(1)}, u32[]{:S(2)}, u32[]{:S(2)}) async-start(bf16[128,1,16,72]{3,2,1,0:T(8,128)(2,1)} %copy.85), calls=%async_computation.7 | async-start | bytes 1048576 | tf_op jit(solution)/shard_map/all_to_all | solution.py:110
  284.8 27.4 %all-to-all-done.7 = bf16[128,1,16,72]{3,2,1,0:T(8,128)(2,1)S(1)} async-done(((bf16[128,1,16,72]{3,2,1,0:T(8,128)(2,1)}), bf16[128,1,16,72]{3,2,1,0:T(8,128)(2,1)S(1)}, u32[]{:S(2)}, u32[]{:S(2)}) %all-to-all-start.7) | async-done | bytes 294944 | tf_op jit(solution)/shard_map/all_to_all | solution.py:110
  312.2 9.5 %all-to-all-start.4 = ((bf16[128,1,16,72]{3,2,1,0:T(8,128)(2,1)}), bf16[128,1,16,72]{3,2,1,0:T(8,128)(2,1)S(1)}, u32[]{:S(2)}, u32[]{:S(2)}) async-start(bf16[128,1,16,72]{3,2,1,0:T(8,128)(2,1)} %copy.77), calls=%async_computation.4 | async-start | bytes 1048576 | tf_op jit(solution)/shard_map/all_to_all | solution.py:110
  323.4 29.0 %all-to-all-done.4 = bf16[128,1,16,72]{3,2,1,0:T(8,128)(2,1)S(1)} async-done(((bf16[128,1,16,72]{3,2,1,0:T(8,128)(2,1)}), bf16[128,1,16,72]{3,2,1,0:T(8,128)(2,1)S(1)}, u32[]{:S(2)}, u32[]{:S(2)}) %all-to-all-start.4) | async-done | bytes 294944 | tf_op jit(solution)/shard_map/all_to_all | solution.py:110
  352.4 10.0 %all-to-all-start.5 = ((bf16[128,1,16,72]{3,2,1,0:T(8,128)(2,1)}), bf16[128,1,16,72]{3,2,1,0:T(8,128)(2,1)}, u32[]{:S(2)}, u32[]{:S(2)}) async-start(bf16[128,1,16,72]{3,2,1,0:T(8,128)(2,1)} %copy.80), calls=%async_computation.5 | async-start | bytes 1048576 | tf_op jit(solution)/shard_map/all_to_all | solution.py:110
  363.6 2.3 reshape.172
  365.9 2.2 copy.86
  368.1 2.3 squeeze_reshape.3
  371.5 2.3 reshape.168
  375.3 33.8 %psum.28 = f32[1152]{0:T(1024)S(1)} all-reduce(f32[1152]{0:T(1024)S(1)} %fusion.6), channel_id=1, replica_groups=mesh['clip'=4,'tx_0'=8,'tx_1'=2,'ty_0'=2,'ty_1'=4] {'tx_0'}, use_global_device_ids=true, to_apply=%region_4.0 | all-reduce | flops 1152 | bytes 9216 | tf_op jit(solution)/shard_map/psum | solution.py:24
  409.2 2.5 psum.29
  411.7 13.8 %psum.30 = f32[1152]{0:T(1024)S(1)} all-reduce(f32[1152]{0:T(1024)S(1)} %psum.29), channel_id=1, replica_groups=mesh['clip'=4,'tx_0'=8,'tx_1'=2,'ty_0'=2,'ty_1'=4] {'ty_0'}, use_global_device_ids=true, to_apply=%region_6.0 | all-reduce | flops 1152 | bytes 9216 | tf_op jit(solution)/shard_map/psum | solution.py:24
  425.4 11.1 %psum.31 = f32[1152]{0:T(1024)} all-reduce(f32[1152]{0:T(1024)S(1)} %psum.30), channel_id=1, replica_groups=mesh['clip'=4,'tx_0'=8,'tx_1'=2,'ty_0'=2,'ty_1'=4] {'ty_1'}, use_global_device_ids=true, to_apply=%region_7.0 | all-reduce | flops 1152 | bytes 9216 | tf_op jit(solution)/shard_map/psum | solution.py:24
  (49 shorter events, 29.7 us)
Async XLA Ops:
  7.2 23.6 %copy-start.5 = (bf16[1,128,1152]{2,1,0:T(8,128)(2,1)S(1)}, bf16[1,128,1152]{2,1,0:T(8,128)(2,1)}, u32[]{:S(2)}) copy-start(bf16[1,128,1152]{2,1,0:T(8,128)(2,1)} %param.7) | copy-start | bytes 884740
  7.2 137.2 %all-gather.2.cloned.1.call-start = ((), (), s32[]{:S(2)}) async-start(), calls=%async_computation.8 | async-start | bytes 2820096 | tf_op jit(solution)/shard_map/all_gather | solution.py:93
  9.8 134.6 %copy-start.4 = (bf16[1,128,1152]{2,1,0:T(8,128)(2,1)S(1)}, bf16[1,128,1152]{2,1,0:T(8,128)(2,1)}, u32[]{:S(2)}) copy-start(bf16[1,128,1152]{2,1,0:T(8,128)(2,1)} %param.9) | copy-start | bytes 884740
  9.8 134.6 %copy-start.8 = (f32[1152]{0:T(1024)S(1)}, f32[1152]{0:T(1024)}, u32[]{:S(2)}) copy-start(f32[1152]{0:T(1024)} %param.10) | copy-start | bytes 13828
  10.8 55.5 %all-to-all-start = ((bf16[1,128,16,72]{3,2,0,1:T(8,128)(2,1)}), bf16[1,128,16,72]{3,2,0,1:T(8,128)(2,1)S(1)}, u32[]{:S(2)}, u32[]{:S(2)}) async-start(bf16[1,128,16,72]{3,2,0,1:T(8,128)(2,1)} %bitcast.2), calls=%async_computation | async-start | bytes 1048576 | tf_op jit(solution)/shard_map/all_to_all | solution.py:102
  66.3 82.7 %all-to-all-start.1 = ((bf16[1,128,16,72]{3,2,0,1:T(8,128)(2,1)}), bf16[1,128,16,72]{3,2,0,1:T(8,128)(2,1)S(1)}, u32[]{:S(2)}, u32[]{:S(2)}) async-start(bf16[1,128,16,72]{3,2,0,1:T(8,128)(2,1)} %bitcast.6), calls=%async_computation.1 | async-start | bytes 1048576 | tf_op jit(solution)/shard_map/all_to_all | solution.py:102
  75.9 85.1 %copy-start.6 = (bf16[1,128,1152]{2,1,0:T(8,128)(2,1)S(1)}, bf16[1,128,1152]{2,1,0:T(8,128)(2,1)}, u32[]{:S(2)}) copy-start(bf16[1,128,1152]{2,1,0:T(8,128)(2,1)} %param.8) | copy-start | bytes 884740
  149.0 42.7 %all-to-all-start.2 = ((bf16[1,128,16,72]{3,2,0,1:T(8,128)(2,1)}), bf16[1,128,16,72]{3,2,0,1:T(8,128)(2,1)S(1)}, u32[]{:S(2)}, u32[]{:S(2)}) async-start(bf16[1,128,16,72]{3,2,0,1:T(8,128)(2,1)} %bitcast.11), calls=%async_computation.2 | async-start | bytes 1048576 | tf_op jit(solution)/shard_map/all_to_all | solution.py:102
  191.7 40.2 %all-to-all-start.3 = ((bf16[1,128,16,72]{3,2,0,1:T(8,128)(2,1)}), bf16[1,128,16,72]{3,2,0,1:T(8,128)(2,1)S(1)}, u32[]{:S(2)}, u32[]{:S(2)}) async-start(bf16[1,128,16,72]{3,2,0,1:T(8,128)(2,1)} %bitcast.15), calls=%async_computation.3 | async-start | bytes 1048576 | tf_op jit(solution)/shard_map/all_to_all | solution.py:102
  231.8 40.2 %all-to-all-start.6 = ((bf16[128,1,16,72]{3,2,1,0:T(8,128)(2,1)}), bf16[128,1,16,72]{3,2,1,0:T(8,128)(2,1)S(1)}, u32[]{:S(2)}, u32[]{:S(2)}) async-start(bf16[128,1,16,72]{3,2,1,0:T(8,128)(2,1)} %copy.83), calls=%async_computation.6 | async-start | bytes 1048576 | tf_op jit(solution)/shard_map/all_to_all | solution.py:110
  241.8 30.2 %copy-start.7 = (bf16[1,128,16,72]{1,3,2,0:T(8,128)(2,1)}, bf16[1,128,16,72]{1,3,2,0:T(8,128)(2,1)S(1)}, u32[]{:S(2)}) copy-start(bf16[1,128,16,72]{1,3,2,0:T(8,128)(2,1)S(1)} %copy.72) | copy-start | bytes 884740
  272.0 40.2 %all-to-all-start.7 = ((bf16[128,1,16,72]{3,2,1,0:T(8,128)(2,1)}), bf16[128,1,16,72]{3,2,1,0:T(8,128)(2,1)S(1)}, u32[]{:S(2)}, u32[]{:S(2)}) async-start(bf16[128,1,16,72]{3,2,1,0:T(8,128)(2,1)} %copy.85), calls=%async_computation.7 | async-start | bytes 1048576 | tf_op jit(solution)/shard_map/all_to_all | solution.py:110
  312.2 50.2 %copy-start.1 = (bf16[128,1,16,72]{3,2,1,0:T(8,128)(2,1)}, bf16[128,1,16,72]{3,2,1,0:T(8,128)(2,1)S(1)}, u32[]{:S(2)}) copy-start(bf16[128,1,16,72]{3,2,1,0:T(8,128)(2,1)S(1)} %all-to-all-done.7) | copy-start | bytes 884740
  312.2 40.2 %all-to-all-start.4 = ((bf16[128,1,16,72]{3,2,1,0:T(8,128)(2,1)}), bf16[128,1,16,72]{3,2,1,0:T(8,128)(2,1)S(1)}, u32[]{:S(2)}, u32[]{:S(2)}) async-start(bf16[128,1,16,72]{3,2,1,0:T(8,128)(2,1)} %copy.77), calls=%async_computation.4 | async-start | bytes 1048576 | tf_op jit(solution)/shard_map/all_to_all | solution.py:110
  352.4 10.1 %copy-start.2 = (bf16[128,1,16,72]{3,2,1,0:T(8,128)(2,1)}, bf16[128,1,16,72]{3,2,1,0:T(8,128)(2,1)S(1)}, u32[]{:S(2)}) copy-start(bf16[128,1,16,72]{3,2,1,0:T(8,128)(2,1)S(1)} %all-to-all-done.4) | copy-start | bytes 884740
  352.4 84.1 %all-to-all-start.5 = ((bf16[128,1,16,72]{3,2,1,0:T(8,128)(2,1)}), bf16[128,1,16,72]{3,2,1,0:T(8,128)(2,1)}, u32[]{:S(2)}, u32[]{:S(2)}) async-start(bf16[128,1,16,72]{3,2,1,0:T(8,128)(2,1)} %copy.80), calls=%async_computation.5 | async-start | bytes 1048576 | tf_op jit(solution)/shard_map/all_to_all | solution.py:110
  362.5 11.3 %copy-start = (bf16[1152,1152]{1,0:T(8,128)(2,1)S(1)}, bf16[1152,1152]{1,0:T(8,128)(2,1)}, u32[]{:S(2)}) copy-start(bf16[1152,1152]{1,0:T(8,128)(2,1)} %all-gather.2.cloned.1.call-done) | copy-start | bytes 7962628
  363.6 6.8 %copy-start.3 = (bf16[128,1,16,72]{3,2,1,0:T(8,128)(2,1)S(1)}, bf16[128,1,16,72]{3,2,1,0:T(8,128)(2,1)}, u32[]{:S(2)}) copy-start(bf16[128,1,16,72]{3,2,1,0:T(8,128)(2,1)} %copy-done.2) | copy-start | bytes 884740
Sparse Core Ops, SparseCore 0:
  10.1 134.2 all-gather.1
where the time goes:
time: 447 us; the launch traced here: 446 us
  waiting for transfers between devices  240 us (54%)
  starting transfers between devices  89.7 us (20%)
  blocking collectives  61.2 us (14%)
  local copies, waits for them, and re-layouts  29.1 us (7%)
  between operations  14.3 us (3%)
  matrix products  11.6 us (3%)
    all_to_all x4, waiting for transfers between devices, per_device(): lax.all_to_all(shortened(prepared), TX_TY, split_axis=1, concat_axis=0, t...  87.1 us
    all_to_all x4, waiting for transfers between devices, per_device(): lax.all_to_all(shortened(outgoing), TX_TY, split_axis=0, concat_axis=1, t...  83.8 us
    all_gather x1, waiting for transfers between devices, per_device(): full_weight = lax.all_gather(out_weight, TX, axis=0, tiled=True)  68.5 us
    psum x4, blocking collectives, over_axes(): x = lax.psum(x, axis)  61.2 us
    all_to_all x4, starting transfers between devices, per_device(): lax.all_to_all(shortened(prepared), TX_TY, split_axis=1, concat_axis=0, t...  51.2 us
    all_to_all x4, starting transfers between devices, per_device(): lax.all_to_all(shortened(outgoing), TX_TY, split_axis=0, concat_axis=1, t...  38.5 us
  transfers between devices with their start and end apart: 9, of which 7 were waited for; matrix products, arithmetic and copies ran while one was open for 9% of the time, Pallas kernels for 0%

commit v1 on v0

v1 whole, which is shorter than its diff:
```python
import functools

import jax
import jax.numpy as jnp
from jax import lax
from jax.experimental import pallas as pl
from jax.experimental.pallas import tpu as pltpu
from jax.sharding import Mesh
from jax.sharding import PartitionSpec as P

HEADS = 16
HEAD_DIM = 72
LANES = 128
WIDTH = HEADS * HEAD_DIM
TILES = WIDTH // LANES
AXES = ("clip", "zl", "core", "zh", "y")
GROUP = ("zl", "core", "zh", "y")
FACTOR = HEAD_DIM ** (-0.5)


def head_tiles(head):
    first = head * HEAD_DIM // LANES
    last = (head * HEAD_DIM + HEAD_DIM - 1) // LANES
    return first, last + 1


def attend_kernel(x_ref, w_ref, gate_ref, out_ref, gate_out_ref, da_ref):
    f32, bf16 = jnp.float32, jnp.bfloat16
    nt = (((1,), (1,)), ((), ()))
    nn = (((1,), (0,)), ((), ()))
    tn = (((0,), (0,)), ((), ()))
    frames = x_ref.shape[1]

    def cat(first, last):
        parts = [x_ref[t] for t in range(first, last)]
        return parts[0] if len(parts) == 1 else jnp.concatenate(parts, axis=1)

    go = cat(3 * TILES, 4 * TILES)
    gated = (go.astype(f32) * gate_ref[...]).astype(bf16)
    da_ref[...] = lax.dot_general(gated, w_ref[...], nt, preferred_element_type=f32).astype(bf16)

    acc = {}

    def add(kind, first, value):
        for n in range(value.shape[1] // LANES):
            key = (kind, first + n)
            part = value[:, n * LANES : (n + 1) * LANES]
            acc[key] = acc[key] + part if key in acc else part

    for head in range(HEADS):
        a, b = head_tiles(head)
        width = (b - a) * LANES
        lane = lax.broadcasted_iota(jnp.int32, (frames, width), 1) + a * LANES
        mask = (lane >= head * HEAD_DIM) & (lane < (head + 1) * HEAD_DIM)

        def masked(value):
            return jnp.where(mask, value, jnp.zeros_like(value))

        q = masked(cat(a, b))
        k = masked(cat(TILES + a, TILES + b))
        v = masked(cat(2 * TILES + a, 2 * TILES + b))
        g = masked(da_ref[:, a * LANES : b * LANES])
        scores = lax.dot_general(q, k, nt, preferred_element_type=f32) * FACTOR
        expon = jnp.exp(scores - jnp.max(scores, axis=-1, keepdims=True))
        probs = expon / jnp.sum(expon, axis=-1, keepdims=True)
        probs_b = probs.astype(bf16)
        add("o", a, lax.dot_general(probs_b, v, nn, preferred_element_type=f32))
        add("v", a, lax.dot_general(probs_b, g, tn, preferred_element_type=f32))
        dprobs = lax.dot_general(g, v, nt, preferred_element_type=f32)
        delta = jnp.sum(probs * dprobs, axis=-1, keepdims=True)
        dscores = (probs * (dprobs - delta) * FACTOR).astype(bf16)
        add("q", a, lax.dot_general(dscores, k, nn, preferred_element_type=f32))
        add("k", a, lax.dot_general(dscores, q, tn, preferred_element_type=f32))
    for n, kind in enumerate("qkv"):
        for t in range(TILES):
            out_ref[n * TILES + t] = acc[(kind, t)].astype(bf16)
    attn = jnp.concatenate([acc[("o", t)].astype(bf16) for t in range(TILES)], axis=1)
    branch = lax.dot_general(attn, w_ref[...], nn, preferred_element_type=f32)
    gate_out_ref[...] = jnp.sum(go.astype(f32) * branch, axis=0, keepdims=True)


def attend(x, weight, gate):
    frames = x.shape[1]
    vmem = pl.BlockSpec(memory_space=pltpu.VMEM)
    return pl.pallas_call(
        attend_kernel,
        out_shape=(
            jax.ShapeDtypeStruct((3 * TILES, frames, LANES), jnp.bfloat16),
            jax.ShapeDtypeStruct((1, WIDTH), jnp.float32),
        ),
        in_specs=[vmem, vmem, vmem],
        out_specs=(vmem, vmem),
        scratch_shapes=[pltpu.VMEM((frames, WIDTH), jnp.bfloat16)],
        compiler_params=pltpu.CompilerParams(vmem_limit_bytes=32 << 20),
        cost_estimate=pl.CostEstimate(
            flops=1_500_000_000, bytes_accessed=5_000_000, transcendentals=300_000
        ),
    )(x, weight, gate)


def z_spot(z):
    return (z % 8) * 2 + z // 8


def along_z(x, to):
    return lax.ppermute(x, ("zl", "zh"), [(z_spot(i), z_spot(to(i) % 16)) for i in range(16)])


def along(x, axis, shift, sources):
    return lax.ppermute(x, axis, [(i, (i + shift) % 4) for i in range(sources)])


def pick(stack, index):
    return lax.dynamic_index_in_dim(stack, index, 0, keepdims=False)


def gather_weight(shard):
    rows = 8
    z = lax.axis_index("zl")
    x = lax.axis_index("clip")
    y = lax.axis_index("y")
    core = lax.axis_index("core")
    row = jnp.minimum(x, 2) * 3 + jnp.minimum(y, 2)
    held = lax.dynamic_slice_in_dim(shard, row * rows, rows, 0)[None]
    held = jnp.concatenate([held, along_z(held, lambda i: i + 1)])
    held = jnp.concatenate([along_z(held, lambda i: i - 2), held])
    held = jnp.concatenate([held, along_z(held, lambda i: i + 4 if i % 2 == 0 else i - 4)])
    held = jnp.stack([pick(held, (z + 2 - n) % 8) for n in range(8)])
    parts = jnp.stack([held] + [along(held, "y", s, 3) for s in (1, 2, 3)])
    held = jnp.stack([pick(parts, (y - n) % 4) for n in range(3)])
    parts = jnp.stack([held] + [along(held, "clip", s, 3) for s in (1, 2, 3)])
    held = jnp.stack([pick(parts, (x - n) % 4) for n in range(3)])
    other = lax.ppermute(held, "core", [(0, 1), (1, 0)])
    both = jnp.stack([jnp.where(core == 0, held, other), jnp.where(core == 0, other, held)])
    return jnp.transpose(both, (3, 0, 1, 2, 4, 5)).reshape(WIDTH, WIDTH)


def sum_over_group(v):
    v = v + lax.ppermute(v, "core", [(0, 1), (1, 0)])
    v = v + along(v, "y", 1, 4) + along(v, "y", 2, 4) + along(v, "y", 3, 4)
    for step in (1, 4):
        hops = [along_z(v, lambda i, n=n: i + n * step) for n in (1, 2, 3)]
        v = v + hops[0] + hops[1] + hops[2]
    return v


def per_device(query_states, key_states, value_states, grad_output, branch_gate, out_weight):
    positions = grad_output.shape[1]
    sources = (query_states, key_states, value_states, grad_output)
    packed = jnp.concatenate([a.reshape(positions, TILES, LANES) for a in sources], axis=1)
    packed = packed.reshape(positions, TILES, 4, LANES)
    moved = lax.all_to_all(packed, GROUP, split_axis=0, concat_axis=0, tiled=True)
    frames = moved.shape[0]
    moved = jnp.transpose(moved.reshape(frames, 4 * TILES, LANES), (1, 0, 2))
    weight = gather_weight(out_weight)
    grads, terms = attend(moved, weight, branch_gate.reshape(1, WIDTH))
    outgoing = jnp.transpose(grads, (1, 0, 2))
    outgoing = jnp.pad(outgoing, ((0, 0), (0, 1), (0, 0))).reshape(frames, 7, 4, LANES)
    returned = lax.all_to_all(outgoing, GROUP, split_axis=0, concat_axis=0, tiled=True)
    returned = returned.reshape(positions, 28, LANES)
    outs = tuple(
        returned[:, n * TILES : (n + 1) * TILES].reshape(1, positions, WIDTH) for n in range(3)
    )
    return outs + (sum_over_group(terms).reshape(WIDTH),)


def solution(mesh):
    split = Mesh(mesh.devices.reshape(mesh.shape["clip"], 8, 2, 2, 4), AXES)
    rows = P(AXES, None, None)
    return jax.shard_map(
        per_device,
        mesh=split,
        in_specs=(rows, rows, rows, rows, P("clip"), P(("zl", "core"), None)),
        out_specs=(rows, rows, rows, P("clip")),
        check_vma=False,
    )
```

time: 447 us -> 193 us (0.43)
  waiting for transfers between devices: 240 us -> 66.9 us
  blocking collectives: 61.2 us -> 0 us
  local copies, waits for them, and re-layouts: 29.1 us -> 13.6 us
  between operations: 14.3 us -> 1.35 us
  matrix products: 11.6 us -> 0 us
  starting transfers between devices: 89.7 us -> 98.6 us
  Pallas kernels: 0 us -> 8.01 us
    all_to_all x8 -> x2, waiting for transfers between devices: 171 us -> 8.04 us  [the longest x1 8.04 us: per_device(): lax.all_to_all(packed, GROUP, split_axis=0, concat_axis=0, tiled=True)]
    ppermute x0 -> x20, starting transfers between devices: none -> 72.9 us  [the longest x9 44.4 us: along_z(): lax.ppermute(x, ('zl', 'zh'), [(z_spot(i), z_spot(to(i) % 16)) for i in r...]
    all_gather x1 -> x0, waiting for transfers between devices: 68.5 us -> none  [per_device(): full_weight = lax.all_gather(out_weight, TX, axis=0, tiled=True)]
    all_to_all x8 -> x2, starting transfers between devices: 89.7 us -> 25.7 us  [the longest x1 15.6 us: per_device(): lax.all_to_all(packed, GROUP, split_axis=0, concat_axis=0, tiled=True)]
    psum x4 -> x0, blocking collectives: 61.2 us -> none  [over_axes(): x = lax.psum(x, axis)]
    ppermute x0 -> x20, waiting for transfers between devices: none -> 58.9 us  [the longest x9 30.1 us: along(): return lax.ppermute(x, axis, [(i, (i + shift) % 4) for i in range(sources)])]
    another operation x11 -> x1, local copies, waits for them, and re-layouts: 13.7 us -> 0.02 us  [gather_weight(): held = jnp.stack([pick(held, (z + 2 - n) % 8) for n in range(8)])]
    dot_general x7 -> x0, matrix products: 10.1 us -> none  [the longest x1 2.66 us: per_device(): lax.dot_general(gated, full_weight, (((1,), (1,)), ((), ())), preferred_e...]
  transfers between devices with their start and end apart: 9 -> 22, of which waited for: 7 -> 13; matrix products, arithmetic and copies ran while one was open for 9% -> 4% of each run, Pallas kernels for 0% -> 0%
where the time goes in v1:
time: 193 us; the launch traced here: 192 us
  starting transfers between devices  98.6 us (51%)
  waiting for transfers between devices  66.9 us (35%)
  local copies, waits for them, and re-layouts  13.6 us (7%)
  Pallas kernels  8.01 us (4%)
  other arithmetic  3.36 us (2%)
    ppermute x9, starting transfers between devices, along_z(): lax.ppermute(x, ('zl', 'zh'), [(z_spot(i), z_spot(to(i) % 16)) for i in r...  44.4 us
    ppermute x9, waiting for transfers between devices, along(): return lax.ppermute(x, axis, [(i, (i + shift) % 4) for i in range(sources)])  30.1 us
    ppermute x9, waiting for transfers between devices, along_z(): lax.ppermute(x, ('zl', 'zh'), [(z_spot(i), z_spot(to(i) % 16)) for i in r...  24.8 us
    ppermute x9, starting transfers between devices, along(): return lax.ppermute(x, axis, [(i, (i + shift) % 4) for i in range(sources)])  24.3 us
    all_to_all x1, starting transfers between devices, per_device(): lax.all_to_all(packed, GROUP, split_axis=0, concat_axis=0, tiled=True)  15.6 us
    all_to_all x1, starting transfers between devices, per_device(): lax.all_to_all(outgoing, GROUP, split_axis=0, concat_axis=0, tiled=True)  10.1 us
    all_to_all x1, waiting for transfers between devices, per_device(): lax.all_to_all(packed, GROUP, split_axis=0, concat_axis=0, tiled=True)  8.04 us
    pallas_call x1, Pallas kernels, attend(): pl.pallas_call(attend_kernel, out_shape=(jax.ShapeDtypeStruct((3 * TILES,...  8.01 us
  transfers between devices with their start and end apart: 22, of which 13 were waited for; matrix products, arithmetic and copies ran while one was open for 4% of the time, Pallas kernels for 0%

profile of v1, /device:TPU:6, one launch (start us, length us, event | category | flops | bytes accessed | tf_op | source)
XLA Modules:
  0.0 191.8 jit_solution(12846406784910418645)
XLA Ops:
  1.6 3.8 %collective-permute-start = (bf16[1,8,1152]{2,1,0:T(8,128)(2,1)S(1)}, bf16[1,8,1152]{2,1,0:T(8,128)(2,1)S(1)}, u32[]{:S(2)}, u32[]{:S(2)}) collective-permute-start(bf16[1,8,1152]{2,1,0:T(8,128)(2,1)S(1)} %dynamic-slice_bitcast_fusion), channel_id=1, source_target_pairs={{0,16},{16,32},{32,48},{48,64},{64,80},{80,96},{96,112},{112,4},{4... | collective-permute-start | bytes 55304 | tf_op jit(solution)/shard_map/ppermute | solution.py:106
  5.4 9.3 %collective-permute-done = bf16[1,8,1152]{2,1,0:T(8,128)(2,1)S(1)} collective-permute-done((bf16[1,8,1152]{2,1,0:T(8,128)(2,1)S(1)}, bf16[1,8,1152]{2,1,0:T(8,128)(2,1)S(1)}, u32[]{:S(2)}, u32[]{:S(2)}) %collective-permute-start) | collective-permute-done | bytes 18464 | tf_op jit(solution)/shard_map/ppermute | solution.py:106
  14.7 4.4 %collective-permute-start.1 = (bf16[2,8,1152]{2,1,0:T(8,128)(2,1)S(1)}, bf16[2,8,1152]{2,1,0:T(8,128)(2,1)S(1)}, u32[]{:S(2)}, u32[]{:S(2)}) collective-permute-start(bf16[2,8,1152]{2,1,0:T(8,128)(2,1)S(1)} %pad_maximum_fusion.8), channel_id=1, source_target_pairs={{0,100},{16,116},{32,0},{48,16},{64,32},{80,48},{96,64},{112,80},{... | collective-permute-start | bytes 110600 | tf_op jit(solution)/shard_map/ppermute | solution.py:106
  26.5 15.6 %all-to-all-start = ((bf16[128,9,4,128]{3,2,1,0:T(4,128)(2,1)}), bf16[128,9,4,128]{3,2,1,0:T(4,128)(2,1)}, u32[]{:S(2)}, u32[]{:S(2)}) async-start(bf16[128,9,4,128]{3,2,1,0:T(4,128)(2,1)} %copy.41), calls=%async_computation | async-start | bytes 2359296 | tf_op jit(solution)/shard_map/all_to_all | solution.py:152
  42.5 3.0 %collective-permute-start.3 = (bf16[8,8,1152]{2,1,0:T(8,128)(2,1)S(1)}, bf16[8,8,1152]{2,1,0:T(8,128)(2,1)S(1)}, u32[]{:S(2)}, u32[]{:S(2)}) collective-permute-start(bf16[8,8,1152]{2,1,0:T(8,128)(2,1)S(1)} %constant_dynamic-update-slice_fusion), channel_id=1, source_target_pairs={{0,1},{1,2},{2,3},{4,5},{5,6},{6,7},{8,9},{9,10},{10,11},{12,13},{... | collective-permute-start | bytes 442376 | tf_op jit(solution)/shard_map/ppermute | solution.py:110
  45.5 4.6 %collective-permute-start.4 = (bf16[8,8,1152]{2,1,0:T(8,128)(2,1)S(1)}, bf16[8,8,1152]{2,1,0:T(8,128)(2,1)S(1)}, u32[]{:S(2)}, u32[]{:S(2)}) collective-permute-start(bf16[8,8,1152]{2,1,0:T(8,128)(2,1)S(1)} %constant_dynamic-update-slice_fusion), channel_id=1, source_target_pairs={{0,2},{1,3},{2,0},{4,6},{5,7},{6,4},{8,10},{9,11},{10,8},{12,14},{... | collective-permute-start | bytes 442376 | tf_op jit(solution)/shard_map/ppermute | solution.py:110
  52.1 5.2 %collective-permute-done.4 = bf16[8,8,1152]{2,1,0:T(8,128)(2,1)S(1)} collective-permute-done((bf16[8,8,1152]{2,1,0:T(8,128)(2,1)S(1)}, bf16[8,8,1152]{2,1,0:T(8,128)(2,1)S(1)}, u32[]{:S(2)}, u32[]{:S(2)}) %collective-permute-start.4) | collective-permute-done | bytes 147488 | tf_op jit(solution)/shard_map/ppermute | solution.py:110
  62.7 11.0 %collective-permute-done.6 = bf16[3,8,8,1152]{3,2,0,1:T(8,128)(2,1)S(1)} collective-permute-done((bf16[3,8,8,1152]{3,2,0,1:T(8,128)(2,1)S(1)}, bf16[3,8,8,1152]{3,2,0,1:T(8,128)(2,1)S(1)}, u32[]{:S(2)}, u32[]{:S(2)}) %collective-permute-start.6) | collective-permute-done | bytes 442400 | tf_op jit(solution)/shard_map/ppermute | solution.py:110
  73.8 2.8 %collective-permute-done.7 = bf16[3,8,8,1152]{3,2,0,1:T(8,128)(2,1)S(1)} collective-permute-done((bf16[3,8,8,1152]{3,2,0,1:T(8,128)(2,1)S(1)}, bf16[3,8,8,1152]{3,2,0,1:T(8,128)(2,1)S(1)}, u32[]{:S(2)}, u32[]{:S(2)}) %collective-permute-start.7) | collective-permute-done | bytes 442400 | tf_op jit(solution)/shard_map/ppermute | solution.py:110
  76.6 7.6 %collective-permute-done.8 = bf16[3,8,8,1152]{3,2,0,1:T(8,128)(2,1)S(1)} collective-permute-done((bf16[3,8,8,1152]{3,2,0,1:T(8,128)(2,1)S(1)}, bf16[3,8,8,1152]{3,2,0,1:T(8,128)(2,1)S(1)}, u32[]{:S(2)}, u32[]{:S(2)}) %collective-permute-start.8) | collective-permute-done | bytes 442400 | tf_op jit(solution)/shard_map/ppermute | solution.py:110
  91.9 8.0 %all-to-all-done = bf16[128,9,4,128]{3,2,1,0:T(4,128)(2,1)} async-done(((bf16[128,9,4,128]{3,2,1,0:T(4,128)(2,1)}), bf16[128,9,4,128]{3,2,1,0:T(4,128)(2,1)}, u32[]{:S(2)}, u32[]{:S(2)}) %all-to-all-start) | async-done | bytes 1179680 | tf_op jit(solution)/shard_map/all_to_all | solution.py:152
  101.4 8.0 %shard_map.93 = (bf16[27,128,128]{2,1,0:T(8,128)(2,1)S(1)}, f32[1,1152]{1,0:T(1,128)S(1)}) custom-call(bf16[36,128,128]{2,1,0:T(8,128)(2,1)S(1)} %bitcast.47, bf16[1152,1152]{1,0:T(8,128)(2,1)S(1)} %bitcast.46, f32[1,1152]{1,0:T(1,128)S(1)} %reshape.57.gate_ref), custom_call_target="tpu_custom_call" | custom-call | flops 1500000000 | bytes 5000000 | tf_op jit(solution)/shard_map/pallas_call | solution.py:85
  111.2 10.1 %all-to-all-start.1 = ((bf16[128,7,4,128]{3,2,1,0:T(4,128)(2,1)}), bf16[128,7,4,128]{3,2,1,0:T(4,128)(2,1)S(1)}, u32[]{:S(2)}, u32[]{:S(2)}) async-start(bf16[128,7,4,128]{3,2,1,0:T(4,128)(2,1)} %copy.50), calls=%async_computation.1 | async-start | bytes 1835008 | tf_op jit(solution)/shard_map/all_to_all | solution.py:159
  124.4 3.0 %collective-permute-start.11 = (f32[1,1152]{1,0:T(1,128)S(1)}, f32[1,1152]{1,0:T(1,128)S(1)}, u32[]{:S(2)}, u32[]{:S(2)}) collective-permute-start(f32[1,1152]{1,0:T(1,128)S(1)} %add.192), channel_id=1, source_target_pairs={{0,1},{1,2},{2,3},{3,0},{4,5},{5,6},{6,7},{7,4},{8,9},{9,10},{10,1... | collective-permute-start | bytes 13832 | tf_op jit(solution)/shard_map/ppermute | solution.py:110
  127.5 4.6 %collective-permute-start.12 = (f32[1,1152]{1,0:T(1,128)S(1)}, f32[1,1152]{1,0:T(1,128)S(1)}, u32[]{:S(2)}, u32[]{:S(2)}) collective-permute-start(f32[1,1152]{1,0:T(1,128)S(1)} %add.192), channel_id=1, source_target_pairs={{0,2},{1,3},{2,0},{3,1},{4,6},{5,7},{6,4},{7,5},{8,10},{9,11},{10,... | collective-permute-start | bytes 13832 | tf_op jit(solution)/shard_map/ppermute | solution.py:110
  132.0 3.4 %collective-permute-start.13 = (f32[1,1152]{1,0:T(1,128)S(1)}, f32[1,1152]{1,0:T(1,128)S(1)}, u32[]{:S(2)}, u32[]{:S(2)}) collective-permute-start(f32[1,1152]{1,0:T(1,128)S(1)} %add.192), channel_id=1, source_target_pairs={{0,3},{1,0},{2,1},{3,2},{4,7},{5,4},{6,5},{7,6},{8,11},{9,8},{10,9... | collective-permute-start | bytes 13832 | tf_op jit(solution)/shard_map/ppermute | solution.py:110
  137.6 3.4 %collective-permute-start.14 = (f32[1,1152]{1,0:T(1,128)S(1)}, f32[1,1152]{1,0:T(1,128)S(1)}, u32[]{:S(2)}, u32[]{:S(2)}) collective-permute-start(f32[1,1152]{1,0:T(1,128)S(1)} %add_add_fusion.1), channel_id=1, source_target_pairs={{0,16},{16,32},{32,48},{48,64},{64,80},{80,96},{96,112},{112,4},{4... | collective-permute-start | bytes 13832 | tf_op jit(solution)/shard_map/ppermute | solution.py:106
  141.0 4.5 %collective-permute-start.15 = (f32[1,1152]{1,0:T(1,128)S(1)}, f32[1,1152]{1,0:T(1,128)S(1)}, u32[]{:S(2)}, u32[]{:S(2)}) collective-permute-start(f32[1,1152]{1,0:T(1,128)S(1)} %add_add_fusion.1), channel_id=1, source_target_pairs={{0,32},{16,48},{32,64},{48,80},{64,96},{80,112},{96,4},{112,20},{4... | collective-permute-start | bytes 13832 | tf_op jit(solution)/shard_map/ppermute | solution.py:106
  145.5 6.7 %collective-permute-start.16 = (f32[1,1152]{1,0:T(1,128)S(1)}, f32[1,1152]{1,0:T(1,128)S(1)}, u32[]{:S(2)}, u32[]{:S(2)}) collective-permute-start(f32[1,1152]{1,0:T(1,128)S(1)} %add_add_fusion.1), channel_id=1, source_target_pairs={{0,48},{16,64},{32,80},{48,96},{64,112},{80,4},{96,20},{112,36},{4... | collective-permute-start | bytes 13832 | tf_op jit(solution)/shard_map/ppermute | solution.py:106
  152.2 10.3 %collective-permute-done.14 = f32[1,1152]{1,0:T(1,128)S(1)} collective-permute-done((f32[1,1152]{1,0:T(1,128)S(1)}, f32[1,1152]{1,0:T(1,128)S(1)}, u32[]{:S(2)}, u32[]{:S(2)}) %collective-permute-start.14) | collective-permute-done | bytes 4640 | tf_op jit(solution)/shard_map/ppermute | solution.py:106
  164.5 3.6 %collective-permute-start.17 = (f32[1,1152]{1,0:T(1,128)S(1)}, f32[1,1152]{1,0:T(1,128)S(1)}, u32[]{:S(2)}, u32[]{:S(2)}) collective-permute-start(f32[1,1152]{1,0:T(1,128)S(1)} %add_add_fusion), channel_id=1, source_target_pairs={{0,64},{16,80},{32,96},{48,112},{64,4},{80,20},{96,36},{112,52},{4... | collective-permute-start | bytes 13832 | tf_op jit(solution)/shard_map/ppermute | solution.py:106
  168.1 9.5 %collective-permute-start.18 = (f32[1,1152]{1,0:T(1,128)S(1)}, f32[1,1152]{1,0:T(1,128)S(1)}, u32[]{:S(2)}, u32[]{:S(2)}) collective-permute-start(f32[1,1152]{1,0:T(1,128)S(1)} %add_add_fusion), channel_id=1, source_target_pairs={{0,4},{16,20},{32,36},{48,52},{64,68},{80,84},{96,100},{112,116},{... | collective-permute-start | bytes 13832 | tf_op jit(solution)/shard_map/ppermute | solution.py:106
  177.6 6.2 %collective-permute-start.19 = (f32[1,1152]{1,0:T(1,128)S(1)}, f32[1,1152]{1,0:T(1,128)S(1)}, u32[]{:S(2)}, u32[]{:S(2)}) collective-permute-start(f32[1,1152]{1,0:T(1,128)S(1)} %add_add_fusion), channel_id=1, source_target_pairs={{0,68},{16,84},{32,100},{48,116},{64,0},{80,16},{96,32},{112,48},{... | collective-permute-start | bytes 13832 | tf_op jit(solution)/shard_map/ppermute | solution.py:106
  183.8 3.2 %collective-permute-done.19 = f32[1,1152]{1,0:T(1,128)S(1)} collective-permute-done((f32[1,1152]{1,0:T(1,128)S(1)}, f32[1,1152]{1,0:T(1,128)S(1)}, u32[]{:S(2)}, u32[]{:S(2)}) %collective-permute-start.19) | collective-permute-done | bytes 4640 | tf_op jit(solution)/shard_map/ppermute | solution.py:106
  (68 shorter events, 38.6 us)
Async XLA Ops:
  0.6 20.8 %copy-start.1 = (bf16[1,128,1152]{2,1,0:T(8,128)(2,1)S(1)}, bf16[1,128,1152]{2,1,0:T(8,128)(2,1)}, u32[]{:S(2)}) copy-start(bf16[1,128,1152]{2,1,0:T(8,128)(2,1)} %param.8) | copy-start | bytes 884740
  0.7 21.0 %copy-start.2 = (bf16[1,128,1152]{2,1,0:T(8,128)(2,1)S(1)}, bf16[1,128,1152]{2,1,0:T(8,128)(2,1)}, u32[]{:S(2)}) copy-start(bf16[1,128,1152]{2,1,0:T(8,128)(2,1)} %param.9) | copy-start | bytes 884740
  1.6 13.1 %collective-permute-start = (bf16[1,8,1152]{2,1,0:T(8,128)(2,1)S(1)}, bf16[1,8,1152]{2,1,0:T(8,128)(2,1)S(1)}, u32[]{:S(2)}, u32[]{:S(2)}) collective-permute-start(bf16[1,8,1152]{2,1,0:T(8,128)(2,1)S(1)} %dynamic-slice_bitcast_fusion), channel_id=1, source_target_pairs={{0,16},{16,32},{32,48},{48,64},{64,80},{80,96},{96,112},{112,4},{4... | collective-permute-start | bytes 55304 | tf_op jit(solution)/shard_map/ppermute | solution.py:106
  14.7 7.2 %collective-permute-start.1 = (bf16[2,8,1152]{2,1,0:T(8,128)(2,1)S(1)}, bf16[2,8,1152]{2,1,0:T(8,128)(2,1)S(1)}, u32[]{:S(2)}, u32[]{:S(2)}) collective-permute-start(bf16[2,8,1152]{2,1,0:T(8,128)(2,1)S(1)} %pad_maximum_fusion.8), channel_id=1, source_target_pairs={{0,100},{16,116},{32,0},{48,16},{64,32},{80,48},{96,64},{112,80},{... | collective-permute-start | bytes 110600 | tf_op jit(solution)/shard_map/ppermute | solution.py:106
  22.0 20.3 %collective-permute-start.2 = (bf16[4,8,1152]{2,1,0:T(8,128)(2,1)S(1)}, bf16[4,8,1152]{2,1,0:T(8,128)(2,1)S(1)}, u32[]{:S(2)}, u32[]{:S(2)}) collective-permute-start(bf16[4,8,1152]{2,1,0:T(8,128)(2,1)S(1)} %pad_maximum_fusion.7), channel_id=1, source_target_pairs={{0,64},{16,84},{32,96},{48,116},{64,4},{80,16},{96,36},{112,48},{4... | collective-permute-start | bytes 221192 | tf_op jit(solution)/shard_map/ppermute | solution.py:106
  26.5 73.4 %all-to-all-start = ((bf16[128,9,4,128]{3,2,1,0:T(4,128)(2,1)}), bf16[128,9,4,128]{3,2,1,0:T(4,128)(2,1)}, u32[]{:S(2)}, u32[]{:S(2)}) async-start(bf16[128,9,4,128]{3,2,1,0:T(4,128)(2,1)} %copy.41), calls=%async_computation | async-start | bytes 2359296 | tf_op jit(solution)/shard_map/all_to_all | solution.py:152
  42.5 9.6 %collective-permute-start.3 = (bf16[8,8,1152]{2,1,0:T(8,128)(2,1)S(1)}, bf16[8,8,1152]{2,1,0:T(8,128)(2,1)S(1)}, u32[]{:S(2)}, u32[]{:S(2)}) collective-permute-start(bf16[8,8,1152]{2,1,0:T(8,128)(2,1)S(1)} %constant_dynamic-update-slice_fusion), channel_id=1, source_target_pairs={{0,1},{1,2},{2,3},{4,5},{5,6},{6,7},{8,9},{9,10},{10,11},{12,13},{... | collective-permute-start | bytes 442376 | tf_op jit(solution)/shard_map/ppermute | solution.py:110
  45.5 11.8 %collective-permute-start.4 = (bf16[8,8,1152]{2,1,0:T(8,128)(2,1)S(1)}, bf16[8,8,1152]{2,1,0:T(8,128)(2,1)S(1)}, u32[]{:S(2)}, u32[]{:S(2)}) collective-permute-start(bf16[8,8,1152]{2,1,0:T(8,128)(2,1)S(1)} %constant_dynamic-update-slice_fusion), channel_id=1, source_target_pairs={{0,2},{1,3},{2,0},{4,6},{5,7},{6,4},{8,10},{9,11},{10,8},{12,14},{... | collective-permute-start | bytes 442376 | tf_op jit(solution)/shard_map/ppermute | solution.py:110
  50.1 8.5 %collective-permute-start.5 = (bf16[8,8,1152]{2,1,0:T(8,128)(2,1)S(1)}, bf16[8,8,1152]{2,1,0:T(8,128)(2,1)S(1)}, u32[]{:S(2)}, u32[]{:S(2)}) collective-permute-start(bf16[8,8,1152]{2,1,0:T(8,128)(2,1)S(1)} %constant_dynamic-update-slice_fusion), channel_id=1, source_target_pairs={{0,3},{1,0},{2,1},{4,7},{5,4},{6,5},{8,11},{9,8},{10,9},{12,15},{1... | collective-permute-start | bytes 442376 | tf_op jit(solution)/shard_map/ppermute | solution.py:110
  58.8 15.0 %collective-permute-start.6 = (bf16[3,8,8,1152]{3,2,0,1:T(8,128)(2,1)S(1)}, bf16[3,8,8,1152]{3,2,0,1:T(8,128)(2,1)S(1)}, u32[]{:S(2)}, u32[]{:S(2)}) collective-permute-start(bf16[3,8,8,1152]{3,2,0,1:T(8,128)(2,1)S(1)} %get-tuple-element.28), channel_id=1, source_target_pairs={{0,128},{128,256},{256,384},{1,129},{129,257},{257,385},{2,130},{1... | collective-permute-start | bytes 1327112 | tf_op jit(solution)/shard_map/ppermute | solution.py:110
  60.1 16.5 %collective-permute-start.7 = (bf16[3,8,8,1152]{3,2,0,1:T(8,128)(2,1)S(1)}, bf16[3,8,8,1152]{3,2,0,1:T(8,128)(2,1)S(1)}, u32[]{:S(2)}, u32[]{:S(2)}) collective-permute-start(bf16[3,8,8,1152]{3,2,0,1:T(8,128)(2,1)S(1)} %get-tuple-element.28), channel_id=1, source_target_pairs={{0,256},{128,384},{256,0},{1,257},{129,385},{257,1},{2,258},{130,3... | collective-permute-start | bytes 1327112 | tf_op jit(solution)/shard_map/ppermute | solution.py:110
  61.4 22.8 %collective-permute-start.8 = (bf16[3,8,8,1152]{3,2,0,1:T(8,128)(2,1)S(1)}, bf16[3,8,8,1152]{3,2,0,1:T(8,128)(2,1)S(1)}, u32[]{:S(2)}, u32[]{:S(2)}) collective-permute-start(bf16[3,8,8,1152]{3,2,0,1:T(8,128)(2,1)S(1)} %get-tuple-element.28), channel_id=1, source_target_pairs={{0,384},{128,0},{256,128},{1,385},{129,1},{257,129},{2,386},{130,2... | collective-permute-start | bytes 1327112 | tf_op jit(solution)/shard_map/ppermute | solution.py:110
  84.8 5.1 %collective-permute-start.9 = (bf16[3,3,8,8,1152]{4,3,1,0,2:T(8,128)(2,1)S(1)}, bf16[3,3,8,8,1152]{4,3,1,0,2:T(8,128)(2,1)}, u32[]{:S(2)}, u32[]{:S(2)}) collective-permute-start(bf16[3,3,8,8,1152]{4,3,1,0,2:T(8,128)(2,1)S(1)} %pad_maximum_fusion.2), channel_id=1, source_target_pairs={{0,8},{8,0},{1,9},{9,1},{2,10},{10,2},{3,11},{11,3},{4,12},{12,4},... | collective-permute-start | bytes 3981320 | tf_op jit(solution)/shard_map/ppermute | solution.py:133
  111.2 76.5 %all-to-all-start.1 = ((bf16[128,7,4,128]{3,2,1,0:T(4,128)(2,1)}), bf16[128,7,4,128]{3,2,1,0:T(4,128)(2,1)S(1)}, u32[]{:S(2)}, u32[]{:S(2)}) async-start(bf16[128,7,4,128]{3,2,1,0:T(4,128)(2,1)} %copy.50), calls=%async_computation.1 | async-start | bytes 1835008 | tf_op jit(solution)/shard_map/all_to_all | solution.py:159
  121.3 3.1 %collective-permute-start.10 = (f32[1,1152]{1,0:T(1,128)S(1)}, f32[1,1152]{1,0:T(1,128)S(1)}, u32[]{:S(2)}, u32[]{:S(2)}) collective-permute-start(f32[1,1152]{1,0:T(1,128)S(1)} %get-tuple-element.7), channel_id=1, source_target_pairs={{0,8},{8,0},{1,9},{9,1},{2,10},{10,2},{3,11},{11,3},{4,12},{12,4},... | collective-permute-start | bytes 13832 | tf_op jit(solution)/shard_map/ppermute | solution.py:139
  124.4 11.0 %collective-permute-start.11 = (f32[1,1152]{1,0:T(1,128)S(1)}, f32[1,1152]{1,0:T(1,128)S(1)}, u32[]{:S(2)}, u32[]{:S(2)}) collective-permute-start(f32[1,1152]{1,0:T(1,128)S(1)} %add.192), channel_id=1, source_target_pairs={{0,1},{1,2},{2,3},{3,0},{4,5},{5,6},{6,7},{7,4},{8,9},{9,10},{10,1... | collective-permute-start | bytes 13832 | tf_op jit(solution)/shard_map/ppermute | solution.py:110
  127.5 8.0 %collective-permute-start.12 = (f32[1,1152]{1,0:T(1,128)S(1)}, f32[1,1152]{1,0:T(1,128)S(1)}, u32[]{:S(2)}, u32[]{:S(2)}) collective-permute-start(f32[1,1152]{1,0:T(1,128)S(1)} %add.192), channel_id=1, source_target_pairs={{0,2},{1,3},{2,0},{3,1},{4,6},{5,7},{6,4},{7,5},{8,10},{9,11},{10,... | collective-permute-start | bytes 13832 | tf_op jit(solution)/shard_map/ppermute | solution.py:110
  132.0 5.5 %collective-permute-start.13 = (f32[1,1152]{1,0:T(1,128)S(1)}, f32[1,1152]{1,0:T(1,128)S(1)}, u32[]{:S(2)}, u32[]{:S(2)}) collective-permute-start(f32[1,1152]{1,0:T(1,128)S(1)} %add.192), channel_id=1, source_target_pairs={{0,3},{1,0},{2,1},{3,2},{4,7},{5,4},{6,5},{7,6},{8,11},{9,8},{10,9... | collective-permute-start | bytes 13832 | tf_op jit(solution)/shard_map/ppermute | solution.py:110
  137.6 24.9 %collective-permute-start.14 = (f32[1,1152]{1,0:T(1,128)S(1)}, f32[1,1152]{1,0:T(1,128)S(1)}, u32[]{:S(2)}, u32[]{:S(2)}) collective-permute-start(f32[1,1152]{1,0:T(1,128)S(1)} %add_add_fusion.1), channel_id=1, source_target_pairs={{0,16},{16,32},{32,48},{48,64},{64,80},{80,96},{96,112},{112,4},{4... | collective-permute-start | bytes 13832 | tf_op jit(solution)/shard_map/ppermute | solution.py:106
  141.0 23.5 %collective-permute-start.15 = (f32[1,1152]{1,0:T(1,128)S(1)}, f32[1,1152]{1,0:T(1,128)S(1)}, u32[]{:S(2)}, u32[]{:S(2)}) collective-permute-start(f32[1,1152]{1,0:T(1,128)S(1)} %add_add_fusion.1), channel_id=1, source_target_pairs={{0,32},{16,48},{32,64},{48,80},{64,96},{80,112},{96,4},{112,20},{4... | collective-permute-start | bytes 13832 | tf_op jit(solution)/shard_map/ppermute | solution.py:106
  145.5 19.0 %collective-permute-start.16 = (f32[1,1152]{1,0:T(1,128)S(1)}, f32[1,1152]{1,0:T(1,128)S(1)}, u32[]{:S(2)}, u32[]{:S(2)}) collective-permute-start(f32[1,1152]{1,0:T(1,128)S(1)} %add_add_fusion.1), channel_id=1, source_target_pairs={{0,48},{16,64},{32,80},{48,96},{64,112},{80,4},{96,20},{112,36},{4... | collective-permute-start | bytes 13832 | tf_op jit(solution)/shard_map/ppermute | solution.py:106
  164.5 19.3 %collective-permute-start.17 = (f32[1,1152]{1,0:T(1,128)S(1)}, f32[1,1152]{1,0:T(1,128)S(1)}, u32[]{:S(2)}, u32[]{:S(2)}) collective-permute-start(f32[1,1152]{1,0:T(1,128)S(1)} %add_add_fusion), channel_id=1, source_target_pairs={{0,64},{16,80},{32,96},{48,112},{64,4},{80,20},{96,36},{112,52},{4... | collective-permute-start | bytes 13832 | tf_op jit(solution)/shard_map/ppermute | solution.py:106
  168.1 15.7 %collective-permute-start.18 = (f32[1,1152]{1,0:T(1,128)S(1)}, f32[1,1152]{1,0:T(1,128)S(1)}, u32[]{:S(2)}, u32[]{:S(2)}) collective-permute-start(f32[1,1152]{1,0:T(1,128)S(1)} %add_add_fusion), channel_id=1, source_target_pairs={{0,4},{16,20},{32,36},{48,52},{64,68},{80,84},{96,100},{112,116},{... | collective-permute-start | bytes 13832 | tf_op jit(solution)/shard_map/ppermute | solution.py:106
  177.6 9.4 %collective-permute-start.19 = (f32[1,1152]{1,0:T(1,128)S(1)}, f32[1,1152]{1,0:T(1,128)S(1)}, u32[]{:S(2)}, u32[]{:S(2)}) collective-permute-start(f32[1,1152]{1,0:T(1,128)S(1)} %add_add_fusion), channel_id=1, source_target_pairs={{0,68},{16,84},{32,100},{48,116},{64,0},{80,16},{96,32},{112,48},{... | collective-permute-start | bytes 13832 | tf_op jit(solution)/shard_map/ppermute | solution.py:106
  (2 other events, 3.3 us)

commit v2 on v1

v2 whole, which is shorter than its diff:
```python
import functools

import jax
import jax.numpy as jnp
from jax import lax
from jax.experimental import pallas as pl
from jax.experimental.pallas import tpu as pltpu
from jax.sharding import Mesh
from jax.sharding import PartitionSpec as P

HEADS = 16
HEAD_DIM = 72
LANES = 128
WIDTH = HEADS * HEAD_DIM
TILES = WIDTH // LANES
AXES = ("clip", "zl", "core", "zh", "y")
GROUP = ("zl", "core", "zh", "y")
GATE_ROWS = 5
ROWS_OUT = 3 * TILES + GATE_ROWS
FACTOR = HEAD_DIM ** (-0.5)


def head_tiles(head):
    first = head * HEAD_DIM // LANES
    last = (head * HEAD_DIM + HEAD_DIM - 1) // LANES
    return first, last + 1


def attend_kernel(moved_ref, w_ref, gate_ref, out_ref, x_ref, da_ref):
    f32, bf16 = jnp.float32, jnp.bfloat16
    nt = (((1,), (1,)), ((), ()))
    nn = (((1,), (0,)), ((), ()))
    tn = (((0,), (0,)), ((), ()))
    frames = moved_ref.shape[0]
    x_ref[...] = jnp.transpose(moved_ref[...].reshape(frames, 4 * TILES, LANES), (1, 0, 2))

    def cat(first, last):
        parts = [x_ref[t] for t in range(first, last)]
        return parts[0] if len(parts) == 1 else jnp.concatenate(parts, axis=1)

    go = cat(3 * TILES, 4 * TILES)
    gated = (go.astype(f32) * gate_ref[...]).astype(bf16)
    da_ref[...] = lax.dot_general(gated, w_ref[...], nt, preferred_element_type=f32).astype(bf16)

    acc = {}

    def add(kind, first, value):
        for n in range(value.shape[1] // LANES):
            key = (kind, first + n)
            part = value[:, n * LANES : (n + 1) * LANES]
            acc[key] = acc[key] + part if key in acc else part

    def operands(head):
        a, b = head_tiles(head)
        lane = lax.broadcasted_iota(jnp.int32, (frames, (b - a) * LANES), 1) + a * LANES
        mask = (lane >= head * HEAD_DIM) & (lane < (head + 1) * HEAD_DIM)

        def masked(value):
            return jnp.where(mask, value, jnp.zeros_like(value))

        q = masked(cat(a, b))
        k = masked(cat(TILES + a, TILES + b))
        v = masked(cat(2 * TILES + a, 2 * TILES + b))
        g = masked(da_ref[:, a * LANES : b * LANES])
        return a, q, k, v, g

    for first in range(0, HEADS, 8):
        heads = range(first, first + 8)
        ops = [operands(h) for h in heads]
        scores = [lax.dot_general(q, k, nt, preferred_element_type=f32) for _, q, k, v, g in ops]
        dprobs = [lax.dot_general(g, v, nt, preferred_element_type=f32) for _, q, k, v, g in ops]
        scores = [s * FACTOR for s in scores]
        expon = [jnp.exp(s - jnp.max(s, axis=-1, keepdims=True)) for s in scores]
        probs = [e / jnp.sum(e, axis=-1, keepdims=True) for e in expon]
        probs_b = [p.astype(bf16) for p in probs]
        delta = [jnp.sum(p * d, axis=-1, keepdims=True) for p, d in zip(probs, dprobs)]
        dscores = [
            (p * (d - e) * FACTOR).astype(bf16) for p, d, e in zip(probs, dprobs, delta)
        ]
        for (a, q, k, v, g), p, d in zip(ops, probs_b, dscores):
            add("o", a, lax.dot_general(p, v, nn, preferred_element_type=f32))
            add("v", a, lax.dot_general(p, g, tn, preferred_element_type=f32))
            add("q", a, lax.dot_general(d, k, nn, preferred_element_type=f32))
            add("k", a, lax.dot_general(d, q, tn, preferred_element_type=f32))
    attn = jnp.concatenate([acc[("o", t)].astype(bf16) for t in range(TILES)], axis=1)
    branch = lax.dot_general(attn, w_ref[...], nn, preferred_element_type=f32)
    terms = jnp.sum(go.astype(f32) * branch, axis=0, keepdims=True)
    rows = [terms[:, t * LANES : (t + 1) * LANES] for t in range(TILES)]

    out = [acc[(kind, t)].astype(bf16) for kind in "qkv" for t in range(TILES)]
    for n in range(GATE_ROWS):
        pair = [jnp.broadcast_to(rows[m], (8, LANES)) for m in (n, n + GATE_ROWS - 1)]
        block = jnp.concatenate(pair, axis=0).astype(bf16)
        out.append(jnp.concatenate([block] * (frames // 16), axis=0))
    out_ref[...] = jnp.transpose(jnp.stack(out), (1, 0, 2)).reshape(out_ref.shape)


def attend(x, weight, gate):
    frames = x.shape[0]
    vmem = pl.BlockSpec(memory_space=pltpu.VMEM)
    return pl.pallas_call(
        attend_kernel,
        out_shape=jax.ShapeDtypeStruct((frames, ROWS_OUT // 4, 4, LANES), jnp.bfloat16),
        in_specs=[vmem, vmem, vmem],
        out_specs=vmem,
        scratch_shapes=[
            pltpu.VMEM((4 * TILES, frames, LANES), jnp.bfloat16),
            pltpu.VMEM((frames, WIDTH), jnp.bfloat16),
        ],
        compiler_params=pltpu.CompilerParams(vmem_limit_bytes=12 << 20),
        cost_estimate=pl.CostEstimate(
            flops=1_500_000_000, bytes_accessed=5_000_000, transcendentals=300_000
        ),
    )(x, weight, gate)


def pack_kernel(*refs):
    out_ref = refs[-1]
    tiles = [ref[0, :, t * LANES : (t + 1) * LANES] for ref in refs[:-1] for t in range(TILES)]
    out_ref[...] = jnp.transpose(jnp.stack(tiles), (1, 0, 2)).reshape(out_ref.shape)


def pack(arrays):
    positions = arrays[0].shape[1]
    vmem = pl.BlockSpec(memory_space=pltpu.VMEM)
    shape = (positions, len(arrays) * TILES // 4, 4, LANES)
    return pl.pallas_call(
        pack_kernel,
        out_shape=jax.ShapeDtypeStruct(shape, jnp.bfloat16),
        in_specs=[vmem] * len(arrays),
        out_specs=vmem,
        cost_estimate=pl.CostEstimate(flops=0, bytes_accessed=2_400_000, transcendentals=0),
    )(*arrays)


def unpack_kernel(x_ref, *out_refs):
    positions, quads = x_ref.shape[0], x_ref.shape[1]
    tiles = jnp.transpose(x_ref[...].reshape(positions, quads * 4, LANES), (1, 0, 2))
    for n, ref in enumerate(out_refs):
        for t in range(TILES):
            ref[0, :, t * LANES : (t + 1) * LANES] = tiles[n * TILES + t]


def unpack(x, count):
    positions = x.shape[0]
    vmem = pl.BlockSpec(memory_space=pltpu.VMEM)
    return pl.pallas_call(
        unpack_kernel,
        out_shape=(jax.ShapeDtypeStruct((1, positions, WIDTH), jnp.bfloat16),) * count,
        in_specs=[vmem],
        out_specs=(vmem,) * count,
        cost_estimate=pl.CostEstimate(flops=0, bytes_accessed=1_800_000, transcendentals=0),
    )(x)


def along(x, axis, shift):
    return lax.ppermute(x, axis, [(i, (i + shift) % 4) for i in range(4)])


def fetch_pairs():
    def spot(x, z, y):
        return ((x * 8 + z % 8) * 2 + z // 8) * 4 + y

    pairs = []
    for x in range(4):
        for y in range(4):
            far = (4 * x + y) // 2 - 3
            pairs += [(spot(x, (z + far) % 16, y), spot(x, z, y)) for z in range(16)]
    return pairs


PART = 40


def assemble_kernel(at_ref, own_ref, other_ref, out_ref):
    x, y, z, core = [at_ref[n] for n in range(4)]
    rows = out_ref.shape[2]

    def copy(source, slot):
        for n in range(8):
            first = lax.rem(n - z + 11, 8) * 2
            for half in range(2):
                owner = first + half
                s = lax.rem(x - lax.div(owner, 4) + 4, 4)
                t = lax.rem(y - lax.rem(owner, 4) + 4, 4)
                if half == 0:
                    out_ref[n, slot, :PART] = source[s, t]
                else:
                    out_ref[n, slot, PART:] = source[s, t, 2 * PART - rows :]

    @pl.when(core == 0)
    def _():
        copy(own_ref, 0)
        copy(other_ref, 1)

    @pl.when(core != 0)
    def _():
        copy(other_ref, 0)
        copy(own_ref, 1)


def assemble(at, own, other, rows):
    vmem = pl.BlockSpec(memory_space=pltpu.VMEM)
    return pl.pallas_call(
        assemble_kernel,
        out_shape=jax.ShapeDtypeStruct((8, 2, rows, WIDTH), jnp.bfloat16),
        in_specs=[pl.BlockSpec(memory_space=pltpu.SMEM), vmem, vmem],
        out_specs=vmem,
        compiler_params=pltpu.CompilerParams(vmem_limit_bytes=10 << 20),
        cost_estimate=pl.CostEstimate(flops=0, bytes_accessed=1000, transcendentals=0),
    )(at, own, other)


def gather_weight(shard, later):
    rows = shard.shape[0]
    y = lax.axis_index("y")
    held = jnp.where(y % 2 == 0, shard[:PART], shard[rows - PART :])
    held = lax.ppermute(held, ("clip", "zl", "zh", "y"), fetch_pairs())
    held, later = lax.optimization_barrier((held, later))
    held = jnp.stack([held] + [along(held, "y", s) for s in (1, 2, 3)])
    held = jnp.stack([held] + [along(held, "clip", s) for s in (1, 2, 3)])
    other = lax.ppermute(held, "core", [(0, 1), (1, 0)])
    at = jnp.stack([lax.axis_index(n) for n in ("clip", "y", "zl", "core")]).astype(jnp.int32)
    return assemble(at, held, other, rows).reshape(WIDTH, WIDTH), later


def sum_of_terms(pieces):
    own = jnp.sum(pieces.astype(jnp.float32), axis=0)
    other = lax.ppermute(own, "core", [(0, 1), (1, 0)])
    core = lax.axis_index("core")
    low = jnp.where(core == 0, own, other)
    high = jnp.where(core == 0, other, own)
    return jnp.concatenate([low, high[1:]], axis=0).reshape(WIDTH)


def per_device(query_states, key_states, value_states, grad_output, branch_gate, out_weight):
    packed = pack((query_states, key_states, value_states, grad_output))
    weight, packed = gather_weight(out_weight, packed)
    moved = lax.all_to_all(packed, GROUP, split_axis=0, concat_axis=0, tiled=True)
    grads = attend(moved, weight, branch_gate.reshape(1, WIDTH))
    returned = lax.all_to_all(grads, GROUP, split_axis=0, concat_axis=0, tiled=True)
    sent = returned.reshape(returned.shape[0], ROWS_OUT, LANES)
    gate_grad = sum_of_terms(sent[:, 3 * TILES :])
    return tuple(unpack(returned, 3)) + (gate_grad,)


def solution(mesh):
    split = Mesh(mesh.devices.reshape(mesh.shape["clip"], 8, 2, 2, 4), AXES)
    rows = P(AXES, None, None)
    return jax.shard_map(
        per_device,
        mesh=split,
        in_specs=(rows, rows, rows, rows, P("clip"), P(("zl", "core"), None)),
        out_specs=(rows, rows, rows, P("clip")),
        check_vma=False,
    )
```

time: 193 us -> 173 us (0.90)
  blocking collectives: 0 us -> 62.8 us
  starting transfers between devices: 98.6 us -> 54 us
  waiting for transfers between devices: 66.9 us -> 37.3 us
  local copies, waits for them, and re-layouts: 13.6 us -> 3.27 us
  Pallas kernels: 8.01 us -> 11.7 us
    all_to_all x0 -> x1, blocking collectives: none -> 62.8 us  [per_device(): lax.all_to_all(grads, GROUP, split_axis=0, concat_axis=0, tiled=True)]
    ppermute x19 -> x8, starting transfers between devices: 70.7 us -> 33.7 us  [the longest x6 18.7 us: along(): return lax.ppermute(x, axis, [(i, (i + shift) % 4) for i in range(4)])]
    ppermute x19 -> x8, waiting for transfers between devices: 56 us -> 23.9 us  [the longest x6 20.9 us: along(): return lax.ppermute(x, axis, [(i, (i + shift) % 4) for i in range(4)])]
    all_to_all x1 -> x0, starting transfers between devices: 10.1 us -> none  [per_device(): lax.all_to_all(outgoing, GROUP, split_axis=0, concat_axis=0, tiled=True)]
    reshape x3 -> x1, local copies, waits for them, and re-layouts: 3.71 us -> 0.01 us  [per_device(): grads = attend(moved, weight, branch_gate.reshape(1, WIDTH))]
    pallas_call x1 -> x4, Pallas kernels: 8.01 us -> 11.7 us  [the longest x1 5.55 us: attend(): pl.pallas_call(attend_kernel, out_shape=jax.ShapeDtypeStruct((frames, ROW...]
    unnamed x22 -> x8, local copies, waits for them, and re-layouts: 6.55 us -> 3.26 us
    all_to_all x2 -> x0, local copies, waits for them, and re-layouts: 2.94 us -> none  [the longest x1 1.54 us: per_device(): lax.all_to_all(packed, GROUP, split_axis=0, concat_axis=0, tiled=True)]
  transfers between devices with their start and end apart: 22 -> 10, of which waited for: 13 -> 7; matrix products, arithmetic and copies ran while one was open for 4% -> 0% of each run, Pallas kernels for 0% -> 4%
where the time goes in v2:
time: 173 us; the launch traced here: 172 us
  blocking collectives  62.8 us (36%)
  starting transfers between devices  54 us (31%)
  waiting for transfers between devices  37.3 us (22%)
  Pallas kernels  11.7 us (7%)
  local copies, waits for them, and re-layouts  3.27 us (2%)
  other arithmetic  2.1 us (1%)
    all_to_all x1, blocking collectives, per_device(): lax.all_to_all(grads, GROUP, split_axis=0, concat_axis=0, tiled=True)  62.8 us
    ppermute x6, waiting for transfers between devices, along(): return lax.ppermute(x, axis, [(i, (i + shift) % 4) for i in range(4)])  20.9 us
    ppermute x6, starting transfers between devices, along(): return lax.ppermute(x, axis, [(i, (i + shift) % 4) for i in range(4)])  18.7 us
    all_to_all x1, starting transfers between devices, per_device(): lax.all_to_all(packed, GROUP, split_axis=0, concat_axis=0, tiled=True)  18.4 us
    ppermute x1, starting transfers between devices, gather_weight(): held = lax.ppermute(held, ('clip', 'zl', 'zh', 'y'), fetch_pairs())  12.3 us
    all_to_all x1, waiting for transfers between devices, per_device(): lax.all_to_all(packed, GROUP, split_axis=0, concat_axis=0, tiled=True)  10.3 us
    pallas_call x1, Pallas kernels, attend(): pl.pallas_call(attend_kernel, out_shape=jax.ShapeDtypeStruct((frames, ROW...  5.55 us
  transfers between devices with their start and end apart: 10, of which 7 were waited for; matrix products, arithmetic and copies ran while one was open for 0% of the time, Pallas kernels for 4%

profile of v2, /device:TPU:6, one launch (start us, length us, event | category | flops | bytes accessed | tf_op | source)
XLA Modules:
  0.0 172.0 jit_solution(17895132886549639150)
XLA Ops:
  0.6 1.0 slice_select_fusion
  1.6 12.3 %collective-permute-start = (bf16[40,1152]{1,0:T(8,128)(2,1)S(1)}, bf16[40,1152]{1,0:T(8,128)(2,1)S(1)}, u32[]{:S(2)}, u32[]{:S(2)}) collective-permute-start(bf16[40,1152]{1,0:T(8,128)(2,1)S(1)} %slice_select_fusion), channel_id=1, source_target_pairs={{84,0},{100,16},{116,32},{0,48},{16,64},{32,80},{48,96},{64,112},{... | collective-permute-start | bytes 276488 | tf_op jit(solution)/shard_map/ppermute | solution.py:218
  13.9 2.8 %shard_map.93 = bf16[128,9,4,128]{3,2,1,0:T(4,128)(2,1)} custom-call(bf16[1,128,1152]{2,1,0:T(8,128)(2,1)} %refs_0_.1, bf16[1,128,1152]{2,1,0:T(8,128)(2,1)} %refs_1_.1, bf16[1,128,1152]{2,1,0:T(8,128)(2,1)} %refs_2_.1, bf16[1,128,1152]{2,1,0:T(8,128)(2,1)} %refs_3_.1), custom_call_target="tpu_custom_call" | custom-call | bytes 2400000 | tf_op jit(solution)/shard_map/pallas_call | solution.py:127
  16.8 3.0 %collective-permute-done = bf16[40,1152]{1,0:T(8,128)(2,1)S(1)} collective-permute-done((bf16[40,1152]{1,0:T(8,128)(2,1)S(1)}, bf16[40,1152]{1,0:T(8,128)(2,1)S(1)}, u32[]{:S(2)}, u32[]{:S(2)}) %collective-permute-start) | collective-permute-done | bytes 92192 | tf_op jit(solution)/shard_map/ppermute | solution.py:218
  19.8 18.4 %all-to-all-start = ((bf16[128,9,4,128]{3,2,1,0:T(4,128)(2,1)}), bf16[128,9,4,128]{3,2,1,0:T(4,128)(2,1)}, u32[]{:S(2)}, u32[]{:S(2)}) async-start(bf16[128,9,4,128]{3,2,1,0:T(4,128)(2,1)} %shard_map.93), calls=%async_computation | async-start | bytes 2359296 | tf_op jit(solution)/shard_map/all_to_all | solution.py:239
  38.2 4.2 %collective-permute-start.3 = (bf16[40,1152]{1,0:T(8,128)(2,1)S(1)}, bf16[40,1152]{1,0:T(8,128)(2,1)S(1)}, u32[]{:S(2)}, u32[]{:S(2)}) collective-permute-start(bf16[40,1152]{1,0:T(8,128)(2,1)S(1)} %collective-permute-done), channel_id=1, source_target_pairs={{0,3},{1,0},{2,1},{3,2},{4,7},{5,4},{6,5},{7,6},{8,11},{9,8},{10,9... | collective-permute-start | bytes 276488 | tf_op jit(solution)/shard_map/ppermute | solution.py:157
  42.4 2.8 %collective-permute-start.2 = (bf16[40,1152]{1,0:T(8,128)(2,1)S(1)}, bf16[40,1152]{1,0:T(8,128)(2,1)S(1)}, u32[]{:S(2)}, u32[]{:S(2)}) collective-permute-start(bf16[40,1152]{1,0:T(8,128)(2,1)S(1)} %collective-permute-done), channel_id=1, source_target_pairs={{0,2},{1,3},{2,0},{3,1},{4,6},{5,7},{6,4},{7,5},{8,10},{9,11},{10,... | collective-permute-start | bytes 276488 | tf_op jit(solution)/shard_map/ppermute | solution.py:157
  45.2 2.8 %collective-permute-start.1 = (bf16[40,1152]{1,0:T(8,128)(2,1)S(1)}, bf16[40,1152]{1,0:T(8,128)(2,1)S(1)}, u32[]{:S(2)}, u32[]{:S(2)}) collective-permute-start(bf16[40,1152]{1,0:T(8,128)(2,1)S(1)} %collective-permute-done), channel_id=1, source_target_pairs={{0,1},{1,2},{2,3},{3,0},{4,5},{5,6},{6,7},{7,4},{8,9},{9,10},{10,1... | collective-permute-start | bytes 276488 | tf_op jit(solution)/shard_map/ppermute | solution.py:157
  47.9 4.1 %collective-permute-done.2 = bf16[40,1152]{1,0:T(8,128)(2,1)S(1)} collective-permute-done((bf16[40,1152]{1,0:T(8,128)(2,1)S(1)}, bf16[40,1152]{1,0:T(8,128)(2,1)S(1)}, u32[]{:S(2)}, u32[]{:S(2)}) %collective-permute-start.2) | collective-permute-done | bytes 92192 | tf_op jit(solution)/shard_map/ppermute | solution.py:157
  52.0 1.8 %collective-permute-done.1 = bf16[40,1152]{1,0:T(8,128)(2,1)S(1)} collective-permute-done((bf16[40,1152]{1,0:T(8,128)(2,1)S(1)}, bf16[40,1152]{1,0:T(8,128)(2,1)S(1)}, u32[]{:S(2)}, u32[]{:S(2)}) %collective-permute-start.1) | collective-permute-done | bytes 92192 | tf_op jit(solution)/shard_map/ppermute | solution.py:157
  53.9 1.9 %collective-permute-start.6 = (bf16[4,40,1152]{2,1,0:T(8,128)(2,1)S(1)}, bf16[4,40,1152]{2,1,0:T(8,128)(2,1)S(1)}, u32[]{:S(2)}, u32[]{:S(2)}) collective-permute-start(bf16[4,40,1152]{2,1,0:T(8,128)(2,1)S(1)} %get-tuple-element.15), channel_id=1, source_target_pairs={{0,384},{128,0},{256,128},{384,256},{1,385},{129,1},{257,129},{385... | collective-permute-start | bytes 1105928 | tf_op jit(solution)/shard_map/ppermute | solution.py:157
  55.8 1.9 %collective-permute-start.5 = (bf16[4,40,1152]{2,1,0:T(8,128)(2,1)S(1)}, bf16[4,40,1152]{2,1,0:T(8,128)(2,1)S(1)}, u32[]{:S(2)}, u32[]{:S(2)}) collective-permute-start(bf16[4,40,1152]{2,1,0:T(8,128)(2,1)S(1)} %get-tuple-element.15), channel_id=1, source_target_pairs={{0,256},{128,384},{256,0},{384,128},{1,257},{129,385},{257,1},{385... | collective-permute-start | bytes 1105928 | tf_op jit(solution)/shard_map/ppermute | solution.py:157
  57.8 5.1 %collective-permute-start.4 = (bf16[4,40,1152]{2,1,0:T(8,128)(2,1)S(1)}, bf16[4,40,1152]{2,1,0:T(8,128)(2,1)S(1)}, u32[]{:S(2)}, u32[]{:S(2)}) collective-permute-start(bf16[4,40,1152]{2,1,0:T(8,128)(2,1)S(1)} %get-tuple-element.15), channel_id=1, source_target_pairs={{0,128},{128,256},{256,384},{384,0},{1,129},{129,257},{257,385},{3... | collective-permute-start | bytes 1105928 | tf_op jit(solution)/shard_map/ppermute | solution.py:157
  62.9 12.5 %collective-permute-done.6 = bf16[4,40,1152]{2,1,0:T(8,128)(2,1)S(1)} collective-permute-done((bf16[4,40,1152]{2,1,0:T(8,128)(2,1)S(1)}, bf16[4,40,1152]{2,1,0:T(8,128)(2,1)S(1)}, u32[]{:S(2)}, u32[]{:S(2)}) %collective-permute-start.6) | collective-permute-done | bytes 368672 | tf_op jit(solution)/shard_map/ppermute | solution.py:157
  75.4 2.5 %collective-permute-done.4 = bf16[4,40,1152]{2,1,0:T(8,128)(2,1)S(1)} collective-permute-done((bf16[4,40,1152]{2,1,0:T(8,128)(2,1)S(1)}, bf16[4,40,1152]{2,1,0:T(8,128)(2,1)S(1)}, u32[]{:S(2)}, u32[]{:S(2)}) %collective-permute-start.4) | collective-permute-done | bytes 368672 | tf_op jit(solution)/shard_map/ppermute | solution.py:157
  78.1 1.9 %collective-permute-start.7 = (bf16[4,4,40,1152]{3,2,1,0:T(8,128)(2,1)S(1)}, bf16[4,4,40,1152]{3,2,1,0:T(8,128)(2,1)S(1)}, u32[]{:S(2)}, u32[]{:S(2)}) collective-permute-start(bf16[4,4,40,1152]{3,2,1,0:T(8,128)(2,1)S(1)} %pad_maximum_fusion.own_ref), channel_id=1, source_target_pairs={{0,8},{8,0},{1,9},{9,1},{2,10},{10,2},{3,11},{11,3},{4,12},{12,4},... | collective-permute-start | bytes 4423688 | tf_op jit(solution)/shard_map/ppermute | solution.py:222
  80.2 3.1 %collective-permute-done.7.other_ref = bf16[4,4,40,1152]{3,2,1,0:T(8,128)(2,1)S(1)} collective-permute-done((bf16[4,4,40,1152]{3,2,1,0:T(8,128)(2,1)S(1)}, bf16[4,4,40,1152]{3,2,1,0:T(8,128)(2,1)S(1)}, u32[]{:S(2)}, u32[]{:S(2)}) %collective-permute-start.7) | collective-permute-done | bytes 1474592 | tf_op jit(solution)/shard_map/ppermute | solution.py:222
  84.1 1.5 copy-done
  85.6 10.3 %all-to-all-done.moved_ref = bf16[128,9,4,128]{3,2,1,0:T(4,128)(2,1)} async-done(((bf16[128,9,4,128]{3,2,1,0:T(4,128)(2,1)}), bf16[128,9,4,128]{3,2,1,0:T(4,128)(2,1)}, u32[]{:S(2)}, u32[]{:S(2)}) %all-to-all-start) | async-done | bytes 1179680 | tf_op jit(solution)/shard_map/all_to_all | solution.py:239
  95.9 1.7 %copy-done.1 = bf16[8,2,72,1152]{3,2,1,0:T(8,128)(2,1)S(1)} copy-done((bf16[8,2,72,1152]{3,2,1,0:T(8,128)(2,1)S(1)}, bf16[8,2,72,1152]{3,2,1,0:T(8,128)(2,1)}, u32[]{:S(2)}) %copy-start.1) | copy-done | bytes 2654232
  97.7 5.6 %shard_map.95 = bf16[128,8,4,128]{3,2,1,0:T(4,128)(2,1)S(1)} custom-call(bf16[128,9,4,128]{3,2,1,0:T(4,128)(2,1)} %all-to-all-done.moved_ref, bf16[1152,1152]{1,0:T(8,128)(2,1)S(1)} %bitcast.17, f32[1,1152]{1,0:T(1,128)S(1)} %reshape.21.gate_ref), custom_call_target="tpu_custom_call" | custom-call | flops 1500000000 | bytes 5000000 | tf_op jit(solution)/shard_map/pallas_call | solution.py:101
  103.2 62.8 %all_to_all.10.x_ref = bf16[128,8,4,128]{3,2,1,0:T(4,128)(2,1)S(1)} all-to-all(bf16[128,8,4,128]{3,2,1,0:T(4,128)(2,1)S(1)} %shard_map.95), channel_id=1, replica_groups=mesh['clip'=4,'zl'=8,'core'=2,'zh'=2,'y'=4] {'zl','core','zh','y'}, dimensions={0} | all-to-all | bytes 2097152 | tf_op jit(solution)/shard_map/all_to_all | solution.py:241
  166.1 2.7 %collective-permute-start.8 = (f32[5,128]{1,0:T(8,128)S(1)}, f32[5,128]{1,0:T(8,128)S(1)}, u32[]{:S(2)}, u32[]{:S(2)}) collective-permute-start(f32[5,128]{1,0:T(8,128)S(1)} %convert_reduce_fusion), channel_id=1, source_target_pairs={{0,8},{8,0},{1,9},{9,1},{2,10},{10,2},{3,11},{11,3},{4,12},{12,4},... | collective-permute-start | bytes 7688 | tf_op jit(solution)/shard_map/ppermute | solution.py:229
  168.9 2.5 %shard_map.96 = (bf16[1,128,1152]{2,1,0:T(8,128)(2,1)}, bf16[1,128,1152]{2,1,0:T(8,128)(2,1)}, bf16[1,128,1152]{2,1,0:T(8,128)(2,1)}) custom-call(bf16[128,8,4,128]{3,2,1,0:T(4,128)(2,1)} %copy-done.2), custom_call_target="tpu_custom_call" | custom-call | bytes 1800000 | tf_op jit(solution)/shard_map/pallas_call | solution.py:147
  (18 shorter events, 2.0 us)
Async XLA Ops:
  1.6 18.1 %collective-permute-start = (bf16[40,1152]{1,0:T(8,128)(2,1)S(1)}, bf16[40,1152]{1,0:T(8,128)(2,1)S(1)}, u32[]{:S(2)}, u32[]{:S(2)}) collective-permute-start(bf16[40,1152]{1,0:T(8,128)(2,1)S(1)} %slice_select_fusion), channel_id=1, source_target_pairs={{84,0},{100,16},{116,32},{0,48},{16,64},{32,80},{48,96},{64,112},{... | collective-permute-start | bytes 276488 | tf_op jit(solution)/shard_map/ppermute | solution.py:218
  19.8 76.2 %all-to-all-start = ((bf16[128,9,4,128]{3,2,1,0:T(4,128)(2,1)}), bf16[128,9,4,128]{3,2,1,0:T(4,128)(2,1)}, u32[]{:S(2)}, u32[]{:S(2)}) async-start(bf16[128,9,4,128]{3,2,1,0:T(4,128)(2,1)} %shard_map.93), calls=%async_computation | async-start | bytes 2359296 | tf_op jit(solution)/shard_map/all_to_all | solution.py:239
  38.2 9.7 %collective-permute-start.3 = (bf16[40,1152]{1,0:T(8,128)(2,1)S(1)}, bf16[40,1152]{1,0:T(8,128)(2,1)S(1)}, u32[]{:S(2)}, u32[]{:S(2)}) collective-permute-start(bf16[40,1152]{1,0:T(8,128)(2,1)S(1)} %collective-permute-done), channel_id=1, source_target_pairs={{0,3},{1,0},{2,1},{3,2},{4,7},{5,4},{6,5},{7,6},{8,11},{9,8},{10,9... | collective-permute-start | bytes 276488 | tf_op jit(solution)/shard_map/ppermute | solution.py:157
  42.4 9.7 %collective-permute-start.2 = (bf16[40,1152]{1,0:T(8,128)(2,1)S(1)}, bf16[40,1152]{1,0:T(8,128)(2,1)S(1)}, u32[]{:S(2)}, u32[]{:S(2)}) collective-permute-start(bf16[40,1152]{1,0:T(8,128)(2,1)S(1)} %collective-permute-done), channel_id=1, source_target_pairs={{0,2},{1,3},{2,0},{3,1},{4,6},{5,7},{6,4},{7,5},{8,10},{9,11},{10,... | collective-permute-start | bytes 276488 | tf_op jit(solution)/shard_map/ppermute | solution.py:157
  45.2 8.7 %collective-permute-start.1 = (bf16[40,1152]{1,0:T(8,128)(2,1)S(1)}, bf16[40,1152]{1,0:T(8,128)(2,1)S(1)}, u32[]{:S(2)}, u32[]{:S(2)}) collective-permute-start(bf16[40,1152]{1,0:T(8,128)(2,1)S(1)} %collective-permute-done), channel_id=1, source_target_pairs={{0,1},{1,2},{2,3},{3,0},{4,5},{5,6},{6,7},{7,4},{8,9},{9,10},{10,1... | collective-permute-start | bytes 276488 | tf_op jit(solution)/shard_map/ppermute | solution.py:157
  53.9 21.5 %collective-permute-start.6 = (bf16[4,40,1152]{2,1,0:T(8,128)(2,1)S(1)}, bf16[4,40,1152]{2,1,0:T(8,128)(2,1)S(1)}, u32[]{:S(2)}, u32[]{:S(2)}) collective-permute-start(bf16[4,40,1152]{2,1,0:T(8,128)(2,1)S(1)} %get-tuple-element.15), channel_id=1, source_target_pairs={{0,384},{128,0},{256,128},{384,256},{1,385},{129,1},{257,129},{385... | collective-permute-start | bytes 1105928 | tf_op jit(solution)/shard_map/ppermute | solution.py:157
  55.8 19.5 %collective-permute-start.5 = (bf16[4,40,1152]{2,1,0:T(8,128)(2,1)S(1)}, bf16[4,40,1152]{2,1,0:T(8,128)(2,1)S(1)}, u32[]{:S(2)}, u32[]{:S(2)}) collective-permute-start(bf16[4,40,1152]{2,1,0:T(8,128)(2,1)S(1)} %get-tuple-element.15), channel_id=1, source_target_pairs={{0,256},{128,384},{256,0},{384,128},{1,257},{129,385},{257,1},{385... | collective-permute-start | bytes 1105928 | tf_op jit(solution)/shard_map/ppermute | solution.py:157
  57.8 20.2 %collective-permute-start.4 = (bf16[4,40,1152]{2,1,0:T(8,128)(2,1)S(1)}, bf16[4,40,1152]{2,1,0:T(8,128)(2,1)S(1)}, u32[]{:S(2)}, u32[]{:S(2)}) collective-permute-start(bf16[4,40,1152]{2,1,0:T(8,128)(2,1)S(1)} %get-tuple-element.15), channel_id=1, source_target_pairs={{0,128},{128,256},{256,384},{384,0},{1,129},{129,257},{257,385},{3... | collective-permute-start | bytes 1105928 | tf_op jit(solution)/shard_map/ppermute | solution.py:157
  77.9 2.2 %copy-start.3 = (f32[1152]{0:T(1024)S(1)}, f32[1152]{0:T(1024)}, u32[]{:S(2)}) copy-start(f32[1152]{0:T(1024)} %param.10) | copy-start | bytes 13828
  78.1 5.2 %collective-permute-start.7 = (bf16[4,4,40,1152]{3,2,1,0:T(8,128)(2,1)S(1)}, bf16[4,4,40,1152]{3,2,1,0:T(8,128)(2,1)S(1)}, u32[]{:S(2)}, u32[]{:S(2)}) collective-permute-start(bf16[4,4,40,1152]{3,2,1,0:T(8,128)(2,1)S(1)} %pad_maximum_fusion.own_ref), channel_id=1, source_target_pairs={{0,8},{8,0},{1,9},{9,1},{2,10},{10,2},{3,11},{11,3},{4,12},{12,4},... | collective-permute-start | bytes 4423688 | tf_op jit(solution)/shard_map/ppermute | solution.py:222
  84.1 1.5 copy-start
  95.9 1.8 %copy-start.1 = (bf16[8,2,72,1152]{3,2,1,0:T(8,128)(2,1)S(1)}, bf16[8,2,72,1152]{3,2,1,0:T(8,128)(2,1)}, u32[]{:S(2)}) copy-start(bf16[8,2,72,1152]{3,2,1,0:T(8,128)(2,1)} %copy-done) | copy-start | bytes 7962628
  166.0 2.9 %copy-start.2 = (bf16[128,8,4,128]{3,2,1,0:T(4,128)(2,1)}, bf16[128,8,4,128]{3,2,1,0:T(4,128)(2,1)S(1)}, u32[]{:S(2)}) copy-start(bf16[128,8,4,128]{3,2,1,0:T(4,128)(2,1)S(1)} %all_to_all.10.x_ref) | copy-start | bytes 3145732
  166.1 5.3 %collective-permute-start.8 = (f32[5,128]{1,0:T(8,128)S(1)}, f32[5,128]{1,0:T(8,128)S(1)}, u32[]{:S(2)}, u32[]{:S(2)}) collective-permute-start(f32[5,128]{1,0:T(8,128)S(1)} %convert_reduce_fusion), channel_id=1, source_target_pairs={{0,8},{8,0},{1,9},{9,1},{2,10},{10,2},{3,11},{11,3},{4,12},{12,4},... | collective-permute-start | bytes 7688 | tf_op jit(solution)/shard_map/ppermute | solution.py:229

commit v3 on v2

--- a/solution.py
+++ b/solution.py
@@ -45,43 +45,51 @@
     acc = {}
 
     def add(kind, first, value):
-        for n in range(value.shape[1] // LANES):
+        for n in range(2):
             key = (kind, first + n)
             part = value[:, n * LANES : (n + 1) * LANES]
             acc[key] = acc[key] + part if key in acc else part
 
-    def operands(head):
-        a, b = head_tiles(head)
-        lane = lax.broadcasted_iota(jnp.int32, (frames, (b - a) * LANES), 1) + a * LANES
-        mask = (lane >= head * HEAD_DIM) & (lane < (head + 1) * HEAD_DIM)
-
-        def masked(value):
-            return jnp.where(mask, value, jnp.zeros_like(value))
-
-        q = masked(cat(a, b))
-        k = masked(cat(TILES + a, TILES + b))
-        v = masked(cat(2 * TILES + a, 2 * TILES + b))
-        g = masked(da_ref[:, a * LANES : b * LANES])
-        return a, q, k, v, g
-
-    for first in range(0, HEADS, 8):
-        heads = range(first, first + 8)
-        ops = [operands(h) for h in heads]
-        scores = [lax.dot_general(q, k, nt, preferred_element_type=f32) for _, q, k, v, g in ops]
-        dprobs = [lax.dot_general(g, v, nt, preferred_element_type=f32) for _, q, k, v, g in ops]
-        scores = [s * FACTOR for s in scores]
+    lane = lax.broadcasted_iota(jnp.int32, (frames, 2 * LANES), 1)
+
+    def both_heads(value, start):
+        zero = jnp.zeros_like(value)
+        heads = [
+            jnp.where((lane >= at) & (lane < at + HEAD_DIM), value, zero)
+            for at in (start, start + HEAD_DIM)
+        ]
+        return jnp.concatenate(heads, axis=0)
+
+    def operands(pair):
+        tile, start = divmod(2 * pair * HEAD_DIM, LANES)
+        q, k, v = [cat(n * TILES + tile, n * TILES + tile + 2) for n in range(3)]
+        g = da_ref[:, tile * LANES : (tile + 2) * LANES]
+        return (tile, q, g) + tuple(both_heads(value, start) for value in (q, k, v, g))
+
+    def heads_of(value):
+        return value[:, :frames], value[:, frames:]
+
+    for first in range(0, HEADS // 2, 4):
+        ops = [operands(pair) for pair in range(first, first + 4)]
+        scores = [lax.dot_general(o[1], o[4], nt, preferred_element_type=f32) for o in ops]
+        dprobs = [lax.dot_general(o[2], o[5], nt, preferred_element_type=f32) for o in ops]
+        scores = [s * FACTOR for pair in scores for s in heads_of(pair)]
+        dprobs = [d for pair in dprobs for d in heads_of(pair)]
         expon = [jnp.exp(s - jnp.max(s, axis=-1, keepdims=True)) for s in scores]
         probs = [e / jnp.sum(e, axis=-1, keepdims=True) for e in expon]
-        probs_b = [p.astype(bf16) for p in probs]
         delta = [jnp.sum(p * d, axis=-1, keepdims=True) for p, d in zip(probs, dprobs)]
         dscores = [
             (p * (d - e) * FACTOR).astype(bf16) for p, d, e in zip(probs, dprobs, delta)
         ]
-        for (a, q, k, v, g), p, d in zip(ops, probs_b, dscores):
-            add("o", a, lax.dot_general(p, v, nn, preferred_element_type=f32))
-            add("v", a, lax.dot_general(p, g, tn, preferred_element_type=f32))
-            add("q", a, lax.dot_general(d, k, nn, preferred_element_type=f32))
-            add("k", a, lax.dot_general(d, q, tn, preferred_element_type=f32))
+        probs = [p.astype(bf16) for p in probs]
+        for n, (tile, _, _, q, k, v, g) in enumerate(ops):
+            p, d = probs[2 * n : 2 * n + 2], dscores[2 * n : 2 * n + 2]
+            p_wide, d_wide = jnp.concatenate(p, axis=1), jnp.concatenate(d, axis=1)
+            p_tall, d_tall = jnp.concatenate(p, axis=0), jnp.concatenate(d, axis=0)
+            add("o", tile, lax.dot_general(p_wide, v, nn, preferred_element_type=f32))
+            add("v", tile, lax.dot_general(p_tall, g, tn, preferred_element_type=f32))
+            add("q", tile, lax.dot_general(d_wide, k, nn, preferred_element_type=f32))
+            add("k", tile, lax.dot_general(d_tall, q, tn, preferred_element_type=f32))
     attn = jnp.concatenate([acc[("o", t)].astype(bf16) for t in range(TILES)], axis=1)
     branch = lax.dot_general(attn, w_ref[...], nn, preferred_element_type=f32)
     terms = jnp.sum(go.astype(f32) * branch, axis=0, keepdims=True)
@@ -122,13 +130,14 @@
 
 def pack(arrays):
     positions = arrays[0].shape[1]
-    vmem = pl.BlockSpec(memory_space=pltpu.VMEM)
+    step = positions // 2
     shape = (positions, len(arrays) * TILES // 4, 4, LANES)
     return pl.pallas_call(
         pack_kernel,
         out_shape=jax.ShapeDtypeStruct(shape, jnp.bfloat16),
-        in_specs=[vmem] * len(arrays),
-        out_specs=vmem,
+        grid=(2,),
+        in_specs=[pl.BlockSpec((1, step, WIDTH), lambda i: (0, i, 0))] * len(arrays),
+        out_specs=pl.BlockSpec((step,) + shape[1:], lambda i: (i, 0, 0, 0)),
         cost_estimate=pl.CostEstimate(flops=0, bytes_accessed=2_400_000, transcendentals=0),
     )(*arrays)
 
@@ -143,12 +152,13 @@
 
 def unpack(x, count):
     positions = x.shape[0]
-    vmem = pl.BlockSpec(memory_space=pltpu.VMEM)
+    step = positions // 2
     return pl.pallas_call(
         unpack_kernel,
         out_shape=(jax.ShapeDtypeStruct((1, positions, WIDTH), jnp.bfloat16),) * count,
-        in_specs=[vmem],
-        out_specs=(vmem,) * count,
+        grid=(2,),
+        in_specs=[pl.BlockSpec((step,) + x.shape[1:], lambda i: (i, 0, 0, 0))],
+        out_specs=(pl.BlockSpec((1, step, WIDTH), lambda i: (0, i, 0)),) * count,
         cost_estimate=pl.CostEstimate(flops=0, bytes_accessed=1_800_000, transcendentals=0),
     )(x)
 
@@ -173,7 +183,7 @@
 
 
 def assemble_kernel(at_ref, own_ref, other_ref, out_ref):
-    x, y, z, core = [at_ref[n] for n in range(4)]
+    x, y, z = [at_ref[n] for n in range(3)]
     rows = out_ref.shape[2]
 
     def copy(source, slot):
@@ -188,15 +198,8 @@
                 else:
                     out_ref[n, slot, PART:] = source[s, t, 2 * PART - rows :]
 
-    @pl.when(core == 0)
-    def _():
-        copy(own_ref, 0)
-        copy(other_ref, 1)
-
-    @pl.when(core != 0)
-    def _():
-        copy(other_ref, 0)
-        copy(own_ref, 1)
+    copy(own_ref, 0)
+    copy(other_ref, 1)
 
 
 def assemble(at, own, other, rows):
@@ -214,14 +217,17 @@
 def gather_weight(shard, later):
     rows = shard.shape[0]
     y = lax.axis_index("y")
-    held = jnp.where(y % 2 == 0, shard[:PART], shard[rows - PART :])
-    held = lax.ppermute(held, ("clip", "zl", "zh", "y"), fetch_pairs())
+    held = lax.ppermute(shard, ("clip", "zl", "zh", "y"), fetch_pairs())
     held, later = lax.optimization_barrier((held, later))
+    held = jnp.where(y % 2 == 0, held[:PART], held[rows - PART :])
     held = jnp.stack([held] + [along(held, "y", s) for s in (1, 2, 3)])
     held = jnp.stack([held] + [along(held, "clip", s) for s in (1, 2, 3)])
     other = lax.ppermute(held, "core", [(0, 1), (1, 0)])
-    at = jnp.stack([lax.axis_index(n) for n in ("clip", "y", "zl", "core")]).astype(jnp.int32)
-    return assemble(at, held, other, rows).reshape(WIDTH, WIDTH), later
+    at = jnp.stack([lax.axis_index(n) for n in ("clip", "y", "zl")]).astype(jnp.int32)
+    pairs = assemble(at, held, other, rows)
+    even = lax.axis_index("core") == 0
+    pairs = jnp.where(even, pairs, pairs[:, ::-1])
+    return pairs.reshape(WIDTH, WIDTH), later
 
 
 def sum_of_terms(pieces):

time: 173 us -> 176 us (1.017)
  waiting for transfers between devices: 37.3 us -> 43.7 us
  local copies, waits for them, and re-layouts: 3.27 us -> 0.02 us
    ppermute x1, waiting for transfers between devices: 3.01 us -> 8.32 us  [gather_weight(): held = lax.ppermute(shard, ('clip', 'zl', 'zh', 'y'), fetch_pairs())]
    unnamed x8 -> x4, local copies, waits for them, and re-layouts: 3.26 us -> 0.01 us
  transfers between devices with their start and end apart: 10 -> 10, of which waited for: 7 -> 7; matrix products, arithmetic and copies ran while one was open for 0% -> 0% of each run, Pallas kernels for 4% -> 3%
where the time goes in v3:
time: 176 us; the launch traced here: 175 us
  blocking collectives  62.8 us (36%)
  starting transfers between devices  55.5 us (32%)
  waiting for transfers between devices  43.7 us (25%)
  Pallas kernels  10.8 us (6%)
    all_to_all x1, blocking collectives, per_device(): lax.all_to_all(grads, GROUP, split_axis=0, concat_axis=0, tiled=True)  62.8 us
    ppermute x6, waiting for transfers between devices, along(): return lax.ppermute(x, axis, [(i, (i + shift) % 4) for i in range(4)])  20.9 us
    all_to_all x1, starting transfers between devices, per_device(): lax.all_to_all(packed, GROUP, split_axis=0, concat_axis=0, tiled=True)  19.9 us
    ppermute x6, starting transfers between devices, along(): return lax.ppermute(x, axis, [(i, (i + shift) % 4) for i in range(4)])  18.7 us
    ppermute x1, starting transfers between devices, gather_weight(): held = lax.ppermute(shard, ('clip', 'zl', 'zh', 'y'), fetch_pairs())  12.3 us
    all_to_all x1, waiting for transfers between devices, per_device(): lax.all_to_all(packed, GROUP, split_axis=0, concat_axis=0, tiled=True)  11.3 us
    ppermute x1, waiting for transfers between devices, gather_weight(): held = lax.ppermute(shard, ('clip', 'zl', 'zh', 'y'), fetch_pairs())  8.32 us
    pallas_call x1, Pallas kernels, attend(): pl.pallas_call(attend_kernel, out_shape=jax.ShapeDtypeStruct((frames, ROW...  5.14 us
  transfers between devices with their start and end apart: 10, of which 7 were waited for; matrix products, arithmetic and copies ran while one was open for 0% of the time, Pallas kernels for 3%

profile of v3, /device:TPU:6, one launch (start us, length us, event | category | flops | bytes accessed | tf_op | source)
XLA Modules:
  0.0 175.2 jit_solution(1914994720598663147)
XLA Ops:
  0.6 12.3 %collective-permute-start = (bf16[72,1152]{1,0:T(8,128)(2,1)}, bf16[72,1152]{1,0:T(8,128)(2,1)S(1)}, u32[]{:S(2)}, u32[]{:S(2)}) collective-permute-start(bf16[72,1152]{1,0:T(8,128)(2,1)} %param.11), channel_id=1, source_target_pairs={{84,0},{100,16},{116,32},{0,48},{16,64},{32,80},{48,96},{64,112},{... | collective-permute-start | bytes 497672 | tf_op jit(solution)/shard_map/ppermute | solution.py:220
  12.9 2.6 %shard_map.93 = bf16[128,9,4,128]{3,2,1,0:T(4,128)(2,1)} custom-call(bf16[1,128,1152]{2,1,0:T(8,128)(2,1)} %refs_0_.1, bf16[1,128,1152]{2,1,0:T(8,128)(2,1)} %refs_1_.1, bf16[1,128,1152]{2,1,0:T(8,128)(2,1)} %refs_2_.1, bf16[1,128,1152]{2,1,0:T(8,128)(2,1)} %refs_3_.1), custom_call_target="tpu_custom_call" | custom-call | bytes 2400000 | tf_op jit(solution)/shard_map/pallas_call | solution.py:135
  15.5 8.3 %collective-permute-done = bf16[72,1152]{1,0:T(8,128)(2,1)S(1)} collective-permute-done((bf16[72,1152]{1,0:T(8,128)(2,1)}, bf16[72,1152]{1,0:T(8,128)(2,1)S(1)}, u32[]{:S(2)}, u32[]{:S(2)}) %collective-permute-start) | collective-permute-done | bytes 165920 | tf_op jit(solution)/shard_map/ppermute | solution.py:220
  23.8 19.9 %all-to-all-start = ((bf16[128,9,4,128]{3,2,1,0:T(4,128)(2,1)}), bf16[128,9,4,128]{3,2,1,0:T(4,128)(2,1)}, u32[]{:S(2)}, u32[]{:S(2)}) async-start(bf16[128,9,4,128]{3,2,1,0:T(4,128)(2,1)} %shard_map.93), calls=%async_computation | async-start | bytes 2359296 | tf_op jit(solution)/shard_map/all_to_all | solution.py:245
  43.8 4.2 %collective-permute-start.3 = (bf16[40,1152]{1,0:T(8,128)(2,1)S(1)}, bf16[40,1152]{1,0:T(8,128)(2,1)S(1)}, u32[]{:S(2)}, u32[]{:S(2)}) collective-permute-start(bf16[40,1152]{1,0:T(8,128)(2,1)S(1)} %slice_select_fusion), channel_id=1, source_target_pairs={{0,3},{1,0},{2,1},{3,2},{4,7},{5,4},{6,5},{7,6},{8,11},{9,8},{10,9... | collective-permute-start | bytes 276488 | tf_op jit(solution)/shard_map/ppermute | solution.py:167
  47.9 2.8 %collective-permute-start.2 = (bf16[40,1152]{1,0:T(8,128)(2,1)S(1)}, bf16[40,1152]{1,0:T(8,128)(2,1)S(1)}, u32[]{:S(2)}, u32[]{:S(2)}) collective-permute-start(bf16[40,1152]{1,0:T(8,128)(2,1)S(1)} %slice_select_fusion), channel_id=1, source_target_pairs={{0,2},{1,3},{2,0},{3,1},{4,6},{5,7},{6,4},{7,5},{8,10},{9,11},{10,... | collective-permute-start | bytes 276488 | tf_op jit(solution)/shard_map/ppermute | solution.py:167
  50.7 2.8 %collective-permute-start.1 = (bf16[40,1152]{1,0:T(8,128)(2,1)S(1)}, bf16[40,1152]{1,0:T(8,128)(2,1)S(1)}, u32[]{:S(2)}, u32[]{:S(2)}) collective-permute-start(bf16[40,1152]{1,0:T(8,128)(2,1)S(1)} %slice_select_fusion), channel_id=1, source_target_pairs={{0,1},{1,2},{2,3},{3,0},{4,5},{5,6},{6,7},{7,4},{8,9},{9,10},{10,1... | collective-permute-start | bytes 276488 | tf_op jit(solution)/shard_map/ppermute | solution.py:167
  53.5 4.1 %collective-permute-done.2 = bf16[40,1152]{1,0:T(8,128)(2,1)S(1)} collective-permute-done((bf16[40,1152]{1,0:T(8,128)(2,1)S(1)}, bf16[40,1152]{1,0:T(8,128)(2,1)S(1)}, u32[]{:S(2)}, u32[]{:S(2)}) %collective-permute-start.2) | collective-permute-done | bytes 92192 | tf_op jit(solution)/shard_map/ppermute | solution.py:167
  57.6 1.8 %collective-permute-done.1 = bf16[40,1152]{1,0:T(8,128)(2,1)S(1)} collective-permute-done((bf16[40,1152]{1,0:T(8,128)(2,1)S(1)}, bf16[40,1152]{1,0:T(8,128)(2,1)S(1)}, u32[]{:S(2)}, u32[]{:S(2)}) %collective-permute-start.1) | collective-permute-done | bytes 92192 | tf_op jit(solution)/shard_map/ppermute | solution.py:167
  59.5 1.9 %collective-permute-start.6 = (bf16[4,40,1152]{2,1,0:T(8,128)(2,1)S(1)}, bf16[4,40,1152]{2,1,0:T(8,128)(2,1)S(1)}, u32[]{:S(2)}, u32[]{:S(2)}) collective-permute-start(bf16[4,40,1152]{2,1,0:T(8,128)(2,1)S(1)} %get-tuple-element.15), channel_id=1, source_target_pairs={{0,384},{128,0},{256,128},{384,256},{1,385},{129,1},{257,129},{385... | collective-permute-start | bytes 1105928 | tf_op jit(solution)/shard_map/ppermute | solution.py:167
  61.4 1.9 %collective-permute-start.5 = (bf16[4,40,1152]{2,1,0:T(8,128)(2,1)S(1)}, bf16[4,40,1152]{2,1,0:T(8,128)(2,1)S(1)}, u32[]{:S(2)}, u32[]{:S(2)}) collective-permute-start(bf16[4,40,1152]{2,1,0:T(8,128)(2,1)S(1)} %get-tuple-element.15), channel_id=1, source_target_pairs={{0,256},{128,384},{256,0},{384,128},{1,257},{129,385},{257,1},{385... | collective-permute-start | bytes 1105928 | tf_op jit(solution)/shard_map/ppermute | solution.py:167
  63.3 5.1 %collective-permute-start.4 = (bf16[4,40,1152]{2,1,0:T(8,128)(2,1)S(1)}, bf16[4,40,1152]{2,1,0:T(8,128)(2,1)S(1)}, u32[]{:S(2)}, u32[]{:S(2)}) collective-permute-start(bf16[4,40,1152]{2,1,0:T(8,128)(2,1)S(1)} %get-tuple-element.15), channel_id=1, source_target_pairs={{0,128},{128,256},{256,384},{384,0},{1,129},{129,257},{257,385},{3... | collective-permute-start | bytes 1105928 | tf_op jit(solution)/shard_map/ppermute | solution.py:167
  68.5 12.5 %collective-permute-done.6 = bf16[4,40,1152]{2,1,0:T(8,128)(2,1)S(1)} collective-permute-done((bf16[4,40,1152]{2,1,0:T(8,128)(2,1)S(1)}, bf16[4,40,1152]{2,1,0:T(8,128)(2,1)S(1)}, u32[]{:S(2)}, u32[]{:S(2)}) %collective-permute-start.6) | collective-permute-done | bytes 368672 | tf_op jit(solution)/shard_map/ppermute | solution.py:167
  81.0 2.5 %collective-permute-done.4 = bf16[4,40,1152]{2,1,0:T(8,128)(2,1)S(1)} collective-permute-done((bf16[4,40,1152]{2,1,0:T(8,128)(2,1)S(1)}, bf16[4,40,1152]{2,1,0:T(8,128)(2,1)S(1)}, u32[]{:S(2)}, u32[]{:S(2)}) %collective-permute-start.4) | collective-permute-done | bytes 368672 | tf_op jit(solution)/shard_map/ppermute | solution.py:167
  83.7 1.9 %collective-permute-start.7 = (bf16[4,4,40,1152]{3,2,1,0:T(8,128)(2,1)S(1)}, bf16[4,4,40,1152]{3,2,1,0:T(8,128)(2,1)S(1)}, u32[]{:S(2)}, u32[]{:S(2)}) collective-permute-start(bf16[4,4,40,1152]{3,2,1,0:T(8,128)(2,1)S(1)} %pad_maximum_fusion.own_ref), channel_id=1, source_target_pairs={{0,8},{8,0},{1,9},{9,1},{2,10},{10,2},{3,11},{11,3},{4,12},{12,4},... | collective-permute-start | bytes 4423688 | tf_op jit(solution)/shard_map/ppermute | solution.py:225
  85.8 3.1 %collective-permute-done.7.other_ref = bf16[4,4,40,1152]{3,2,1,0:T(8,128)(2,1)S(1)} collective-permute-done((bf16[4,4,40,1152]{3,2,1,0:T(8,128)(2,1)S(1)}, bf16[4,4,40,1152]{3,2,1,0:T(8,128)(2,1)S(1)}, u32[]{:S(2)}, u32[]{:S(2)}) %collective-permute-start.7) | collective-permute-done | bytes 1474592 | tf_op jit(solution)/shard_map/ppermute | solution.py:225
  88.9 0.8 shard_map.94
  89.7 0.4 reverse_select_fusion
  90.1 11.3 %all-to-all-done.moved_ref = bf16[128,9,4,128]{3,2,1,0:T(4,128)(2,1)} async-done(((bf16[128,9,4,128]{3,2,1,0:T(4,128)(2,1)}), bf16[128,9,4,128]{3,2,1,0:T(4,128)(2,1)}, u32[]{:S(2)}, u32[]{:S(2)}) %all-to-all-start) | async-done | bytes 1179680 | tf_op jit(solution)/shard_map/all_to_all | solution.py:245
  101.5 5.1 %shard_map.95 = bf16[128,8,4,128]{3,2,1,0:T(4,128)(2,1)S(1)} custom-call(bf16[128,9,4,128]{3,2,1,0:T(4,128)(2,1)} %all-to-all-done.moved_ref, bf16[1152,1152]{1,0:T(8,128)(2,1)S(1)} %bitcast.17, f32[1,1152]{1,0:T(1,128)S(1)} %reshape.21.gate_ref), custom_call_target="tpu_custom_call" | custom-call | flops 1500000000 | bytes 5000000 | tf_op jit(solution)/shard_map/pallas_call | solution.py:109
  106.6 62.8 %all_to_all.10.x_ref = bf16[128,8,4,128]{3,2,1,0:T(4,128)(2,1)S(1)} all-to-all(bf16[128,8,4,128]{3,2,1,0:T(4,128)(2,1)S(1)} %shard_map.95), channel_id=1, replica_groups=mesh['clip'=4,'zl'=8,'core'=2,'zh'=2,'y'=4] {'zl','core','zh','y'}, dimensions={0} | all-to-all | bytes 2097152 | tf_op jit(solution)/shard_map/all_to_all | solution.py:247
  169.5 2.7 %collective-permute-start.8 = (f32[5,128]{1,0:T(8,128)S(1)}, f32[5,128]{1,0:T(8,128)S(1)}, u32[]{:S(2)}, u32[]{:S(2)}) collective-permute-start(f32[5,128]{1,0:T(8,128)S(1)} %convert_reduce_fusion), channel_id=1, source_target_pairs={{0,8},{8,0},{1,9},{9,1},{2,10},{10,2},{3,11},{11,3},{4,12},{12,4},... | collective-permute-start | bytes 7688 | tf_op jit(solution)/shard_map/ppermute | solution.py:235
  172.3 2.3 %shard_map.96 = (bf16[1,128,1152]{2,1,0:T(8,128)(2,1)}, bf16[1,128,1152]{2,1,0:T(8,128)(2,1)}, bf16[1,128,1152]{2,1,0:T(8,128)(2,1)}) custom-call(bf16[128,8,4,128]{3,2,1,0:T(4,128)(2,1)} %copy-done), custom_call_target="tpu_custom_call" | custom-call | bytes 1800000 | tf_op jit(solution)/shard_map/pallas_call | solution.py:156
  174.6 0.6 maximum_bitcast_fusion
  (16 shorter events, 0.6 us)
Async XLA Ops:
  0.6 23.2 %collective-permute-start = (bf16[72,1152]{1,0:T(8,128)(2,1)}, bf16[72,1152]{1,0:T(8,128)(2,1)S(1)}, u32[]{:S(2)}, u32[]{:S(2)}) collective-permute-start(bf16[72,1152]{1,0:T(8,128)(2,1)} %param.11), channel_id=1, source_target_pairs={{84,0},{100,16},{116,32},{0,48},{16,64},{32,80},{48,96},{64,112},{... | collective-permute-start | bytes 497672 | tf_op jit(solution)/shard_map/ppermute | solution.py:220
  23.8 77.6 %all-to-all-start = ((bf16[128,9,4,128]{3,2,1,0:T(4,128)(2,1)}), bf16[128,9,4,128]{3,2,1,0:T(4,128)(2,1)}, u32[]{:S(2)}, u32[]{:S(2)}) async-start(bf16[128,9,4,128]{3,2,1,0:T(4,128)(2,1)} %shard_map.93), calls=%async_computation | async-start | bytes 2359296 | tf_op jit(solution)/shard_map/all_to_all | solution.py:245
  43.8 9.8 %collective-permute-start.3 = (bf16[40,1152]{1,0:T(8,128)(2,1)S(1)}, bf16[40,1152]{1,0:T(8,128)(2,1)S(1)}, u32[]{:S(2)}, u32[]{:S(2)}) collective-permute-start(bf16[40,1152]{1,0:T(8,128)(2,1)S(1)} %slice_select_fusion), channel_id=1, source_target_pairs={{0,3},{1,0},{2,1},{3,2},{4,7},{5,4},{6,5},{7,6},{8,11},{9,8},{10,9... | collective-permute-start | bytes 276488 | tf_op jit(solution)/shard_map/ppermute | solution.py:167
  47.9 9.7 %collective-permute-start.2 = (bf16[40,1152]{1,0:T(8,128)(2,1)S(1)}, bf16[40,1152]{1,0:T(8,128)(2,1)S(1)}, u32[]{:S(2)}, u32[]{:S(2)}) collective-permute-start(bf16[40,1152]{1,0:T(8,128)(2,1)S(1)} %slice_select_fusion), channel_id=1, source_target_pairs={{0,2},{1,3},{2,0},{3,1},{4,6},{5,7},{6,4},{7,5},{8,10},{9,11},{10,... | collective-permute-start | bytes 276488 | tf_op jit(solution)/shard_map/ppermute | solution.py:167
  50.7 8.7 %collective-permute-start.1 = (bf16[40,1152]{1,0:T(8,128)(2,1)S(1)}, bf16[40,1152]{1,0:T(8,128)(2,1)S(1)}, u32[]{:S(2)}, u32[]{:S(2)}) collective-permute-start(bf16[40,1152]{1,0:T(8,128)(2,1)S(1)} %slice_select_fusion), channel_id=1, source_target_pairs={{0,1},{1,2},{2,3},{3,0},{4,5},{5,6},{6,7},{7,4},{8,9},{9,10},{10,1... | collective-permute-start | bytes 276488 | tf_op jit(solution)/shard_map/ppermute | solution.py:167
  59.5 21.5 %collective-permute-start.6 = (bf16[4,40,1152]{2,1,0:T(8,128)(2,1)S(1)}, bf16[4,40,1152]{2,1,0:T(8,128)(2,1)S(1)}, u32[]{:S(2)}, u32[]{:S(2)}) collective-permute-start(bf16[4,40,1152]{2,1,0:T(8,128)(2,1)S(1)} %get-tuple-element.15), channel_id=1, source_target_pairs={{0,384},{128,0},{256,128},{384,256},{1,385},{129,1},{257,129},{385... | collective-permute-start | bytes 1105928 | tf_op jit(solution)/shard_map/ppermute | solution.py:167
  61.4 19.5 %collective-permute-start.5 = (bf16[4,40,1152]{2,1,0:T(8,128)(2,1)S(1)}, bf16[4,40,1152]{2,1,0:T(8,128)(2,1)S(1)}, u32[]{:S(2)}, u32[]{:S(2)}) collective-permute-start(bf16[4,40,1152]{2,1,0:T(8,128)(2,1)S(1)} %get-tuple-element.15), channel_id=1, source_target_pairs={{0,256},{128,384},{256,0},{384,128},{1,257},{129,385},{257,1},{385... | collective-permute-start | bytes 1105928 | tf_op jit(solution)/shard_map/ppermute | solution.py:167
  63.3 20.2 %collective-permute-start.4 = (bf16[4,40,1152]{2,1,0:T(8,128)(2,1)S(1)}, bf16[4,40,1152]{2,1,0:T(8,128)(2,1)S(1)}, u32[]{:S(2)}, u32[]{:S(2)}) collective-permute-start(bf16[4,40,1152]{2,1,0:T(8,128)(2,1)S(1)} %get-tuple-element.15), channel_id=1, source_target_pairs={{0,128},{128,256},{256,384},{384,0},{1,129},{129,257},{257,385},{3... | collective-permute-start | bytes 1105928 | tf_op jit(solution)/shard_map/ppermute | solution.py:167
  83.5 2.2 %copy-start.1 = (f32[1152]{0:T(1024)S(1)}, f32[1152]{0:T(1024)}, u32[]{:S(2)}) copy-start(f32[1152]{0:T(1024)} %param.10) | copy-start | bytes 13828
  83.7 5.2 %collective-permute-start.7 = (bf16[4,4,40,1152]{3,2,1,0:T(8,128)(2,1)S(1)}, bf16[4,4,40,1152]{3,2,1,0:T(8,128)(2,1)S(1)}, u32[]{:S(2)}, u32[]{:S(2)}) collective-permute-start(bf16[4,4,40,1152]{3,2,1,0:T(8,128)(2,1)S(1)} %pad_maximum_fusion.own_ref), channel_id=1, source_target_pairs={{0,8},{8,0},{1,9},{9,1},{2,10},{10,2},{3,11},{11,3},{4,12},{12,4},... | collective-permute-start | bytes 4423688 | tf_op jit(solution)/shard_map/ppermute | solution.py:225
  169.4 2.9 %copy-start = (bf16[128,8,4,128]{3,2,1,0:T(4,128)(2,1)}, bf16[128,8,4,128]{3,2,1,0:T(4,128)(2,1)S(1)}, u32[]{:S(2)}) copy-start(bf16[128,8,4,128]{3,2,1,0:T(4,128)(2,1)S(1)} %all_to_all.10.x_ref) | copy-start | bytes 3145732
  169.5 5.0 %collective-permute-start.8 = (f32[5,128]{1,0:T(8,128)S(1)}, f32[5,128]{1,0:T(8,128)S(1)}, u32[]{:S(2)}, u32[]{:S(2)}) collective-permute-start(f32[5,128]{1,0:T(8,128)S(1)} %convert_reduce_fusion), channel_id=1, source_target_pairs={{0,8},{8,0},{1,9},{9,1},{2,10},{10,2},{3,11},{11,3},{4,12},{12,4},... | collective-permute-start | bytes 7688 | tf_op jit(solution)/shard_map/ppermute | solution.py:235

commit v4 on v3

--- a/solution.py
+++ b/solution.py
@@ -168,14 +168,16 @@
 
 
 def fetch_pairs():
-    def spot(x, z, y):
-        return ((x * 8 + z % 8) * 2 + z // 8) * 4 + y
+    def spot(x, z, core, y):
+        return (((x * 8 + z % 8) * 2 + core) * 2 + z // 8) * 4 + y
 
     pairs = []
     for x in range(4):
         for y in range(4):
-            far = (4 * x + y) // 2 - 3
-            pairs += [(spot(x, (z + far) % 16, y), spot(x, z, y)) for z in range(16)]
+            near = (4 * x + y) // 2
+            for core, far in ((0, near - 3), (1, 4 - near)):
+                for z in range(16):
+                    pairs.append((spot(x, (z + far) % 16, core, y), spot(x, z, core, y)))
     return pairs
 
 
@@ -183,12 +185,13 @@
 
 
 def assemble_kernel(at_ref, own_ref, other_ref, out_ref):
-    x, y, z = [at_ref[n] for n in range(3)]
+    x, y, z, core = [at_ref[n] for n in range(4)]
     rows = out_ref.shape[2]
 
-    def copy(source, slot):
+    def copy(source, slot, mirrored):
         for n in range(8):
-            first = lax.rem(n - z + 11, 8) * 2
+            near = lax.rem(n - z + 11, 8)
+            first = 2 * jnp.where(mirrored, 7 - near, near)
             for half in range(2):
                 owner = first + half
                 s = lax.rem(x - lax.div(owner, 4) + 4, 4)
@@ -198,8 +201,8 @@
                 else:
                     out_ref[n, slot, PART:] = source[s, t, 2 * PART - rows :]
 
-    copy(own_ref, 0)
-    copy(other_ref, 1)
+    copy(own_ref, 0, core == 1)
+    copy(other_ref, 1, core == 0)
 
 
 def assemble(at, own, other, rows):
@@ -217,13 +220,13 @@
 def gather_weight(shard, later):
     rows = shard.shape[0]
     y = lax.axis_index("y")
-    held = lax.ppermute(shard, ("clip", "zl", "zh", "y"), fetch_pairs())
+    held = jnp.where(y % 2 == 0, shard[:PART], shard[rows - PART :])
+    held = lax.ppermute(held, AXES, fetch_pairs())
     held, later = lax.optimization_barrier((held, later))
-    held = jnp.where(y % 2 == 0, held[:PART], held[rows - PART :])
     held = jnp.stack([held] + [along(held, "y", s) for s in (1, 2, 3)])
     held = jnp.stack([held] + [along(held, "clip", s) for s in (1, 2, 3)])
     other = lax.ppermute(held, "core", [(0, 1), (1, 0)])
-    at = jnp.stack([lax.axis_index(n) for n in ("clip", "y", "zl")]).astype(jnp.int32)
+    at = jnp.stack([lax.axis_index(n) for n in ("clip", "y", "zl", "core")]).astype(jnp.int32)
     pairs = assemble(at, held, other, rows)
     even = lax.axis_index("core") == 0
     pairs = jnp.where(even, pairs, pairs[:, ::-1])

time: 176 us -> 167 us (0.949)
  waiting for transfers between devices: 43.7 us -> 36.8 us
  starting transfers between devices: 55.5 us -> 51.7 us
    ppermute x1, waiting for transfers between devices: 8.32 us -> 1.46 us  [gather_weight(): held = lax.ppermute(held, AXES, fetch_pairs())]
    all_to_all x1, starting transfers between devices: 19.9 us -> 16.1 us  [per_device(): lax.all_to_all(packed, GROUP, split_axis=0, concat_axis=0, tiled=True)]
where the time goes in v4:
time: 167 us; the launch traced here: 166 us
  blocking collectives  62.8 us (38%)
  starting transfers between devices  51.7 us (31%)
  waiting for transfers between devices  36.8 us (22%)
  Pallas kernels  10.9 us (7%)
  other arithmetic  2.54 us (2%)
    all_to_all x1, blocking collectives, per_device(): lax.all_to_all(grads, GROUP, split_axis=0, concat_axis=0, tiled=True)  62.8 us
    ppermute x6, waiting for transfers between devices, along(): return lax.ppermute(x, axis, [(i, (i + shift) % 4) for i in range(4)])  20.9 us
    ppermute x6, starting transfers between devices, along(): return lax.ppermute(x, axis, [(i, (i + shift) % 4) for i in range(4)])  18.7 us
    all_to_all x1, starting transfers between devices, per_device(): lax.all_to_all(packed, GROUP, split_axis=0, concat_axis=0, tiled=True)  16.1 us
    ppermute x1, starting transfers between devices, gather_weight(): held = lax.ppermute(held, AXES, fetch_pairs())  12.3 us
    all_to_all x1, waiting for transfers between devices, per_device(): lax.all_to_all(packed, GROUP, split_axis=0, concat_axis=0, tiled=True)  11.3 us
    pallas_call x1, Pallas kernels, attend(): pl.pallas_call(attend_kernel, out_shape=jax.ShapeDtypeStruct((frames, ROW...  5.14 us
  transfers between devices with their start and end apart: 10, of which 7 were waited for; matrix products, arithmetic and copies ran while one was open for 0% of the time, Pallas kernels for 3%

profile of v4, /device:TPU:6, one launch (start us, length us, event | category | flops | bytes accessed | tf_op | source)
XLA Modules:
  0.0 165.5 jit_solution(6823909051237834196)
XLA Ops:
  0.6 1.0 slice_select_fusion
  1.6 12.3 %collective-permute-start = (bf16[40,1152]{1,0:T(8,128)(2,1)S(1)}, bf16[40,1152]{1,0:T(8,128)(2,1)S(1)}, u32[]{:S(2)}, u32[]{:S(2)}) collective-permute-start(bf16[40,1152]{1,0:T(8,128)(2,1)S(1)} %slice_select_fusion), channel_id=1, source_target_pairs={{84,0},{100,16},{116,32},{0,48},{16,64},{32,80},{48,96},{64,112},{... | collective-permute-start | bytes 276488 | tf_op jit(solution)/shard_map/ppermute | solution.py:224
  13.9 2.6 %shard_map.93 = bf16[128,9,4,128]{3,2,1,0:T(4,128)(2,1)} custom-call(bf16[1,128,1152]{2,1,0:T(8,128)(2,1)} %refs_0_.1, bf16[1,128,1152]{2,1,0:T(8,128)(2,1)} %refs_1_.1, bf16[1,128,1152]{2,1,0:T(8,128)(2,1)} %refs_2_.1, bf16[1,128,1152]{2,1,0:T(8,128)(2,1)} %refs_3_.1), custom_call_target="tpu_custom_call" | custom-call | bytes 2400000 | tf_op jit(solution)/shard_map/pallas_call | solution.py:135
  16.5 1.5 collective-permute-done
  18.0 16.1 %all-to-all-start = ((bf16[128,9,4,128]{3,2,1,0:T(4,128)(2,1)}), bf16[128,9,4,128]{3,2,1,0:T(4,128)(2,1)}, u32[]{:S(2)}, u32[]{:S(2)}) async-start(bf16[128,9,4,128]{3,2,1,0:T(4,128)(2,1)} %shard_map.93), calls=%async_computation | async-start | bytes 2359296 | tf_op jit(solution)/shard_map/all_to_all | solution.py:248
  34.1 4.2 %collective-permute-start.3 = (bf16[40,1152]{1,0:T(8,128)(2,1)S(1)}, bf16[40,1152]{1,0:T(8,128)(2,1)S(1)}, u32[]{:S(2)}, u32[]{:S(2)}) collective-permute-start(bf16[40,1152]{1,0:T(8,128)(2,1)S(1)} %collective-permute-done), channel_id=1, source_target_pairs={{0,3},{1,0},{2,1},{3,2},{4,7},{5,4},{6,5},{7,6},{8,11},{9,8},{10,9... | collective-permute-start | bytes 276488 | tf_op jit(solution)/shard_map/ppermute | solution.py:167
  38.3 2.8 %collective-permute-start.2 = (bf16[40,1152]{1,0:T(8,128)(2,1)S(1)}, bf16[40,1152]{1,0:T(8,128)(2,1)S(1)}, u32[]{:S(2)}, u32[]{:S(2)}) collective-permute-start(bf16[40,1152]{1,0:T(8,128)(2,1)S(1)} %collective-permute-done), channel_id=1, source_target_pairs={{0,2},{1,3},{2,0},{3,1},{4,6},{5,7},{6,4},{7,5},{8,10},{9,11},{10,... | collective-permute-start | bytes 276488 | tf_op jit(solution)/shard_map/ppermute | solution.py:167
  41.0 2.8 %collective-permute-start.1 = (bf16[40,1152]{1,0:T(8,128)(2,1)S(1)}, bf16[40,1152]{1,0:T(8,128)(2,1)S(1)}, u32[]{:S(2)}, u32[]{:S(2)}) collective-permute-start(bf16[40,1152]{1,0:T(8,128)(2,1)S(1)} %collective-permute-done), channel_id=1, source_target_pairs={{0,1},{1,2},{2,3},{3,0},{4,5},{5,6},{6,7},{7,4},{8,9},{9,10},{10,1... | collective-permute-start | bytes 276488 | tf_op jit(solution)/shard_map/ppermute | solution.py:167
  43.8 4.1 %collective-permute-done.2 = bf16[40,1152]{1,0:T(8,128)(2,1)S(1)} collective-permute-done((bf16[40,1152]{1,0:T(8,128)(2,1)S(1)}, bf16[40,1152]{1,0:T(8,128)(2,1)S(1)}, u32[]{:S(2)}, u32[]{:S(2)}) %collective-permute-start.2) | collective-permute-done | bytes 92192 | tf_op jit(solution)/shard_map/ppermute | solution.py:167
  47.9 1.8 %collective-permute-done.1 = bf16[40,1152]{1,0:T(8,128)(2,1)S(1)} collective-permute-done((bf16[40,1152]{1,0:T(8,128)(2,1)S(1)}, bf16[40,1152]{1,0:T(8,128)(2,1)S(1)}, u32[]{:S(2)}, u32[]{:S(2)}) %collective-permute-start.1) | collective-permute-done | bytes 92192 | tf_op jit(solution)/shard_map/ppermute | solution.py:167
  49.8 1.9 %collective-permute-start.6 = (bf16[4,40,1152]{2,1,0:T(8,128)(2,1)S(1)}, bf16[4,40,1152]{2,1,0:T(8,128)(2,1)S(1)}, u32[]{:S(2)}, u32[]{:S(2)}) collective-permute-start(bf16[4,40,1152]{2,1,0:T(8,128)(2,1)S(1)} %get-tuple-element.15), channel_id=1, source_target_pairs={{0,384},{128,0},{256,128},{384,256},{1,385},{129,1},{257,129},{385... | collective-permute-start | bytes 1105928 | tf_op jit(solution)/shard_map/ppermute | solution.py:167
  51.7 1.9 %collective-permute-start.5 = (bf16[4,40,1152]{2,1,0:T(8,128)(2,1)S(1)}, bf16[4,40,1152]{2,1,0:T(8,128)(2,1)S(1)}, u32[]{:S(2)}, u32[]{:S(2)}) collective-permute-start(bf16[4,40,1152]{2,1,0:T(8,128)(2,1)S(1)} %get-tuple-element.15), channel_id=1, source_target_pairs={{0,256},{128,384},{256,0},{384,128},{1,257},{129,385},{257,1},{385... | collective-permute-start | bytes 1105928 | tf_op jit(solution)/shard_map/ppermute | solution.py:167
  53.7 5.1 %collective-permute-start.4 = (bf16[4,40,1152]{2,1,0:T(8,128)(2,1)S(1)}, bf16[4,40,1152]{2,1,0:T(8,128)(2,1)S(1)}, u32[]{:S(2)}, u32[]{:S(2)}) collective-permute-start(bf16[4,40,1152]{2,1,0:T(8,128)(2,1)S(1)} %get-tuple-element.15), channel_id=1, source_target_pairs={{0,128},{128,256},{256,384},{384,0},{1,129},{129,257},{257,385},{3... | collective-permute-start | bytes 1105928 | tf_op jit(solution)/shard_map/ppermute | solution.py:167
  58.8 12.5 %collective-permute-done.6 = bf16[4,40,1152]{2,1,0:T(8,128)(2,1)S(1)} collective-permute-done((bf16[4,40,1152]{2,1,0:T(8,128)(2,1)S(1)}, bf16[4,40,1152]{2,1,0:T(8,128)(2,1)S(1)}, u32[]{:S(2)}, u32[]{:S(2)}) %collective-permute-start.6) | collective-permute-done | bytes 368672 | tf_op jit(solution)/shard_map/ppermute | solution.py:167
  71.3 2.5 %collective-permute-done.4 = bf16[4,40,1152]{2,1,0:T(8,128)(2,1)S(1)} collective-permute-done((bf16[4,40,1152]{2,1,0:T(8,128)(2,1)S(1)}, bf16[4,40,1152]{2,1,0:T(8,128)(2,1)S(1)}, u32[]{:S(2)}, u32[]{:S(2)}) %collective-permute-start.4) | collective-permute-done | bytes 368672 | tf_op jit(solution)/shard_map/ppermute | solution.py:167
  74.0 1.9 %collective-permute-start.7 = (bf16[4,4,40,1152]{3,2,1,0:T(8,128)(2,1)S(1)}, bf16[4,4,40,1152]{3,2,1,0:T(8,128)(2,1)S(1)}, u32[]{:S(2)}, u32[]{:S(2)}) collective-permute-start(bf16[4,4,40,1152]{3,2,1,0:T(8,128)(2,1)S(1)} %pad_maximum_fusion.own_ref), channel_id=1, source_target_pairs={{0,8},{8,0},{1,9},{9,1},{2,10},{10,2},{3,11},{11,3},{4,12},{12,4},... | collective-permute-start | bytes 4423688 | tf_op jit(solution)/shard_map/ppermute | solution.py:228
  76.1 3.1 %collective-permute-done.7.other_ref = bf16[4,4,40,1152]{3,2,1,0:T(8,128)(2,1)S(1)} collective-permute-done((bf16[4,4,40,1152]{3,2,1,0:T(8,128)(2,1)S(1)}, bf16[4,4,40,1152]{3,2,1,0:T(8,128)(2,1)S(1)}, u32[]{:S(2)}, u32[]{:S(2)}) %collective-permute-start.7) | collective-permute-done | bytes 1474592 | tf_op jit(solution)/shard_map/ppermute | solution.py:228
  79.2 0.9 shard_map.94
  80.5 11.3 %all-to-all-done.moved_ref = bf16[128,9,4,128]{3,2,1,0:T(4,128)(2,1)} async-done(((bf16[128,9,4,128]{3,2,1,0:T(4,128)(2,1)}), bf16[128,9,4,128]{3,2,1,0:T(4,128)(2,1)}, u32[]{:S(2)}, u32[]{:S(2)}) %all-to-all-start) | async-done | bytes 1179680 | tf_op jit(solution)/shard_map/all_to_all | solution.py:248
  91.8 5.1 %shard_map.95 = bf16[128,8,4,128]{3,2,1,0:T(4,128)(2,1)S(1)} custom-call(bf16[128,9,4,128]{3,2,1,0:T(4,128)(2,1)} %all-to-all-done.moved_ref, bf16[1152,1152]{1,0:T(8,128)(2,1)S(1)} %bitcast.17, f32[1,1152]{1,0:T(1,128)S(1)} %reshape.21.gate_ref), custom_call_target="tpu_custom_call" | custom-call | flops 1500000000 | bytes 5000000 | tf_op jit(solution)/shard_map/pallas_call | solution.py:109
  97.0 62.8 %all_to_all.10.x_ref = bf16[128,8,4,128]{3,2,1,0:T(4,128)(2,1)S(1)} all-to-all(bf16[128,8,4,128]{3,2,1,0:T(4,128)(2,1)S(1)} %shard_map.95), channel_id=1, replica_groups=mesh['clip'=4,'zl'=8,'core'=2,'zh'=2,'y'=4] {'zl','core','zh','y'}, dimensions={0} | all-to-all | bytes 2097152 | tf_op jit(solution)/shard_map/all_to_all | solution.py:250
  159.9 2.7 %collective-permute-start.8 = (f32[5,128]{1,0:T(8,128)S(1)}, f32[5,128]{1,0:T(8,128)S(1)}, u32[]{:S(2)}, u32[]{:S(2)}) collective-permute-start(f32[5,128]{1,0:T(8,128)S(1)} %convert_reduce_fusion), channel_id=1, source_target_pairs={{0,8},{8,0},{1,9},{9,1},{2,10},{10,2},{3,11},{11,3},{4,12},{12,4},... | collective-permute-start | bytes 7688 | tf_op jit(solution)/shard_map/ppermute | solution.py:238
  162.6 2.3 %shard_map.96 = (bf16[1,128,1152]{2,1,0:T(8,128)(2,1)}, bf16[1,128,1152]{2,1,0:T(8,128)(2,1)}, bf16[1,128,1152]{2,1,0:T(8,128)(2,1)}) custom-call(bf16[128,8,4,128]{3,2,1,0:T(4,128)(2,1)} %copy-done), custom_call_target="tpu_custom_call" | custom-call | bytes 1800000 | tf_op jit(solution)/shard_map/pallas_call | solution.py:156
  164.9 0.6 maximum_bitcast_fusion
  (15 shorter events, 1.0 us)
Async XLA Ops:
  1.6 16.4 %collective-permute-start = (bf16[40,1152]{1,0:T(8,128)(2,1)S(1)}, bf16[40,1152]{1,0:T(8,128)(2,1)S(1)}, u32[]{:S(2)}, u32[]{:S(2)}) collective-permute-start(bf16[40,1152]{1,0:T(8,128)(2,1)S(1)} %slice_select_fusion), channel_id=1, source_target_pairs={{84,0},{100,16},{116,32},{0,48},{16,64},{32,80},{48,96},{64,112},{... | collective-permute-start | bytes 276488 | tf_op jit(solution)/shard_map/ppermute | solution.py:224
  18.0 73.8 %all-to-all-start = ((bf16[128,9,4,128]{3,2,1,0:T(4,128)(2,1)}), bf16[128,9,4,128]{3,2,1,0:T(4,128)(2,1)}, u32[]{:S(2)}, u32[]{:S(2)}) async-start(bf16[128,9,4,128]{3,2,1,0:T(4,128)(2,1)} %shard_map.93), calls=%async_computation | async-start | bytes 2359296 | tf_op jit(solution)/shard_map/all_to_all | solution.py:248
  34.1 9.7 %collective-permute-start.3 = (bf16[40,1152]{1,0:T(8,128)(2,1)S(1)}, bf16[40,1152]{1,0:T(8,128)(2,1)S(1)}, u32[]{:S(2)}, u32[]{:S(2)}) collective-permute-start(bf16[40,1152]{1,0:T(8,128)(2,1)S(1)} %collective-permute-done), channel_id=1, source_target_pairs={{0,3},{1,0},{2,1},{3,2},{4,7},{5,4},{6,5},{7,6},{8,11},{9,8},{10,9... | collective-permute-start | bytes 276488 | tf_op jit(solution)/shard_map/ppermute | solution.py:167
  38.3 9.7 %collective-permute-start.2 = (bf16[40,1152]{1,0:T(8,128)(2,1)S(1)}, bf16[40,1152]{1,0:T(8,128)(2,1)S(1)}, u32[]{:S(2)}, u32[]{:S(2)}) collective-permute-start(bf16[40,1152]{1,0:T(8,128)(2,1)S(1)} %collective-permute-done), channel_id=1, source_target_pairs={{0,2},{1,3},{2,0},{3,1},{4,6},{5,7},{6,4},{7,5},{8,10},{9,11},{10,... | collective-permute-start | bytes 276488 | tf_op jit(solution)/shard_map/ppermute | solution.py:167
  41.0 8.7 %collective-permute-start.1 = (bf16[40,1152]{1,0:T(8,128)(2,1)S(1)}, bf16[40,1152]{1,0:T(8,128)(2,1)S(1)}, u32[]{:S(2)}, u32[]{:S(2)}) collective-permute-start(bf16[40,1152]{1,0:T(8,128)(2,1)S(1)} %collective-permute-done), channel_id=1, source_target_pairs={{0,1},{1,2},{2,3},{3,0},{4,5},{5,6},{6,7},{7,4},{8,9},{9,10},{10,1... | collective-permute-start | bytes 276488 | tf_op jit(solution)/shard_map/ppermute | solution.py:167
  49.8 21.5 %collective-permute-start.6 = (bf16[4,40,1152]{2,1,0:T(8,128)(2,1)S(1)}, bf16[4,40,1152]{2,1,0:T(8,128)(2,1)S(1)}, u32[]{:S(2)}, u32[]{:S(2)}) collective-permute-start(bf16[4,40,1152]{2,1,0:T(8,128)(2,1)S(1)} %get-tuple-element.15), channel_id=1, source_target_pairs={{0,384},{128,0},{256,128},{384,256},{1,385},{129,1},{257,129},{385... | collective-permute-start | bytes 1105928 | tf_op jit(solution)/shard_map/ppermute | solution.py:167
  51.7 19.5 %collective-permute-start.5 = (bf16[4,40,1152]{2,1,0:T(8,128)(2,1)S(1)}, bf16[4,40,1152]{2,1,0:T(8,128)(2,1)S(1)}, u32[]{:S(2)}, u32[]{:S(2)}) collective-permute-start(bf16[4,40,1152]{2,1,0:T(8,128)(2,1)S(1)} %get-tuple-element.15), channel_id=1, source_target_pairs={{0,256},{128,384},{256,0},{384,128},{1,257},{129,385},{257,1},{385... | collective-permute-start | bytes 1105928 | tf_op jit(solution)/shard_map/ppermute | solution.py:167
  53.7 20.2 %collective-permute-start.4 = (bf16[4,40,1152]{2,1,0:T(8,128)(2,1)S(1)}, bf16[4,40,1152]{2,1,0:T(8,128)(2,1)S(1)}, u32[]{:S(2)}, u32[]{:S(2)}) collective-permute-start(bf16[4,40,1152]{2,1,0:T(8,128)(2,1)S(1)} %get-tuple-element.15), channel_id=1, source_target_pairs={{0,128},{128,256},{256,384},{384,0},{1,129},{129,257},{257,385},{3... | collective-permute-start | bytes 1105928 | tf_op jit(solution)/shard_map/ppermute | solution.py:167
  73.8 2.2 %copy-start.1 = (f32[1152]{0:T(1024)S(1)}, f32[1152]{0:T(1024)}, u32[]{:S(2)}) copy-start(f32[1152]{0:T(1024)} %param.10) | copy-start | bytes 13828
  74.0 5.2 %collective-permute-start.7 = (bf16[4,4,40,1152]{3,2,1,0:T(8,128)(2,1)S(1)}, bf16[4,4,40,1152]{3,2,1,0:T(8,128)(2,1)S(1)}, u32[]{:S(2)}, u32[]{:S(2)}) collective-permute-start(bf16[4,4,40,1152]{3,2,1,0:T(8,128)(2,1)S(1)} %pad_maximum_fusion.own_ref), channel_id=1, source_target_pairs={{0,8},{8,0},{1,9},{9,1},{2,10},{10,2},{3,11},{11,3},{4,12},{12,4},... | collective-permute-start | bytes 4423688 | tf_op jit(solution)/shard_map/ppermute | solution.py:228
  159.7 2.9 %copy-start = (bf16[128,8,4,128]{3,2,1,0:T(4,128)(2,1)}, bf16[128,8,4,128]{3,2,1,0:T(4,128)(2,1)S(1)}, u32[]{:S(2)}) copy-start(bf16[128,8,4,128]{3,2,1,0:T(4,128)(2,1)S(1)} %all_to_all.10.x_ref) | copy-start | bytes 3145732
  159.9 5.0 %collective-permute-start.8 = (f32[5,128]{1,0:T(8,128)S(1)}, f32[5,128]{1,0:T(8,128)S(1)}, u32[]{:S(2)}, u32[]{:S(2)}) collective-permute-start(f32[5,128]{1,0:T(8,128)S(1)} %convert_reduce_fusion), channel_id=1, source_target_pairs={{0,8},{8,0},{1,9},{9,1},{2,10},{10,2},{3,11},{11,3},{4,12},{12,4},... | collective-permute-start | bytes 7688 | tf_op jit(solution)/shard_map/ppermute | solution.py:238

commit v5 on v4

--- a/solution.py
+++ b/solution.py
@@ -184,6 +184,13 @@
 PART = 40
 
 
+def same(x, passes):
+    for n in range(passes):
+        one = jnp.where(lax.axis_index("clip") >= -n, 1.0, 2.0).astype(x.dtype)
+        x = lax.optimization_barrier(x * one)
+    return x
+
+
 def assemble_kernel(at_ref, own_ref, other_ref, out_ref):
     x, y, z, core = [at_ref[n] for n in range(4)]
     rows = out_ref.shape[2]
@@ -222,15 +229,16 @@
     y = lax.axis_index("y")
     held = jnp.where(y % 2 == 0, shard[:PART], shard[rows - PART :])
     held = lax.ppermute(held, AXES, fetch_pairs())
-    held, later = lax.optimization_barrier((held, later))
+    held, _ = lax.optimization_barrier((held, later))
+    held = same(held, 2)
     held = jnp.stack([held] + [along(held, "y", s) for s in (1, 2, 3)])
     held = jnp.stack([held] + [along(held, "clip", s) for s in (1, 2, 3)])
     other = lax.ppermute(held, "core", [(0, 1), (1, 0)])
     at = jnp.stack([lax.axis_index(n) for n in ("clip", "y", "zl", "core")]).astype(jnp.int32)
     pairs = assemble(at, held, other, rows)
     even = lax.axis_index("core") == 0
-    pairs = jnp.where(even, pairs, pairs[:, ::-1])
-    return pairs.reshape(WIDTH, WIDTH), later
+    pairs = same(jnp.where(even, pairs, pairs[:, ::-1]), 2)
+    return pairs.reshape(WIDTH, WIDTH)
 
 
 def sum_of_terms(pieces):
@@ -244,7 +252,7 @@
 
 def per_device(query_states, key_states, value_states, grad_output, branch_gate, out_weight):
     packed = pack((query_states, key_states, value_states, grad_output))
-    weight, packed = gather_weight(out_weight, packed)
+    weight = gather_weight(out_weight, packed)
     moved = lax.all_to_all(packed, GROUP, split_axis=0, concat_axis=0, tiled=True)
     grads = attend(moved, weight, branch_gate.reshape(1, WIDTH))
     returned = lax.all_to_all(grads, GROUP, split_axis=0, concat_axis=0, tiled=True)

time: 167 us -> 161 us (0.964)
  starting transfers between devices: 51.7 us -> 48.1 us
  waiting for transfers between devices: 36.8 us -> 33.4 us
    ppermute x6, waiting for transfers between devices: 20.9 us -> 15.3 us  [along(): return lax.ppermute(x, axis, [(i, (i + shift) % 4) for i in range(4)])]
    all_to_all x1, starting transfers between devices: 16.1 us -> 11.1 us  [per_device(): lax.all_to_all(packed, GROUP, split_axis=0, concat_axis=0, tiled=True)]
    all_to_all x1, waiting for transfers between devices: 11.3 us -> 15.1 us  [per_device(): lax.all_to_all(packed, GROUP, split_axis=0, concat_axis=0, tiled=True)]
  transfers between devices with their start and end apart: 10 -> 10, of which waited for: 7 -> 6; matrix products, arithmetic and copies ran while one was open for 0% -> 1% of each run, Pallas kernels for 3% -> 4%
where the time goes in v5:
time: 161 us; the launch traced here: 159 us
  blocking collectives  62.8 us (39%)
  starting transfers between devices  48.1 us (30%)
  waiting for transfers between devices  33.4 us (21%)
  Pallas kernels  10.9 us (7%)
  other arithmetic  3.03 us (2%)
    all_to_all x1, blocking collectives, per_device(): lax.all_to_all(grads, GROUP, split_axis=0, concat_axis=0, tiled=True)  62.8 us
    ppermute x6, starting transfers between devices, along(): return lax.ppermute(x, axis, [(i, (i + shift) % 4) for i in range(4)])  19.9 us
    ppermute x6, waiting for transfers between devices, along(): return lax.ppermute(x, axis, [(i, (i + shift) % 4) for i in range(4)])  15.3 us
    all_to_all x1, waiting for transfers between devices, per_device(): lax.all_to_all(packed, GROUP, split_axis=0, concat_axis=0, tiled=True)  15.1 us
    ppermute x1, starting transfers between devices, gather_weight(): held = lax.ppermute(held, AXES, fetch_pairs())  12.3 us
    all_to_all x1, starting transfers between devices, per_device(): lax.all_to_all(packed, GROUP, split_axis=0, concat_axis=0, tiled=True)  11.1 us
    pallas_call x1, Pallas kernels, attend(): pl.pallas_call(attend_kernel, out_shape=jax.ShapeDtypeStruct((frames, ROW...  5.14 us
  transfers between devices with their start and end apart: 10, of which 6 were waited for; matrix products, arithmetic and copies ran while one was open for 1% of the time, Pallas kernels for 4%

profile of v5, /device:TPU:6, one launch (start us, length us, event | category | flops | bytes accessed | tf_op | source)
XLA Modules:
  0.0 159.1 jit_solution(18213402484588256149)
XLA Ops:
  0.6 1.0 slice_select_fusion
  1.6 12.3 %collective-permute-start = (bf16[40,1152]{1,0:T(8,128)(2,1)S(1)}, bf16[40,1152]{1,0:T(8,128)(2,1)S(1)}, u32[]{:S(2)}, u32[]{:S(2)}) collective-permute-start(bf16[40,1152]{1,0:T(8,128)(2,1)S(1)} %slice_select_fusion), channel_id=1, source_target_pairs={{84,0},{100,16},{116,32},{0,48},{16,64},{32,80},{48,96},{64,112},{... | collective-permute-start | bytes 276488 | tf_op jit(solution)/shard_map/ppermute | solution.py:231
  13.9 2.6 %shard_map.93 = bf16[128,9,4,128]{3,2,1,0:T(4,128)(2,1)} custom-call(bf16[1,128,1152]{2,1,0:T(8,128)(2,1)} %refs_0_.1, bf16[1,128,1152]{2,1,0:T(8,128)(2,1)} %refs_1_.1, bf16[1,128,1152]{2,1,0:T(8,128)(2,1)} %refs_2_.1, bf16[1,128,1152]{2,1,0:T(8,128)(2,1)} %refs_3_.1), custom_call_target="tpu_custom_call" | custom-call | bytes 2400000 | tf_op jit(solution)/shard_map/pallas_call | solution.py:135
  16.5 11.1 %all-to-all-start = ((bf16[128,9,4,128]{3,2,1,0:T(4,128)(2,1)}), bf16[128,9,4,128]{3,2,1,0:T(4,128)(2,1)}, u32[]{:S(2)}, u32[]{:S(2)}) async-start(bf16[128,9,4,128]{3,2,1,0:T(4,128)(2,1)} %shard_map.93), calls=%async_computation | async-start | bytes 2359296 | tf_op jit(solution)/shard_map/all_to_all | solution.py:256
  27.7 3.0 %collective-permute-start.1 = (bf16[40,1152]{1,0:T(8,128)(2,1)S(1)}, bf16[40,1152]{1,0:T(8,128)(2,1)S(1)}, u32[]{:S(2)}, u32[]{:S(2)}) collective-permute-start(bf16[40,1152]{1,0:T(8,128)(2,1)S(1)} %broadcast_multiply_fusion.1), channel_id=1, source_target_pairs={{0,1},{1,2},{2,3},{3,0},{4,5},{5,6},{6,7},{7,4},{8,9},{9,10},{10,1... | collective-permute-start | bytes 276488 | tf_op jit(solution)/shard_map/ppermute | solution.py:167
  30.7 4.6 %collective-permute-start.2 = (bf16[40,1152]{1,0:T(8,128)(2,1)S(1)}, bf16[40,1152]{1,0:T(8,128)(2,1)S(1)}, u32[]{:S(2)}, u32[]{:S(2)}) collective-permute-start(bf16[40,1152]{1,0:T(8,128)(2,1)S(1)} %broadcast_multiply_fusion.1), channel_id=1, source_target_pairs={{0,2},{1,3},{2,0},{3,1},{4,6},{5,7},{6,4},{7,5},{8,10},{9,11},{10,... | collective-permute-start | bytes 276488 | tf_op jit(solution)/shard_map/ppermute | solution.py:167
  35.3 3.4 %collective-permute-start.3 = (bf16[40,1152]{1,0:T(8,128)(2,1)S(1)}, bf16[40,1152]{1,0:T(8,128)(2,1)S(1)}, u32[]{:S(2)}, u32[]{:S(2)}) collective-permute-start(bf16[40,1152]{1,0:T(8,128)(2,1)S(1)} %broadcast_multiply_fusion.1), channel_id=1, source_target_pairs={{0,3},{1,0},{2,1},{3,2},{4,7},{5,4},{6,5},{7,6},{8,11},{9,8},{10,9... | collective-permute-start | bytes 276488 | tf_op jit(solution)/shard_map/ppermute | solution.py:167
  38.7 0.8 collective-permute-done.2
  39.5 2.8 %collective-permute-done.3 = bf16[40,1152]{1,0:T(8,128)(2,1)S(1)} collective-permute-done((bf16[40,1152]{1,0:T(8,128)(2,1)S(1)}, bf16[40,1152]{1,0:T(8,128)(2,1)S(1)}, u32[]{:S(2)}, u32[]{:S(2)}) %collective-permute-start.3) | collective-permute-done | bytes 92192 | tf_op jit(solution)/shard_map/ppermute | solution.py:167
  42.3 1.9 %collective-permute-start.5 = (bf16[4,40,1152]{2,1,0:T(8,128)(2,1)S(1)}, bf16[4,40,1152]{2,1,0:T(8,128)(2,1)S(1)}, u32[]{:S(2)}, u32[]{:S(2)}) collective-permute-start(bf16[4,40,1152]{2,1,0:T(8,128)(2,1)S(1)} %get-tuple-element.13), channel_id=1, source_target_pairs={{0,256},{128,384},{256,0},{384,128},{1,257},{129,385},{257,1},{385... | collective-permute-start | bytes 1105928 | tf_op jit(solution)/shard_map/ppermute | solution.py:167
  44.3 3.6 %collective-permute-start.6 = (bf16[4,40,1152]{2,1,0:T(8,128)(2,1)S(1)}, bf16[4,40,1152]{2,1,0:T(8,128)(2,1)S(1)}, u32[]{:S(2)}, u32[]{:S(2)}) collective-permute-start(bf16[4,40,1152]{2,1,0:T(8,128)(2,1)S(1)} %get-tuple-element.13), channel_id=1, source_target_pairs={{0,384},{128,0},{256,128},{384,256},{1,385},{129,1},{257,129},{385... | collective-permute-start | bytes 1105928 | tf_op jit(solution)/shard_map/ppermute | solution.py:167
  47.9 3.5 %collective-permute-start.4 = (bf16[4,40,1152]{2,1,0:T(8,128)(2,1)S(1)}, bf16[4,40,1152]{2,1,0:T(8,128)(2,1)S(1)}, u32[]{:S(2)}, u32[]{:S(2)}) collective-permute-start(bf16[4,40,1152]{2,1,0:T(8,128)(2,1)S(1)} %get-tuple-element.13), channel_id=1, source_target_pairs={{0,128},{128,256},{256,384},{384,0},{1,129},{129,257},{257,385},{3... | collective-permute-start | bytes 1105928 | tf_op jit(solution)/shard_map/ppermute | solution.py:167
  51.4 5.9 %collective-permute-done.5 = bf16[4,40,1152]{2,1,0:T(8,128)(2,1)S(1)} collective-permute-done((bf16[4,40,1152]{2,1,0:T(8,128)(2,1)S(1)}, bf16[4,40,1152]{2,1,0:T(8,128)(2,1)S(1)}, u32[]{:S(2)}, u32[]{:S(2)}) %collective-permute-start.5) | collective-permute-done | bytes 368672 | tf_op jit(solution)/shard_map/ppermute | solution.py:167
  57.3 5.8 %collective-permute-done.6 = bf16[4,40,1152]{2,1,0:T(8,128)(2,1)S(1)} collective-permute-done((bf16[4,40,1152]{2,1,0:T(8,128)(2,1)S(1)}, bf16[4,40,1152]{2,1,0:T(8,128)(2,1)S(1)}, u32[]{:S(2)}, u32[]{:S(2)}) %collective-permute-start.6) | collective-permute-done | bytes 368672 | tf_op jit(solution)/shard_map/ppermute | solution.py:167
  63.3 2.0 %collective-permute-start.7 = (bf16[4,4,40,1152]{3,2,1,0:T(8,128)(2,1)S(1)}, bf16[4,4,40,1152]{3,2,1,0:T(8,128)(2,1)S(1)}, u32[]{:S(2)}, u32[]{:S(2)}) collective-permute-start(bf16[4,4,40,1152]{3,2,1,0:T(8,128)(2,1)S(1)} %pad_maximum_fusion.own_ref), channel_id=1, source_target_pairs={{0,8},{8,0},{1,9},{9,1},{2,10},{10,2},{3,11},{11,3},{4,12},{12,4},... | collective-permute-start | bytes 4423688 | tf_op jit(solution)/shard_map/ppermute | solution.py:236
  65.5 3.0 %collective-permute-done.7.other_ref = bf16[4,4,40,1152]{3,2,1,0:T(8,128)(2,1)S(1)} collective-permute-done((bf16[4,4,40,1152]{3,2,1,0:T(8,128)(2,1)S(1)}, bf16[4,4,40,1152]{3,2,1,0:T(8,128)(2,1)S(1)}, u32[]{:S(2)}, u32[]{:S(2)}) %collective-permute-start.7) | collective-permute-done | bytes 1474592 | tf_op jit(solution)/shard_map/ppermute | solution.py:236
  68.5 0.9 shard_map.94
  69.4 0.7 fusion
  70.3 15.1 %all-to-all-done.moved_ref = bf16[128,9,4,128]{3,2,1,0:T(4,128)(2,1)} async-done(((bf16[128,9,4,128]{3,2,1,0:T(4,128)(2,1)}), bf16[128,9,4,128]{3,2,1,0:T(4,128)(2,1)}, u32[]{:S(2)}, u32[]{:S(2)}) %all-to-all-start) | async-done | bytes 1179680 | tf_op jit(solution)/shard_map/all_to_all | solution.py:256
  85.4 5.1 %shard_map.95 = bf16[128,8,4,128]{3,2,1,0:T(4,128)(2,1)S(1)} custom-call(bf16[128,9,4,128]{3,2,1,0:T(4,128)(2,1)} %all-to-all-done.moved_ref, bf16[1152,1152]{1,0:T(8,128)(2,1)S(1)} %bitcast.17, f32[1,1152]{1,0:T(1,128)S(1)} %reshape.21.gate_ref), custom_call_target="tpu_custom_call" | custom-call | flops 1500000000 | bytes 5000000 | tf_op jit(solution)/shard_map/pallas_call | solution.py:109
  90.6 62.8 %all_to_all.10.x_ref = bf16[128,8,4,128]{3,2,1,0:T(4,128)(2,1)S(1)} all-to-all(bf16[128,8,4,128]{3,2,1,0:T(4,128)(2,1)S(1)} %shard_map.95), channel_id=1, replica_groups=mesh['clip'=4,'zl'=8,'core'=2,'zh'=2,'y'=4] {'zl','core','zh','y'}, dimensions={0} | all-to-all | bytes 2097152 | tf_op jit(solution)/shard_map/all_to_all | solution.py:258
  153.4 2.7 %collective-permute-start.8 = (f32[5,128]{1,0:T(8,128)S(1)}, f32[5,128]{1,0:T(8,128)S(1)}, u32[]{:S(2)}, u32[]{:S(2)}) collective-permute-start(f32[5,128]{1,0:T(8,128)S(1)} %convert_reduce_fusion), channel_id=1, source_target_pairs={{0,8},{8,0},{1,9},{9,1},{2,10},{10,2},{3,11},{11,3},{4,12},{12,4},... | collective-permute-start | bytes 7688 | tf_op jit(solution)/shard_map/ppermute | solution.py:246
  156.2 2.3 %shard_map.96 = (bf16[1,128,1152]{2,1,0:T(8,128)(2,1)}, bf16[1,128,1152]{2,1,0:T(8,128)(2,1)}, bf16[1,128,1152]{2,1,0:T(8,128)(2,1)}) custom-call(bf16[128,8,4,128]{3,2,1,0:T(4,128)(2,1)} %copy-done), custom_call_target="tpu_custom_call" | custom-call | bytes 1800000 | tf_op jit(solution)/shard_map/pallas_call | solution.py:156
  158.5 0.6 maximum_bitcast_fusion
  (18 shorter events, 0.8 us)
Async XLA Ops:
  1.6 26.0 %collective-permute-start = (bf16[40,1152]{1,0:T(8,128)(2,1)S(1)}, bf16[40,1152]{1,0:T(8,128)(2,1)S(1)}, u32[]{:S(2)}, u32[]{:S(2)}) collective-permute-start(bf16[40,1152]{1,0:T(8,128)(2,1)S(1)} %slice_select_fusion), channel_id=1, source_target_pairs={{84,0},{100,16},{116,32},{0,48},{16,64},{32,80},{48,96},{64,112},{... | collective-permute-start | bytes 276488 | tf_op jit(solution)/shard_map/ppermute | solution.py:231
  16.5 68.9 %all-to-all-start = ((bf16[128,9,4,128]{3,2,1,0:T(4,128)(2,1)}), bf16[128,9,4,128]{3,2,1,0:T(4,128)(2,1)}, u32[]{:S(2)}, u32[]{:S(2)}) async-start(bf16[128,9,4,128]{3,2,1,0:T(4,128)(2,1)} %shard_map.93), calls=%async_computation | async-start | bytes 2359296 | tf_op jit(solution)/shard_map/all_to_all | solution.py:256
  27.6 37.7 %copy-start.1 = (f32[1152]{0:T(1024)S(1)}, f32[1152]{0:T(1024)}, u32[]{:S(2)}) copy-start(f32[1152]{0:T(1024)} %param.10) | copy-start | bytes 13828
  27.7 11.0 %collective-permute-start.1 = (bf16[40,1152]{1,0:T(8,128)(2,1)S(1)}, bf16[40,1152]{1,0:T(8,128)(2,1)S(1)}, u32[]{:S(2)}, u32[]{:S(2)}) collective-permute-start(bf16[40,1152]{1,0:T(8,128)(2,1)S(1)} %broadcast_multiply_fusion.1), channel_id=1, source_target_pairs={{0,1},{1,2},{2,3},{3,0},{4,5},{5,6},{6,7},{7,4},{8,9},{9,10},{10,1... | collective-permute-start | bytes 276488 | tf_op jit(solution)/shard_map/ppermute | solution.py:167
  30.7 8.8 %collective-permute-start.2 = (bf16[40,1152]{1,0:T(8,128)(2,1)S(1)}, bf16[40,1152]{1,0:T(8,128)(2,1)S(1)}, u32[]{:S(2)}, u32[]{:S(2)}) collective-permute-start(bf16[40,1152]{1,0:T(8,128)(2,1)S(1)} %broadcast_multiply_fusion.1), channel_id=1, source_target_pairs={{0,2},{1,3},{2,0},{3,1},{4,6},{5,7},{6,4},{7,5},{8,10},{9,11},{10,... | collective-permute-start | bytes 276488 | tf_op jit(solution)/shard_map/ppermute | solution.py:167
  35.3 7.0 %collective-permute-start.3 = (bf16[40,1152]{1,0:T(8,128)(2,1)S(1)}, bf16[40,1152]{1,0:T(8,128)(2,1)S(1)}, u32[]{:S(2)}, u32[]{:S(2)}) collective-permute-start(bf16[40,1152]{1,0:T(8,128)(2,1)S(1)} %broadcast_multiply_fusion.1), channel_id=1, source_target_pairs={{0,3},{1,0},{2,1},{3,2},{4,7},{5,4},{6,5},{7,6},{8,11},{9,8},{10,9... | collective-permute-start | bytes 276488 | tf_op jit(solution)/shard_map/ppermute | solution.py:167
  42.3 15.0 %collective-permute-start.5 = (bf16[4,40,1152]{2,1,0:T(8,128)(2,1)S(1)}, bf16[4,40,1152]{2,1,0:T(8,128)(2,1)S(1)}, u32[]{:S(2)}, u32[]{:S(2)}) collective-permute-start(bf16[4,40,1152]{2,1,0:T(8,128)(2,1)S(1)} %get-tuple-element.13), channel_id=1, source_target_pairs={{0,256},{128,384},{256,0},{384,128},{1,257},{129,385},{257,1},{385... | collective-permute-start | bytes 1105928 | tf_op jit(solution)/shard_map/ppermute | solution.py:167
  44.3 18.8 %collective-permute-start.6 = (bf16[4,40,1152]{2,1,0:T(8,128)(2,1)S(1)}, bf16[4,40,1152]{2,1,0:T(8,128)(2,1)S(1)}, u32[]{:S(2)}, u32[]{:S(2)}) collective-permute-start(bf16[4,40,1152]{2,1,0:T(8,128)(2,1)S(1)} %get-tuple-element.13), channel_id=1, source_target_pairs={{0,384},{128,0},{256,128},{384,256},{1,385},{129,1},{257,129},{385... | collective-permute-start | bytes 1105928 | tf_op jit(solution)/shard_map/ppermute | solution.py:167
  47.9 15.2 %collective-permute-start.4 = (bf16[4,40,1152]{2,1,0:T(8,128)(2,1)S(1)}, bf16[4,40,1152]{2,1,0:T(8,128)(2,1)S(1)}, u32[]{:S(2)}, u32[]{:S(2)}) collective-permute-start(bf16[4,40,1152]{2,1,0:T(8,128)(2,1)S(1)} %get-tuple-element.13), channel_id=1, source_target_pairs={{0,128},{128,256},{256,384},{384,0},{1,129},{129,257},{257,385},{3... | collective-permute-start | bytes 1105928 | tf_op jit(solution)/shard_map/ppermute | solution.py:167
  63.3 5.2 %collective-permute-start.7 = (bf16[4,4,40,1152]{3,2,1,0:T(8,128)(2,1)S(1)}, bf16[4,4,40,1152]{3,2,1,0:T(8,128)(2,1)S(1)}, u32[]{:S(2)}, u32[]{:S(2)}) collective-permute-start(bf16[4,4,40,1152]{3,2,1,0:T(8,128)(2,1)S(1)} %pad_maximum_fusion.own_ref), channel_id=1, source_target_pairs={{0,8},{8,0},{1,9},{9,1},{2,10},{10,2},{3,11},{11,3},{4,12},{12,4},... | collective-permute-start | bytes 4423688 | tf_op jit(solution)/shard_map/ppermute | solution.py:236
  153.3 2.9 %copy-start = (bf16[128,8,4,128]{3,2,1,0:T(4,128)(2,1)}, bf16[128,8,4,128]{3,2,1,0:T(4,128)(2,1)S(1)}, u32[]{:S(2)}) copy-start(bf16[128,8,4,128]{3,2,1,0:T(4,128)(2,1)S(1)} %all_to_all.10.x_ref) | copy-start | bytes 3145732
  153.4 5.0 %collective-permute-start.8 = (f32[5,128]{1,0:T(8,128)S(1)}, f32[5,128]{1,0:T(8,128)S(1)}, u32[]{:S(2)}, u32[]{:S(2)}) collective-permute-start(f32[5,128]{1,0:T(8,128)S(1)} %convert_reduce_fusion), channel_id=1, source_target_pairs={{0,8},{8,0},{1,9},{9,1},{2,10},{10,2},{3,11},{11,3},{4,12},{12,4},... | collective-permute-start | bytes 7688 | tf_op jit(solution)/shard_map/ppermute | solution.py:246

commit v6 on v5

--- a/solution.py
+++ b/solution.py
@@ -227,9 +227,9 @@
 def gather_weight(shard, later):
     rows = shard.shape[0]
     y = lax.axis_index("y")
-    held = jnp.where(y % 2 == 0, shard[:PART], shard[rows - PART :])
-    held = lax.ppermute(held, AXES, fetch_pairs())
+    held = lax.ppermute(shard, AXES, fetch_pairs())
     held, _ = lax.optimization_barrier((held, later))
+    held = jnp.where(y % 2 == 0, held[:PART], held[rows - PART :])
     held = same(held, 2)
     held = jnp.stack([held] + [along(held, "y", s) for s in (1, 2, 3)])
     held = jnp.stack([held] + [along(held, "clip", s) for s in (1, 2, 3)])

time: 161 us -> 160 us (level)
  no operation moved by 1% of the time
where the time goes in v6:
time: 160 us; the launch traced here: 158 us
  blocking collectives  62.8 us (39%)
  starting transfers between devices  48.1 us (30%)
  waiting for transfers between devices  33.4 us (21%)
  Pallas kernels  10.9 us (7%)
  other arithmetic  2.06 us (1%)
    all_to_all x1, blocking collectives, per_device(): lax.all_to_all(grads, GROUP, split_axis=0, concat_axis=0, tiled=True)  62.8 us
    ppermute x6, starting transfers between devices, along(): return lax.ppermute(x, axis, [(i, (i + shift) % 4) for i in range(4)])  19.9 us
    ppermute x6, waiting for transfers between devices, along(): return lax.ppermute(x, axis, [(i, (i + shift) % 4) for i in range(4)])  15.3 us
    all_to_all x1, waiting for transfers between devices, per_device(): lax.all_to_all(packed, GROUP, split_axis=0, concat_axis=0, tiled=True)  15.1 us
    ppermute x1, starting transfers between devices, gather_weight(): held = lax.ppermute(shard, AXES, fetch_pairs())  12.3 us
    all_to_all x1, starting transfers between devices, per_device(): lax.all_to_all(packed, GROUP, split_axis=0, concat_axis=0, tiled=True)  11.1 us
    pallas_call x1, Pallas kernels, attend(): pl.pallas_call(attend_kernel, out_shape=jax.ShapeDtypeStruct((frames, ROW...  5.14 us
  transfers between devices with their start and end apart: 10, of which 6 were waited for; matrix products, arithmetic and copies ran while one was open for 1% of the time, Pallas kernels for 4%

profile of v6, /device:TPU:6, one launch (start us, length us, event | category | flops | bytes accessed | tf_op | source)
XLA Modules:
  0.0 158.1 jit_solution(2833811168455914387)
XLA Ops:
  0.6 12.3 %collective-permute-start = (bf16[72,1152]{1,0:T(8,128)(2,1)}, bf16[72,1152]{1,0:T(8,128)(2,1)S(1)}, u32[]{:S(2)}, u32[]{:S(2)}) collective-permute-start(bf16[72,1152]{1,0:T(8,128)(2,1)} %param.11), channel_id=1, source_target_pairs={{84,0},{100,16},{116,32},{0,48},{16,64},{32,80},{48,96},{64,112},{... | collective-permute-start | bytes 497672 | tf_op jit(solution)/shard_map/ppermute | solution.py:230
  12.9 2.6 %shard_map.93 = bf16[128,9,4,128]{3,2,1,0:T(4,128)(2,1)} custom-call(bf16[1,128,1152]{2,1,0:T(8,128)(2,1)} %refs_0_.1, bf16[1,128,1152]{2,1,0:T(8,128)(2,1)} %refs_1_.1, bf16[1,128,1152]{2,1,0:T(8,128)(2,1)} %refs_2_.1, bf16[1,128,1152]{2,1,0:T(8,128)(2,1)} %refs_3_.1), custom_call_target="tpu_custom_call" | custom-call | bytes 2400000 | tf_op jit(solution)/shard_map/pallas_call | solution.py:135
  15.5 11.1 %all-to-all-start = ((bf16[128,9,4,128]{3,2,1,0:T(4,128)(2,1)}), bf16[128,9,4,128]{3,2,1,0:T(4,128)(2,1)}, u32[]{:S(2)}, u32[]{:S(2)}) async-start(bf16[128,9,4,128]{3,2,1,0:T(4,128)(2,1)} %shard_map.93), calls=%async_computation | async-start | bytes 2359296 | tf_op jit(solution)/shard_map/all_to_all | solution.py:256
  26.7 3.0 %collective-permute-start.1 = (bf16[40,1152]{1,0:T(8,128)(2,1)S(1)}, bf16[40,1152]{1,0:T(8,128)(2,1)S(1)}, u32[]{:S(2)}, u32[]{:S(2)}) collective-permute-start(bf16[40,1152]{1,0:T(8,128)(2,1)S(1)} %broadcast_multiply_fusion.1), channel_id=1, source_target_pairs={{0,1},{1,2},{2,3},{3,0},{4,5},{5,6},{6,7},{7,4},{8,9},{9,10},{10,1... | collective-permute-start | bytes 276488 | tf_op jit(solution)/shard_map/ppermute | solution.py:167
  29.7 4.6 %collective-permute-start.2 = (bf16[40,1152]{1,0:T(8,128)(2,1)S(1)}, bf16[40,1152]{1,0:T(8,128)(2,1)S(1)}, u32[]{:S(2)}, u32[]{:S(2)}) collective-permute-start(bf16[40,1152]{1,0:T(8,128)(2,1)S(1)} %broadcast_multiply_fusion.1), channel_id=1, source_target_pairs={{0,2},{1,3},{2,0},{3,1},{4,6},{5,7},{6,4},{7,5},{8,10},{9,11},{10,... | collective-permute-start | bytes 276488 | tf_op jit(solution)/shard_map/ppermute | solution.py:167
  34.3 3.4 %collective-permute-start.3 = (bf16[40,1152]{1,0:T(8,128)(2,1)S(1)}, bf16[40,1152]{1,0:T(8,128)(2,1)S(1)}, u32[]{:S(2)}, u32[]{:S(2)}) collective-permute-start(bf16[40,1152]{1,0:T(8,128)(2,1)S(1)} %broadcast_multiply_fusion.1), channel_id=1, source_target_pairs={{0,3},{1,0},{2,1},{3,2},{4,7},{5,4},{6,5},{7,6},{8,11},{9,8},{10,9... | collective-permute-start | bytes 276488 | tf_op jit(solution)/shard_map/ppermute | solution.py:167
  37.7 0.8 collective-permute-done.2
  38.5 2.8 %collective-permute-done.3 = bf16[40,1152]{1,0:T(8,128)(2,1)S(1)} collective-permute-done((bf16[40,1152]{1,0:T(8,128)(2,1)S(1)}, bf16[40,1152]{1,0:T(8,128)(2,1)S(1)}, u32[]{:S(2)}, u32[]{:S(2)}) %collective-permute-start.3) | collective-permute-done | bytes 92192 | tf_op jit(solution)/shard_map/ppermute | solution.py:167
  41.4 1.9 %collective-permute-start.5 = (bf16[4,40,1152]{2,1,0:T(8,128)(2,1)S(1)}, bf16[4,40,1152]{2,1,0:T(8,128)(2,1)S(1)}, u32[]{:S(2)}, u32[]{:S(2)}) collective-permute-start(bf16[4,40,1152]{2,1,0:T(8,128)(2,1)S(1)} %get-tuple-element.13), channel_id=1, source_target_pairs={{0,256},{128,384},{256,0},{384,128},{1,257},{129,385},{257,1},{385... | collective-permute-start | bytes 1105928 | tf_op jit(solution)/shard_map/ppermute | solution.py:167
  43.3 3.6 %collective-permute-start.6 = (bf16[4,40,1152]{2,1,0:T(8,128)(2,1)S(1)}, bf16[4,40,1152]{2,1,0:T(8,128)(2,1)S(1)}, u32[]{:S(2)}, u32[]{:S(2)}) collective-permute-start(bf16[4,40,1152]{2,1,0:T(8,128)(2,1)S(1)} %get-tuple-element.13), channel_id=1, source_target_pairs={{0,384},{128,0},{256,128},{384,256},{1,385},{129,1},{257,129},{385... | collective-permute-start | bytes 1105928 | tf_op jit(solution)/shard_map/ppermute | solution.py:167
  46.9 3.5 %collective-permute-start.4 = (bf16[4,40,1152]{2,1,0:T(8,128)(2,1)S(1)}, bf16[4,40,1152]{2,1,0:T(8,128)(2,1)S(1)}, u32[]{:S(2)}, u32[]{:S(2)}) collective-permute-start(bf16[4,40,1152]{2,1,0:T(8,128)(2,1)S(1)} %get-tuple-element.13), channel_id=1, source_target_pairs={{0,128},{128,256},{256,384},{384,0},{1,129},{129,257},{257,385},{3... | collective-permute-start | bytes 1105928 | tf_op jit(solution)/shard_map/ppermute | solution.py:167
  50.4 5.9 %collective-permute-done.5 = bf16[4,40,1152]{2,1,0:T(8,128)(2,1)S(1)} collective-permute-done((bf16[4,40,1152]{2,1,0:T(8,128)(2,1)S(1)}, bf16[4,40,1152]{2,1,0:T(8,128)(2,1)S(1)}, u32[]{:S(2)}, u32[]{:S(2)}) %collective-permute-start.5) | collective-permute-done | bytes 368672 | tf_op jit(solution)/shard_map/ppermute | solution.py:167
  56.3 5.8 %collective-permute-done.6 = bf16[4,40,1152]{2,1,0:T(8,128)(2,1)S(1)} collective-permute-done((bf16[4,40,1152]{2,1,0:T(8,128)(2,1)S(1)}, bf16[4,40,1152]{2,1,0:T(8,128)(2,1)S(1)}, u32[]{:S(2)}, u32[]{:S(2)}) %collective-permute-start.6) | collective-permute-done | bytes 368672 | tf_op jit(solution)/shard_map/ppermute | solution.py:167
  62.4 2.0 %collective-permute-start.7 = (bf16[4,4,40,1152]{3,2,1,0:T(8,128)(2,1)S(1)}, bf16[4,4,40,1152]{3,2,1,0:T(8,128)(2,1)S(1)}, u32[]{:S(2)}, u32[]{:S(2)}) collective-permute-start(bf16[4,4,40,1152]{3,2,1,0:T(8,128)(2,1)S(1)} %pad_maximum_fusion.own_ref), channel_id=1, source_target_pairs={{0,8},{8,0},{1,9},{9,1},{2,10},{10,2},{3,11},{11,3},{4,12},{12,4},... | collective-permute-start | bytes 4423688 | tf_op jit(solution)/shard_map/ppermute | solution.py:236
  64.5 3.0 %collective-permute-done.7.other_ref = bf16[4,4,40,1152]{3,2,1,0:T(8,128)(2,1)S(1)} collective-permute-done((bf16[4,4,40,1152]{3,2,1,0:T(8,128)(2,1)S(1)}, bf16[4,4,40,1152]{3,2,1,0:T(8,128)(2,1)S(1)}, u32[]{:S(2)}, u32[]{:S(2)}) %collective-permute-start.7) | collective-permute-done | bytes 1474592 | tf_op jit(solution)/shard_map/ppermute | solution.py:236
  67.5 0.9 shard_map.94
  68.4 0.7 fusion
  69.1 0.2 broadcast_multiply_fusion
  69.3 15.1 %all-to-all-done.moved_ref = bf16[128,9,4,128]{3,2,1,0:T(4,128)(2,1)} async-done(((bf16[128,9,4,128]{3,2,1,0:T(4,128)(2,1)}), bf16[128,9,4,128]{3,2,1,0:T(4,128)(2,1)}, u32[]{:S(2)}, u32[]{:S(2)}) %all-to-all-start) | async-done | bytes 1179680 | tf_op jit(solution)/shard_map/all_to_all | solution.py:256
  84.4 5.1 %shard_map.95 = bf16[128,8,4,128]{3,2,1,0:T(4,128)(2,1)S(1)} custom-call(bf16[128,9,4,128]{3,2,1,0:T(4,128)(2,1)} %all-to-all-done.moved_ref, bf16[1152,1152]{1,0:T(8,128)(2,1)S(1)} %bitcast.17, f32[1,1152]{1,0:T(1,128)S(1)} %reshape.21.gate_ref), custom_call_target="tpu_custom_call" | custom-call | flops 1500000000 | bytes 5000000 | tf_op jit(solution)/shard_map/pallas_call | solution.py:109
  89.5 62.8 %all_to_all.10.x_ref = bf16[128,8,4,128]{3,2,1,0:T(4,128)(2,1)S(1)} all-to-all(bf16[128,8,4,128]{3,2,1,0:T(4,128)(2,1)S(1)} %shard_map.95), channel_id=1, replica_groups=mesh['clip'=4,'zl'=8,'core'=2,'zh'=2,'y'=4] {'zl','core','zh','y'}, dimensions={0} | all-to-all | bytes 2097152 | tf_op jit(solution)/shard_map/all_to_all | solution.py:258
  152.5 2.7 %collective-permute-start.8 = (f32[5,128]{1,0:T(8,128)S(1)}, f32[5,128]{1,0:T(8,128)S(1)}, u32[]{:S(2)}, u32[]{:S(2)}) collective-permute-start(f32[5,128]{1,0:T(8,128)S(1)} %convert_reduce_fusion), channel_id=1, source_target_pairs={{0,8},{8,0},{1,9},{9,1},{2,10},{10,2},{3,11},{11,3},{4,12},{12,4},... | collective-permute-start | bytes 7688 | tf_op jit(solution)/shard_map/ppermute | solution.py:246
  155.2 2.3 %shard_map.96 = (bf16[1,128,1152]{2,1,0:T(8,128)(2,1)}, bf16[1,128,1152]{2,1,0:T(8,128)(2,1)}, bf16[1,128,1152]{2,1,0:T(8,128)(2,1)}) custom-call(bf16[128,8,4,128]{3,2,1,0:T(4,128)(2,1)} %copy-done), custom_call_target="tpu_custom_call" | custom-call | bytes 1800000 | tf_op jit(solution)/shard_map/pallas_call | solution.py:156
  157.5 0.6 maximum_bitcast_fusion
  (17 shorter events, 0.6 us)
Async XLA Ops:
  0.6 26.0 %collective-permute-start = (bf16[72,1152]{1,0:T(8,128)(2,1)}, bf16[72,1152]{1,0:T(8,128)(2,1)S(1)}, u32[]{:S(2)}, u32[]{:S(2)}) collective-permute-start(bf16[72,1152]{1,0:T(8,128)(2,1)} %param.11), channel_id=1, source_target_pairs={{84,0},{100,16},{116,32},{0,48},{16,64},{32,80},{48,96},{64,112},{... | collective-permute-start | bytes 497672 | tf_op jit(solution)/shard_map/ppermute | solution.py:230
  15.5 68.9 %all-to-all-start = ((bf16[128,9,4,128]{3,2,1,0:T(4,128)(2,1)}), bf16[128,9,4,128]{3,2,1,0:T(4,128)(2,1)}, u32[]{:S(2)}, u32[]{:S(2)}) async-start(bf16[128,9,4,128]{3,2,1,0:T(4,128)(2,1)} %shard_map.93), calls=%async_computation | async-start | bytes 2359296 | tf_op jit(solution)/shard_map/all_to_all | solution.py:256
  26.7 37.8 %copy-start.1 = (f32[1152]{0:T(1024)S(1)}, f32[1152]{0:T(1024)}, u32[]{:S(2)}) copy-start(f32[1152]{0:T(1024)} %param.10) | copy-start | bytes 13828
  26.7 11.0 %collective-permute-start.1 = (bf16[40,1152]{1,0:T(8,128)(2,1)S(1)}, bf16[40,1152]{1,0:T(8,128)(2,1)S(1)}, u32[]{:S(2)}, u32[]{:S(2)}) collective-permute-start(bf16[40,1152]{1,0:T(8,128)(2,1)S(1)} %broadcast_multiply_fusion.1), channel_id=1, source_target_pairs={{0,1},{1,2},{2,3},{3,0},{4,5},{5,6},{6,7},{7,4},{8,9},{9,10},{10,1... | collective-permute-start | bytes 276488 | tf_op jit(solution)/shard_map/ppermute | solution.py:167
  29.7 8.8 %collective-permute-start.2 = (bf16[40,1152]{1,0:T(8,128)(2,1)S(1)}, bf16[40,1152]{1,0:T(8,128)(2,1)S(1)}, u32[]{:S(2)}, u32[]{:S(2)}) collective-permute-start(bf16[40,1152]{1,0:T(8,128)(2,1)S(1)} %broadcast_multiply_fusion.1), channel_id=1, source_target_pairs={{0,2},{1,3},{2,0},{3,1},{4,6},{5,7},{6,4},{7,5},{8,10},{9,11},{10,... | collective-permute-start | bytes 276488 | tf_op jit(solution)/shard_map/ppermute | solution.py:167
  34.3 7.0 %collective-permute-start.3 = (bf16[40,1152]{1,0:T(8,128)(2,1)S(1)}, bf16[40,1152]{1,0:T(8,128)(2,1)S(1)}, u32[]{:S(2)}, u32[]{:S(2)}) collective-permute-start(bf16[40,1152]{1,0:T(8,128)(2,1)S(1)} %broadcast_multiply_fusion.1), channel_id=1, source_target_pairs={{0,3},{1,0},{2,1},{3,2},{4,7},{5,4},{6,5},{7,6},{8,11},{9,8},{10,9... | collective-permute-start | bytes 276488 | tf_op jit(solution)/shard_map/ppermute | solution.py:167
  41.4 15.0 %collective-permute-start.5 = (bf16[4,40,1152]{2,1,0:T(8,128)(2,1)S(1)}, bf16[4,40,1152]{2,1,0:T(8,128)(2,1)S(1)}, u32[]{:S(2)}, u32[]{:S(2)}) collective-permute-start(bf16[4,40,1152]{2,1,0:T(8,128)(2,1)S(1)} %get-tuple-element.13), channel_id=1, source_target_pairs={{0,256},{128,384},{256,0},{384,128},{1,257},{129,385},{257,1},{385... | collective-permute-start | bytes 1105928 | tf_op jit(solution)/shard_map/ppermute | solution.py:167
  43.3 18.8 %collective-permute-start.6 = (bf16[4,40,1152]{2,1,0:T(8,128)(2,1)S(1)}, bf16[4,40,1152]{2,1,0:T(8,128)(2,1)S(1)}, u32[]{:S(2)}, u32[]{:S(2)}) collective-permute-start(bf16[4,40,1152]{2,1,0:T(8,128)(2,1)S(1)} %get-tuple-element.13), channel_id=1, source_target_pairs={{0,384},{128,0},{256,128},{384,256},{1,385},{129,1},{257,129},{385... | collective-permute-start | bytes 1105928 | tf_op jit(solution)/shard_map/ppermute | solution.py:167
  46.9 15.2 %collective-permute-start.4 = (bf16[4,40,1152]{2,1,0:T(8,128)(2,1)S(1)}, bf16[4,40,1152]{2,1,0:T(8,128)(2,1)S(1)}, u32[]{:S(2)}, u32[]{:S(2)}) collective-permute-start(bf16[4,40,1152]{2,1,0:T(8,128)(2,1)S(1)} %get-tuple-element.13), channel_id=1, source_target_pairs={{0,128},{128,256},{256,384},{384,0},{1,129},{129,257},{257,385},{3... | collective-permute-start | bytes 1105928 | tf_op jit(solution)/shard_map/ppermute | solution.py:167
  62.4 5.2 %collective-permute-start.7 = (bf16[4,4,40,1152]{3,2,1,0:T(8,128)(2,1)S(1)}, bf16[4,4,40,1152]{3,2,1,0:T(8,128)(2,1)S(1)}, u32[]{:S(2)}, u32[]{:S(2)}) collective-permute-start(bf16[4,4,40,1152]{3,2,1,0:T(8,128)(2,1)S(1)} %pad_maximum_fusion.own_ref), channel_id=1, source_target_pairs={{0,8},{8,0},{1,9},{9,1},{2,10},{10,2},{3,11},{11,3},{4,12},{12,4},... | collective-permute-start | bytes 4423688 | tf_op jit(solution)/shard_map/ppermute | solution.py:236
  152.3 2.9 %copy-start = (bf16[128,8,4,128]{3,2,1,0:T(4,128)(2,1)}, bf16[128,8,4,128]{3,2,1,0:T(4,128)(2,1)S(1)}, u32[]{:S(2)}) copy-start(bf16[128,8,4,128]{3,2,1,0:T(4,128)(2,1)S(1)} %all_to_all.10.x_ref) | copy-start | bytes 3145732
  152.5 5.0 %collective-permute-start.8 = (f32[5,128]{1,0:T(8,128)S(1)}, f32[5,128]{1,0:T(8,128)S(1)}, u32[]{:S(2)}, u32[]{:S(2)}) collective-permute-start(f32[5,128]{1,0:T(8,128)S(1)} %convert_reduce_fusion), channel_id=1, source_target_pairs={{0,8},{8,0},{1,9},{9,1},{2,10},{10,2},{3,11},{11,3},{4,12},{12,4},... | collective-permute-start | bytes 7688 | tf_op jit(solution)/shard_map/ppermute | solution.py:246

commit v7 on v6

--- a/solution.py
+++ b/solution.py
@@ -15,6 +15,7 @@
 TILES = WIDTH // LANES
 AXES = ("clip", "zl", "core", "zh", "y")
 GROUP = ("zl", "core", "zh", "y")
+CHUNKS = 4
 GATE_ROWS = 5
 ROWS_OUT = 3 * TILES + GATE_ROWS
 FACTOR = HEAD_DIM ** (-0.5)
@@ -26,13 +27,24 @@
     return first, last + 1
 
 
-def attend_kernel(moved_ref, w_ref, gate_ref, out_ref, x_ref, da_ref):
+def attend_kernel(moved_hbm, w_ref, gate_ref, out_ref, moved_ref, x_ref, da_ref, sems):
     f32, bf16 = jnp.float32, jnp.bfloat16
     nt = (((1,), (1,)), ((), ()))
     nn = (((1,), (0,)), ((), ()))
     tn = (((0,), (0,)), ((), ()))
     frames = moved_ref.shape[0]
-    x_ref[...] = jnp.transpose(moved_ref[...].reshape(frames, 4 * TILES, LANES), (1, 0, 2))
+    step = frames // CHUNKS
+    spans = [pl.ds(n * step, step) for n in range(CHUNKS)]
+    loads = [
+        pltpu.make_async_copy(moved_hbm.at[span], moved_ref.at[span], sems.at[n])
+        for n, span in enumerate(spans)
+    ]
+    for load in loads:
+        load.start()
+    for load, span in zip(loads, spans):
+        load.wait()
+        part = moved_ref[span].reshape(step, 4 * TILES, LANES)
+        x_ref[:, span] = jnp.transpose(part, (1, 0, 2))
 
     def cat(first, last):
         parts = [x_ref[t] for t in range(first, last)]
@@ -109,13 +121,15 @@
     return pl.pallas_call(
         attend_kernel,
         out_shape=jax.ShapeDtypeStruct((frames, ROWS_OUT // 4, 4, LANES), jnp.bfloat16),
-        in_specs=[vmem, vmem, vmem],
+        in_specs=[pl.BlockSpec(memory_space=pl.ANY), vmem, vmem],
         out_specs=vmem,
         scratch_shapes=[
+            pltpu.VMEM(x.shape, jnp.bfloat16),
             pltpu.VMEM((4 * TILES, frames, LANES), jnp.bfloat16),
             pltpu.VMEM((frames, WIDTH), jnp.bfloat16),
+            pltpu.SemaphoreType.DMA((CHUNKS,)),
         ],
-        compiler_params=pltpu.CompilerParams(vmem_limit_bytes=12 << 20),
+        compiler_params=pltpu.CompilerParams(vmem_limit_bytes=16 << 20),
         cost_estimate=pl.CostEstimate(
             flops=1_500_000_000, bytes_accessed=5_000_000, transcendentals=300_000
         ),

time: 160 us -> 160 us (level)
  no operation moved by 1% of the time
where the time goes in v7:
time: 160 us; the launch traced here: 158 us
  blocking collectives  62.8 us (39%)
  starting transfers between devices  48.1 us (30%)
  waiting for transfers between devices  33.4 us (21%)
  Pallas kernels  10.9 us (7%)
  other arithmetic  2.06 us (1%)
    all_to_all x1, blocking collectives, per_device(): lax.all_to_all(grads, GROUP, split_axis=0, concat_axis=0, tiled=True)  62.8 us
    ppermute x6, starting transfers between devices, along(): return lax.ppermute(x, axis, [(i, (i + shift) % 4) for i in range(4)])  19.9 us
    ppermute x6, waiting for transfers between devices, along(): return lax.ppermute(x, axis, [(i, (i + shift) % 4) for i in range(4)])  15.3 us
    all_to_all x1, waiting for transfers between devices, per_device(): lax.all_to_all(packed, GROUP, split_axis=0, concat_axis=0, tiled=True)  15.1 us
    ppermute x1, starting transfers between devices, gather_weight(): held = lax.ppermute(shard, AXES, fetch_pairs())  12.3 us
    all_to_all x1, starting transfers between devices, per_device(): lax.all_to_all(packed, GROUP, split_axis=0, concat_axis=0, tiled=True)  11.1 us
    pallas_call x1, Pallas kernels, attend(): pl.pallas_call(attend_kernel, out_shape=jax.ShapeDtypeStruct((frames, ROW...  5.13 us
  transfers between devices with their start and end apart: 10, of which 6 were waited for; matrix products, arithmetic and copies ran while one was open for 1% of the time, Pallas kernels for 4%

profile of v7, /device:TPU:6, one launch (start us, length us, event | category | flops | bytes accessed | tf_op | source)
XLA Modules:
  0.0 158.1 jit_solution(2313942164186637357)
XLA Ops:
  0.6 12.3 %collective-permute-start = (bf16[72,1152]{1,0:T(8,128)(2,1)}, bf16[72,1152]{1,0:T(8,128)(2,1)S(1)}, u32[]{:S(2)}, u32[]{:S(2)}) collective-permute-start(bf16[72,1152]{1,0:T(8,128)(2,1)} %param.11), channel_id=1, source_target_pairs={{84,0},{100,16},{116,32},{0,48},{16,64},{32,80},{48,96},{64,112},{... | collective-permute-start | bytes 497672 | tf_op jit(solution)/shard_map/ppermute | solution.py:244
  12.9 2.6 %shard_map.93 = bf16[128,9,4,128]{3,2,1,0:T(4,128)(2,1)} custom-call(bf16[1,128,1152]{2,1,0:T(8,128)(2,1)} %refs_0_.1, bf16[1,128,1152]{2,1,0:T(8,128)(2,1)} %refs_1_.1, bf16[1,128,1152]{2,1,0:T(8,128)(2,1)} %refs_2_.1, bf16[1,128,1152]{2,1,0:T(8,128)(2,1)} %refs_3_.1), custom_call_target="tpu_custom_call" | custom-call | bytes 2400000 | tf_op jit(solution)/shard_map/pallas_call | solution.py:149
  15.5 11.1 %all-to-all-start = ((bf16[128,9,4,128]{3,2,1,0:T(4,128)(2,1)}), bf16[128,9,4,128]{3,2,1,0:T(4,128)(2,1)}, u32[]{:S(2)}, u32[]{:S(2)}) async-start(bf16[128,9,4,128]{3,2,1,0:T(4,128)(2,1)} %shard_map.93), calls=%async_computation | async-start | bytes 2359296 | tf_op jit(solution)/shard_map/all_to_all | solution.py:270
  26.7 3.0 %collective-permute-start.1 = (bf16[40,1152]{1,0:T(8,128)(2,1)S(1)}, bf16[40,1152]{1,0:T(8,128)(2,1)S(1)}, u32[]{:S(2)}, u32[]{:S(2)}) collective-permute-start(bf16[40,1152]{1,0:T(8,128)(2,1)S(1)} %broadcast_multiply_fusion.1), channel_id=1, source_target_pairs={{0,1},{1,2},{2,3},{3,0},{4,5},{5,6},{6,7},{7,4},{8,9},{9,10},{10,1... | collective-permute-start | bytes 276488 | tf_op jit(solution)/shard_map/ppermute | solution.py:181
  29.7 4.6 %collective-permute-start.2 = (bf16[40,1152]{1,0:T(8,128)(2,1)S(1)}, bf16[40,1152]{1,0:T(8,128)(2,1)S(1)}, u32[]{:S(2)}, u32[]{:S(2)}) collective-permute-start(bf16[40,1152]{1,0:T(8,128)(2,1)S(1)} %broadcast_multiply_fusion.1), channel_id=1, source_target_pairs={{0,2},{1,3},{2,0},{3,1},{4,6},{5,7},{6,4},{7,5},{8,10},{9,11},{10,... | collective-permute-start | bytes 276488 | tf_op jit(solution)/shard_map/ppermute | solution.py:181
  34.3 3.4 %collective-permute-start.3 = (bf16[40,1152]{1,0:T(8,128)(2,1)S(1)}, bf16[40,1152]{1,0:T(8,128)(2,1)S(1)}, u32[]{:S(2)}, u32[]{:S(2)}) collective-permute-start(bf16[40,1152]{1,0:T(8,128)(2,1)S(1)} %broadcast_multiply_fusion.1), channel_id=1, source_target_pairs={{0,3},{1,0},{2,1},{3,2},{4,7},{5,4},{6,5},{7,6},{8,11},{9,8},{10,9... | collective-permute-start | bytes 276488 | tf_op jit(solution)/shard_map/ppermute | solution.py:181
  37.7 0.8 collective-permute-done.2
  38.5 2.8 %collective-permute-done.3 = bf16[40,1152]{1,0:T(8,128)(2,1)S(1)} collective-permute-done((bf16[40,1152]{1,0:T(8,128)(2,1)S(1)}, bf16[40,1152]{1,0:T(8,128)(2,1)S(1)}, u32[]{:S(2)}, u32[]{:S(2)}) %collective-permute-start.3) | collective-permute-done | bytes 92192 | tf_op jit(solution)/shard_map/ppermute | solution.py:181
  41.4 1.9 %collective-permute-start.5 = (bf16[4,40,1152]{2,1,0:T(8,128)(2,1)S(1)}, bf16[4,40,1152]{2,1,0:T(8,128)(2,1)S(1)}, u32[]{:S(2)}, u32[]{:S(2)}) collective-permute-start(bf16[4,40,1152]{2,1,0:T(8,128)(2,1)S(1)} %get-tuple-element.13), channel_id=1, source_target_pairs={{0,256},{128,384},{256,0},{384,128},{1,257},{129,385},{257,1},{385... | collective-permute-start | bytes 1105928 | tf_op jit(solution)/shard_map/ppermute | solution.py:181
  43.3 3.6 %collective-permute-start.6 = (bf16[4,40,1152]{2,1,0:T(8,128)(2,1)S(1)}, bf16[4,40,1152]{2,1,0:T(8,128)(2,1)S(1)}, u32[]{:S(2)}, u32[]{:S(2)}) collective-permute-start(bf16[4,40,1152]{2,1,0:T(8,128)(2,1)S(1)} %get-tuple-element.13), channel_id=1, source_target_pairs={{0,384},{128,0},{256,128},{384,256},{1,385},{129,1},{257,129},{385... | collective-permute-start | bytes 1105928 | tf_op jit(solution)/shard_map/ppermute | solution.py:181
  46.9 3.5 %collective-permute-start.4 = (bf16[4,40,1152]{2,1,0:T(8,128)(2,1)S(1)}, bf16[4,40,1152]{2,1,0:T(8,128)(2,1)S(1)}, u32[]{:S(2)}, u32[]{:S(2)}) collective-permute-start(bf16[4,40,1152]{2,1,0:T(8,128)(2,1)S(1)} %get-tuple-element.13), channel_id=1, source_target_pairs={{0,128},{128,256},{256,384},{384,0},{1,129},{129,257},{257,385},{3... | collective-permute-start | bytes 1105928 | tf_op jit(solution)/shard_map/ppermute | solution.py:181
  50.4 5.9 %collective-permute-done.5 = bf16[4,40,1152]{2,1,0:T(8,128)(2,1)S(1)} collective-permute-done((bf16[4,40,1152]{2,1,0:T(8,128)(2,1)S(1)}, bf16[4,40,1152]{2,1,0:T(8,128)(2,1)S(1)}, u32[]{:S(2)}, u32[]{:S(2)}) %collective-permute-start.5) | collective-permute-done | bytes 368672 | tf_op jit(solution)/shard_map/ppermute | solution.py:181
  56.3 5.8 %collective-permute-done.6 = bf16[4,40,1152]{2,1,0:T(8,128)(2,1)S(1)} collective-permute-done((bf16[4,40,1152]{2,1,0:T(8,128)(2,1)S(1)}, bf16[4,40,1152]{2,1,0:T(8,128)(2,1)S(1)}, u32[]{:S(2)}, u32[]{:S(2)}) %collective-permute-start.6) | collective-permute-done | bytes 368672 | tf_op jit(solution)/shard_map/ppermute | solution.py:181
  62.4 2.0 %collective-permute-start.7 = (bf16[4,4,40,1152]{3,2,1,0:T(8,128)(2,1)S(1)}, bf16[4,4,40,1152]{3,2,1,0:T(8,128)(2,1)S(1)}, u32[]{:S(2)}, u32[]{:S(2)}) collective-permute-start(bf16[4,4,40,1152]{3,2,1,0:T(8,128)(2,1)S(1)} %pad_maximum_fusion.own_ref), channel_id=1, source_target_pairs={{0,8},{8,0},{1,9},{9,1},{2,10},{10,2},{3,11},{11,3},{4,12},{12,4},... | collective-permute-start | bytes 4423688 | tf_op jit(solution)/shard_map/ppermute | solution.py:250
  64.5 3.0 %collective-permute-done.7.other_ref = bf16[4,4,40,1152]{3,2,1,0:T(8,128)(2,1)S(1)} collective-permute-done((bf16[4,4,40,1152]{3,2,1,0:T(8,128)(2,1)S(1)}, bf16[4,4,40,1152]{3,2,1,0:T(8,128)(2,1)S(1)}, u32[]{:S(2)}, u32[]{:S(2)}) %collective-permute-start.7) | collective-permute-done | bytes 1474592 | tf_op jit(solution)/shard_map/ppermute | solution.py:250
  67.5 0.9 shard_map.94
  68.4 0.7 fusion
  69.1 0.2 broadcast_multiply_fusion
  69.3 15.1 %all-to-all-done.moved_hbm = bf16[128,9,4,128]{3,2,1,0:T(4,128)(2,1)} async-done(((bf16[128,9,4,128]{3,2,1,0:T(4,128)(2,1)}), bf16[128,9,4,128]{3,2,1,0:T(4,128)(2,1)}, u32[]{:S(2)}, u32[]{:S(2)}) %all-to-all-start) | async-done | bytes 1179680 | tf_op jit(solution)/shard_map/all_to_all | solution.py:270
  84.4 5.1 %shard_map.95 = bf16[128,8,4,128]{3,2,1,0:T(4,128)(2,1)S(1)} custom-call(bf16[128,9,4,128]{3,2,1,0:T(4,128)(2,1)} %all-to-all-done.moved_hbm, bf16[1152,1152]{1,0:T(8,128)(2,1)S(1)} %bitcast.17, f32[1,1152]{1,0:T(1,128)S(1)} %reshape.21.gate_ref), custom_call_target="tpu_custom_call" | custom-call | flops 1500000000 | bytes 5000000 | tf_op jit(solution)/shard_map/pallas_call | solution.py:121
  89.5 62.8 %all_to_all.10.x_ref = bf16[128,8,4,128]{3,2,1,0:T(4,128)(2,1)S(1)} all-to-all(bf16[128,8,4,128]{3,2,1,0:T(4,128)(2,1)S(1)} %shard_map.95), channel_id=1, replica_groups=mesh['clip'=4,'zl'=8,'core'=2,'zh'=2,'y'=4] {'zl','core','zh','y'}, dimensions={0} | all-to-all | bytes 2097152 | tf_op jit(solution)/shard_map/all_to_all | solution.py:272
  152.4 2.7 %collective-permute-start.8 = (f32[5,128]{1,0:T(8,128)S(1)}, f32[5,128]{1,0:T(8,128)S(1)}, u32[]{:S(2)}, u32[]{:S(2)}) collective-permute-start(f32[5,128]{1,0:T(8,128)S(1)} %convert_reduce_fusion), channel_id=1, source_target_pairs={{0,8},{8,0},{1,9},{9,1},{2,10},{10,2},{3,11},{11,3},{4,12},{12,4},... | collective-permute-start | bytes 7688 | tf_op jit(solution)/shard_map/ppermute | solution.py:260
  155.2 2.3 %shard_map.96 = (bf16[1,128,1152]{2,1,0:T(8,128)(2,1)}, bf16[1,128,1152]{2,1,0:T(8,128)(2,1)}, bf16[1,128,1152]{2,1,0:T(8,128)(2,1)}) custom-call(bf16[128,8,4,128]{3,2,1,0:T(4,128)(2,1)} %copy-done), custom_call_target="tpu_custom_call" | custom-call | bytes 1800000 | tf_op jit(solution)/shard_map/pallas_call | solution.py:170
  157.5 0.6 maximum_bitcast_fusion
  (17 shorter events, 0.6 us)
Async XLA Ops:
  0.6 26.0 %collective-permute-start = (bf16[72,1152]{1,0:T(8,128)(2,1)}, bf16[72,1152]{1,0:T(8,128)(2,1)S(1)}, u32[]{:S(2)}, u32[]{:S(2)}) collective-permute-start(bf16[72,1152]{1,0:T(8,128)(2,1)} %param.11), channel_id=1, source_target_pairs={{84,0},{100,16},{116,32},{0,48},{16,64},{32,80},{48,96},{64,112},{... | collective-permute-start | bytes 497672 | tf_op jit(solution)/shard_map/ppermute | solution.py:244
  15.5 68.9 %all-to-all-start = ((bf16[128,9,4,128]{3,2,1,0:T(4,128)(2,1)}), bf16[128,9,4,128]{3,2,1,0:T(4,128)(2,1)}, u32[]{:S(2)}, u32[]{:S(2)}) async-start(bf16[128,9,4,128]{3,2,1,0:T(4,128)(2,1)} %shard_map.93), calls=%async_computation | async-start | bytes 2359296 | tf_op jit(solution)/shard_map/all_to_all | solution.py:270
  26.7 37.8 %copy-start.1 = (f32[1152]{0:T(1024)S(1)}, f32[1152]{0:T(1024)}, u32[]{:S(2)}) copy-start(f32[1152]{0:T(1024)} %param.10) | copy-start | bytes 13828
  26.7 11.0 %collective-permute-start.1 = (bf16[40,1152]{1,0:T(8,128)(2,1)S(1)}, bf16[40,1152]{1,0:T(8,128)(2,1)S(1)}, u32[]{:S(2)}, u32[]{:S(2)}) collective-permute-start(bf16[40,1152]{1,0:T(8,128)(2,1)S(1)} %broadcast_multiply_fusion.1), channel_id=1, source_target_pairs={{0,1},{1,2},{2,3},{3,0},{4,5},{5,6},{6,7},{7,4},{8,9},{9,10},{10,1... | collective-permute-start | bytes 276488 | tf_op jit(solution)/shard_map/ppermute | solution.py:181
  29.7 8.8 %collective-permute-start.2 = (bf16[40,1152]{1,0:T(8,128)(2,1)S(1)}, bf16[40,1152]{1,0:T(8,128)(2,1)S(1)}, u32[]{:S(2)}, u32[]{:S(2)}) collective-permute-start(bf16[40,1152]{1,0:T(8,128)(2,1)S(1)} %broadcast_multiply_fusion.1), channel_id=1, source_target_pairs={{0,2},{1,3},{2,0},{3,1},{4,6},{5,7},{6,4},{7,5},{8,10},{9,11},{10,... | collective-permute-start | bytes 276488 | tf_op jit(solution)/shard_map/ppermute | solution.py:181
  34.3 7.0 %collective-permute-start.3 = (bf16[40,1152]{1,0:T(8,128)(2,1)S(1)}, bf16[40,1152]{1,0:T(8,128)(2,1)S(1)}, u32[]{:S(2)}, u32[]{:S(2)}) collective-permute-start(bf16[40,1152]{1,0:T(8,128)(2,1)S(1)} %broadcast_multiply_fusion.1), channel_id=1, source_target_pairs={{0,3},{1,0},{2,1},{3,2},{4,7},{5,4},{6,5},{7,6},{8,11},{9,8},{10,9... | collective-permute-start | bytes 276488 | tf_op jit(solution)/shard_map/ppermute | solution.py:181
  41.4 15.0 %collective-permute-start.5 = (bf16[4,40,1152]{2,1,0:T(8,128)(2,1)S(1)}, bf16[4,40,1152]{2,1,0:T(8,128)(2,1)S(1)}, u32[]{:S(2)}, u32[]{:S(2)}) collective-permute-start(bf16[4,40,1152]{2,1,0:T(8,128)(2,1)S(1)} %get-tuple-element.13), channel_id=1, source_target_pairs={{0,256},{128,384},{256,0},{384,128},{1,257},{129,385},{257,1},{385... | collective-permute-start | bytes 1105928 | tf_op jit(solution)/shard_map/ppermute | solution.py:181
  43.3 18.8 %collective-permute-start.6 = (bf16[4,40,1152]{2,1,0:T(8,128)(2,1)S(1)}, bf16[4,40,1152]{2,1,0:T(8,128)(2,1)S(1)}, u32[]{:S(2)}, u32[]{:S(2)}) collective-permute-start(bf16[4,40,1152]{2,1,0:T(8,128)(2,1)S(1)} %get-tuple-element.13), channel_id=1, source_target_pairs={{0,384},{128,0},{256,128},{384,256},{1,385},{129,1},{257,129},{385... | collective-permute-start | bytes 1105928 | tf_op jit(solution)/shard_map/ppermute | solution.py:181
  46.9 15.2 %collective-permute-start.4 = (bf16[4,40,1152]{2,1,0:T(8,128)(2,1)S(1)}, bf16[4,40,1152]{2,1,0:T(8,128)(2,1)S(1)}, u32[]{:S(2)}, u32[]{:S(2)}) collective-permute-start(bf16[4,40,1152]{2,1,0:T(8,128)(2,1)S(1)} %get-tuple-element.13), channel_id=1, source_target_pairs={{0,128},{128,256},{256,384},{384,0},{1,129},{129,257},{257,385},{3... | collective-permute-start | bytes 1105928 | tf_op jit(solution)/shard_map/ppermute | solution.py:181
  62.4 5.2 %collective-permute-start.7 = (bf16[4,4,40,1152]{3,2,1,0:T(8,128)(2,1)S(1)}, bf16[4,4,40,1152]{3,2,1,0:T(8,128)(2,1)S(1)}, u32[]{:S(2)}, u32[]{:S(2)}) collective-permute-start(bf16[4,4,40,1152]{3,2,1,0:T(8,128)(2,1)S(1)} %pad_maximum_fusion.own_ref), channel_id=1, source_target_pairs={{0,8},{8,0},{1,9},{9,1},{2,10},{10,2},{3,11},{11,3},{4,12},{12,4},... | collective-permute-start | bytes 4423688 | tf_op jit(solution)/shard_map/ppermute | solution.py:250
  152.3 2.9 %copy-start = (bf16[128,8,4,128]{3,2,1,0:T(4,128)(2,1)}, bf16[128,8,4,128]{3,2,1,0:T(4,128)(2,1)S(1)}, u32[]{:S(2)}) copy-start(bf16[128,8,4,128]{3,2,1,0:T(4,128)(2,1)S(1)} %all_to_all.10.x_ref) | copy-start | bytes 3145732
  152.4 5.0 %collective-permute-start.8 = (f32[5,128]{1,0:T(8,128)S(1)}, f32[5,128]{1,0:T(8,128)S(1)}, u32[]{:S(2)}, u32[]{:S(2)}) collective-permute-start(f32[5,128]{1,0:T(8,128)S(1)} %convert_reduce_fusion), channel_id=1, source_target_pairs={{0,8},{8,0},{1,9},{9,1},{2,10},{10,2},{3,11},{11,3},{4,12},{12,4},... | collective-permute-start | bytes 7688 | tf_op jit(solution)/shard_map/ppermute | solution.py:260
